TPU v7x, 256 devices: a whole 4x4x8 slice. The times are simulated.
256 devices in a mesh: gx: 16 (over x, y), gy: 16 (over z, core).
Axes of the slice: x: 4, y: 4, z: 8, core: 2. Of those that a mesh axis runs over, the one named last changes fastest.
Arguments:
- density: float32 [8, 128, 32768], P(None, 'gy', 'gx'), may hold values from 0.04 to 80, as said below
- drift: float32 [2, 128, 32768], P(None, 'gy', 'gx'), may hold values from -0.1 to 0.1
- kill: float32 [128, 32768], P('gy', 'gx'), may hold values from 0.02 to 0.1
- diffusion: float32 [8], replicated, may hold values from 0.05 to 0.1
- jump_rate: float32 [8], replicated, may hold values from 0.1 to 0.5
- kernel_vals: float32 [8, 8192], replicated, may hold values from 0.001 to 1
- jump_len: int32 [8], replicated, may hold values from 2048 to 8192
- rate_table: float32 [64], replicated, may hold values from 0.002 to 0.035
- rate_index: int32 [8, 8], replicated, may hold values from 0 to 63
Outputs:
- density_out: float32 [8, 128, 32768], P(None, 'gy', 'gx')
Inputs may be any that keep to these rules, and one draw needn't show every extreme that they name: Every density is positive.
All inputs are finite; a program needn't handle non-finite values.
Results may differ from a plain program's by a relative error of at most 0.0001.
Values sent between devices are 32-bit elements; how exact they have to be, the bound alone decides.
A program may use at most 64 MiB of HBM per device.

v0:
```python
import math

import jax
import jax.numpy as jnp
from jax import lax
from jax.sharding import PartitionSpec as P

SWEEPS = 2


HIGHEST_PRECISION = lax.Precision.HIGHEST


def with_halo(array, sides, width):
    for axis, dim in sides:
        peers, length = (lax.axis_size(axis), array.shape[dim])
        up = [(i, (i + 1) % peers) for i in range(peers)]
        down = [(j, i) for i, j in up]
        last = lax.slice_in_dim(array, length - width, length, axis=dim)
        leading = lax.slice_in_dim(array, 0, width, axis=dim)
        before = lax.ppermute(last, axis, up)
        after = lax.ppermute(leading, axis, down)
        array = jnp.concatenate([before, array, after], axis=dim)
    return array


def angle_table(height, breadth, period):
    product = (
        lax.broadcasted_iota(jnp.int32, (height, breadth), 0)
        * lax.broadcasted_iota(jnp.int32, (height, breadth), 1)
        % period
    )
    angles = product.astype(jnp.float32) * (2.0 * math.pi / period)
    return (jnp.cos(angles), jnp.sin(angles))


def factor_pair(length):
    low_factor = 1
    factor = 1
    while factor * factor <= length:
        if length % factor == 0:
            low_factor = factor
        factor += 1
    return (low_factor, length // low_factor)


def forward_lines(line_data, tables):
    (cos_a, sin_a), (cos_b, sin_b), (cos_t, sin_t) = tables
    width_a = cos_a.shape[0]
    width_b = cos_b.shape[0]
    line_count = line_data.shape[0]
    blocks = line_data.reshape(line_count, width_a, width_b)
    first_re = jnp.einsum("mab,ak->mkb", blocks, cos_a, precision=HIGHEST_PRECISION)
    first_im = -jnp.einsum("mab,ak->mkb", blocks, sin_a, precision=HIGHEST_PRECISION)
    turned_re = first_re * cos_t + first_im * sin_t
    turned_im = first_im * cos_t - first_re * sin_t
    final_re = jnp.einsum(
        "mkb,bj->mkj", turned_re, cos_b, precision=HIGHEST_PRECISION
    ) + jnp.einsum("mkb,bj->mkj", turned_im, sin_b, precision=HIGHEST_PRECISION)
    final_im = jnp.einsum(
        "mkb,bj->mkj", turned_im, cos_b, precision=HIGHEST_PRECISION
    ) - jnp.einsum("mkb,bj->mkj", turned_re, sin_b, precision=HIGHEST_PRECISION)
    return (final_re, final_im)


def inverse_lines(spec_re, spec_im, tables):
    (cos_a, sin_a), (cos_b, sin_b), (cos_t, sin_t) = tables
    line_count, width_a, width_b = spec_re.shape
    back_re = jnp.einsum("mkj,jb->mkb", spec_re, cos_b, precision=HIGHEST_PRECISION) - jnp.einsum(
        "mkj,jb->mkb", spec_im, sin_b, precision=HIGHEST_PRECISION
    )
    back_im = jnp.einsum("mkj,jb->mkb", spec_re, sin_b, precision=HIGHEST_PRECISION) + jnp.einsum(
        "mkj,jb->mkb", spec_im, cos_b, precision=HIGHEST_PRECISION
    )
    turned_re = back_re * cos_t - back_im * sin_t
    turned_im = back_re * sin_t + back_im * cos_t
    result = jnp.einsum("mkb,ka->mab", turned_re, cos_a, precision=HIGHEST_PRECISION) - jnp.einsum(
        "mkb,ka->mab", turned_im, sin_a, precision=HIGHEST_PRECISION
    )
    return result.reshape(line_count, width_a * width_b) / (width_a * width_b)


def generator(rate_table, rate_index):
    regimes = rate_index.shape[0]
    entries = rate_table.shape[0]
    picked = (rate_index[:, :, None] == lax.iota(jnp.int32, entries)[None, None, :]).astype(
        jnp.float32
    )
    offdiag = jnp.sum(picked * rate_table[None, None, :], axis=2) * (
        1.0 - jnp.eye(regimes, dtype=jnp.float32)
    )
    return offdiag - jnp.diag(jnp.sum(offdiag, axis=1))


def tree_sum(values):
    for axis in ("gx", "gy"):
        peers = lax.axis_size(axis)
        step = 1
        while step < peers:
            pairs = [(i, i ^ step) for i in range(peers)]
            values = values + lax.ppermute(values, axis, pairs)
            step *= 2
    return values


def local(
    density, drift, kill, diffusion, jump_rate, kernel_vals, jump_len, rate_table, rate_index
):
    regimes, y_rows, x_cols = density.shape
    groups = lax.axis_size("gx")
    length = x_cols * groups
    per_dev = regimes * y_rows // groups
    width_a, width_b = factor_pair(length)
    tables = (
        angle_table(width_a, width_a, width_a),
        angle_table(width_b, width_b, width_b),
        angle_table(width_a, width_b, length),
    )
    support = kernel_vals.shape[1]
    inside = lax.broadcasted_iota(jnp.int32, (regimes, support), 1) < jump_len[:, None]
    weights = jnp.where(inside, kernel_vals, jnp.zeros_like(kernel_vals))
    weights = weights / jnp.sum(weights, axis=1, keepdims=True)
    padded = jnp.concatenate(
        [
            jnp.zeros((regimes, 1), jnp.float32),
            weights,
            jnp.zeros((regimes, length - support - 1), jnp.float32),
        ],
        axis=1,
    )
    first_line = lax.axis_index("gx") * per_dev
    if y_rows % per_dev == 0:
        own = lax.dynamic_slice_in_dim(padded, first_line // y_rows, 1, axis=0)
        own_re, own_im = forward_lines(own, tables)
        line_re = jnp.broadcast_to(own_re, (per_dev,) + own_re.shape[1:])
        line_im = jnp.broadcast_to(own_im, (per_dev,) + own_im.shape[1:])
    else:
        kern_re, kern_im = forward_lines(padded, tables)
        line_ids = first_line + lax.iota(jnp.int32, per_dev)
        owner_mask = (line_ids // y_rows)[:, None] == lax.iota(jnp.int32, regimes)[None, :]
        select = owner_mask.astype(jnp.float32)
        line_re = jnp.einsum("lr,rkj->lkj", select, kern_re, precision=HIGHEST_PRECISION)
        line_im = jnp.einsum("lr,rkj->lkj", select, kern_im, precision=HIGHEST_PRECISION)
    generator_matrix = generator(rate_table, rate_index)
    scale_diff = diffusion[:, None, None]
    scale_jump = jump_rate[:, None, None]
    field = density
    sums = []
    for sweep_index in range(SWEEPS):
        line_data = lax.all_to_all(
            field.reshape(regimes * y_rows, x_cols), "gx", split_axis=0, concat_axis=1, tiled=True
        )
        spec_re, spec_im = forward_lines(line_data, tables)
        prod_re = spec_re * line_re - spec_im * line_im
        prod_im = spec_re * line_im + spec_im * line_re
        jump_line = inverse_lines(prod_re, prod_im, tables)
        mixing = jnp.einsum("rs,ryx->syx", generator_matrix, field, precision=HIGHEST_PRECISION)
        jumped = lax.all_to_all(jump_line, "gx", split_axis=1, concat_axis=0, tiled=True).reshape(
            regimes, y_rows, x_cols
        )
        beside_all = with_halo(
            jnp.stack([field, drift[0][None] * field, drift[1][None] * field]),
            (("gx", 3), ("gy", 2)),
            1,
        )
        field_pad = beside_all[0]
        laplace = (
            field_pad[:, 1:-1, 2:]
            + field_pad[:, 1:-1, :-2]
            + field_pad[:, 2:, 1:-1]
            + field_pad[:, :-2, 1:-1]
            - 4.0 * field
        )
        flow_x = (beside_all[1][:, 1:-1, 2:] - beside_all[1][:, 1:-1, :-2]) * 0.5
        flow_y = (beside_all[2][:, 2:, 1:-1] - beside_all[2][:, :-2, 1:-1]) * 0.5
        updated = (
            field
            + scale_diff * laplace
            - flow_x
            - flow_y
            + scale_jump * (jumped - field)
            - kill[None] * field
            + mixing
        )
        sums.append(jnp.sum(updated))
        field = updated
    cell_count = field.size * lax.axis_size("gx") * lax.axis_size("gy")
    totals = tree_sum(jnp.broadcast_to(jnp.stack(sums)[:, None], (len(sums), 128)))[:, 0]
    scale = jnp.float32(1.0)
    for sweep_index in range(SWEEPS):
        mass_mean = totals[sweep_index] / scale / cell_count
        if sweep_index == SWEEPS - 1:
            field = field / scale / mass_mean
        scale = scale * mass_mean
    return field


def solution(mesh):
    return jax.shard_map(
        local,
        mesh=mesh,
        in_specs=(
            P(None, "gy", "gx"),
            P(None, "gy", "gx"),
            P("gy", "gx"),
            P(),
            P(),
            P(),
            P(),
            P(),
            P(),
        ),
        out_specs=P(None, "gy", "gx"),
        check_vma=False,
    )
```

profile of v0, /device:TPU:32, one launch (start us, length us, event | category | flops | bytes accessed | tf_op | source)
XLA Modules:
  0.0 192.1 jit_solution(3168898550453237916)
XLA Ops:
  2.1 7.0 %all-to-all-start = ((f32[16,4,2048]{2,1,0:T(4,128)}), f32[16,4,2048]{2,1,0:T(4,128)S(1)}, u32[]{:S(2)}, u32[]{:S(2)}) async-start(f32[16,4,2048]{2,1,0:T(4,128)} %all_to_all.44), calls=%async_computation | async-start | bytes 1048576 | tf_op jit(solution)/shard_map/all_to_all | solution.py:150
  13.0 3.4 %collective-permute-start.1 = (f32[3,8,8,1]{3,1,2,0:T(8,128)S(1)}, f32[3,8,8,1]{3,1,2,0:T(8,128)}, u32[]{:S(2)}, u32[]{:S(2)}) collective-permute-start(f32[3,8,8,1]{3,1,2,0:T(8,128)S(1)} %get-tuple-element.17), channel_id=1, source_target_pairs={{16,0},{32,16},{48,32},{64,48},{80,64},{96,80},{112,96},{128,112},... | collective-permute-start | bytes 2312 | tf_op jit(solution)/shard_map/ppermute | solution.py:22
  28.2 2.3 %concatenate.15 = f32[3,8,8,2050]{3,1,2,0:T(8,128)S(1)} concatenate(f32[3,8,8,1]{3,1,2,0:T(8,128)S(1)} %collective-permute-done, f32[3,8,8,2048]{3,1,2,0:T(8,128)} %copy-done.2, f32[3,8,8,1]{3,1,2,0:T(8,128)} %collective-permute-done.1), dimensions={3} | concatenate | bytes 3148800 | tf_op jit(solution)/shard_map/concatenate | solution.py:23
  32.6 3.2 %collective-permute-done.2 = f32[3,8,1,2050]{3,1,2,0:T(8,128)S(1)} collective-permute-done((f32[3,8,1,2050]{3,1,2,0:T(8,128)S(1)}, f32[3,8,1,2050]{3,1,2,0:T(8,128)S(1)}, u32[]{:S(2)}, u32[]{:S(2)}) %collective-permute-start.2) | collective-permute-done | bytes 196832 | tf_op jit(solution)/shard_map/ppermute | solution.py:21
  57.2 2.2 %copy.58 = f32[4,16,2048]{2,0,1:T(4,128)} copy(f32[4,16,2048]{2,1,0:T(8,128)} %div.53) | data formatting | bytes 1048576 | tf_op jit(solution)/shard_map/div | solution.py:80
  59.3 4.2 %all-to-all-start.1 = ((f32[4,16,2048]{2,0,1:T(4,128)}), f32[4,16,2048]{2,0,1:T(4,128)}, u32[]{:S(2)}, u32[]{:S(2)}) async-start(f32[4,16,2048]{2,0,1:T(4,128)} %copy.58), calls=%async_computation.1 | async-start | bytes 1048576 | tf_op jit(solution)/shard_map/all_to_all | solution.py:158
  65.0 10.2 %all-to-all-done.1 = f32[4,16,2048]{2,0,1:T(4,128)} async-done(((f32[4,16,2048]{2,0,1:T(4,128)}), f32[4,16,2048]{2,0,1:T(4,128)}, u32[]{:S(2)}, u32[]{:S(2)}) %all-to-all-start.1) | async-done | bytes 524320 | tf_op jit(solution)/shard_map/all_to_all | solution.py:158
  76.4 3.3 %convolution_add_fusion.1 = f32[8,8,2048]{2,0,1:T(8,128)S(1)} fusion(f32[8,10,2050]{2,0,1:T(8,128)} %get-tuple-element.9, f32[8,10,2050]{2,0,1:T(8,128)} %get-tuple-element.10, f32[8,10,2050]{2,0,1:T(8,128)} %get-tuple-element.8, f32[8,8,2048]{2,1,0:T(8,128)S(1)} %reshape.115, f32[8,8,2048]{2,1,0:T(8,128)S(1)} %copy-done.4, f32[8,2048]{1,0:T(8,128)S(1)} %copy-done.10, ...), kind=kOutput, calls=%fused_computation.1 | convolution fusion | flops 15073664 | bytes 6362624 | tf_op jit(solution)/shard_map/rs,ryx->syx/dot_general | solution.py:157
  81.5 4.8 %collective-permute-start.5 = (f32[3,8,8,1]{3,1,2,0:T(8,128)S(1)}, f32[3,8,8,1]{3,1,2,0:T(8,128)S(1)}, u32[]{:S(2)}, u32[]{:S(2)}) collective-permute-start(f32[3,8,8,1]{3,1,2,0:T(8,128)S(1)} %get-tuple-element.15), channel_id=1, source_target_pairs={{16,0},{32,16},{48,32},{64,48},{80,64},{96,80},{112,96},{128,112},... | collective-permute-start | bytes 2312 | tf_op jit(solution)/shard_map/ppermute | solution.py:22
  86.3 3.5 %collective-permute-done.4 = f32[3,8,8,1]{3,1,2,0:T(8,128)S(1)} collective-permute-done((f32[3,8,8,1]{3,1,2,0:T(8,128)S(1)}, f32[3,8,8,1]{3,1,2,0:T(8,128)S(1)}, u32[]{:S(2)}, u32[]{:S(2)}) %collective-permute-start.4) | collective-permute-done | bytes 800 | tf_op jit(solution)/shard_map/ppermute | solution.py:21
  95.6 6.9 %all-to-all-start.2 = ((f32[16,4,2048]{2,1,0:T(4,128)}), f32[16,4,2048]{2,1,0:T(4,128)S(1)}, u32[]{:S(2)}, u32[]{:S(2)}) async-start(f32[16,4,2048]{2,1,0:T(4,128)} %all_to_all.49), calls=%async_computation.2 | async-start | bytes 1048576 | tf_op jit(solution)/shard_map/all_to_all | solution.py:150
  102.5 2.5 %pad_maximum_fusion.1 = f32[3,8,10,2050]{3,1,2,0:T(8,128)} fusion(f32[3,8,1,2050]{3,1,2,0:T(8,128)} %collective-permute-done.7, f32[3,8,8,2050]{3,1,2,0:T(8,128)S(1)} %concatenate.18, f32[3,8,1,2050]{3,1,2,0:T(8,128)} %collective-permute-done.6), kind=kLoop, calls=%fused_computation.3 | loop fusion | flops 984000 | bytes 3936000 | tf_op jit(solution)/shard_map/concatenate | solution.py:23
  105.0 9.2 %all-to-all-done.2 = f32[16,4,2048]{2,1,0:T(4,128)S(1)} async-done(((f32[16,4,2048]{2,1,0:T(4,128)}), f32[16,4,2048]{2,1,0:T(4,128)S(1)}, u32[]{:S(2)}, u32[]{:S(2)}) %all-to-all-start.2) | async-done | bytes 524320 | tf_op jit(solution)/shard_map/all_to_all | solution.py:150
  134.3 3.6 %all-to-all-start.3 = ((f32[4,16,2048]{2,0,1:T(4,128)}), f32[4,16,2048]{2,0,1:T(4,128)S(1)}, u32[]{:S(2)}, u32[]{:S(2)}) async-start(f32[4,16,2048]{2,0,1:T(4,128)} %copy.66), calls=%async_computation.3 | async-start | bytes 1048576 | tf_op jit(solution)/shard_map/all_to_all | solution.py:158
  139.2 9.3 %all-to-all-done.3 = f32[4,16,2048]{2,0,1:T(4,128)S(1)} async-done(((f32[4,16,2048]{2,0,1:T(4,128)}), f32[4,16,2048]{2,0,1:T(4,128)S(1)}, u32[]{:S(2)}, u32[]{:S(2)}) %all-to-all-start.3) | async-done | bytes 524320 | tf_op jit(solution)/shard_map/all_to_all | solution.py:158
  148.7 3.7 %fusion.300 = (f32[]{:T(128)}, f32[8,8,2048]{2,0,1:T(8,128)S(1)}) fusion(f32[8,8,2048]{2,0,1:T(8,128)S(1)} %convolution_add_fusion.1, f32[8,8]{1,0:T(8,128)S(1)} %select_reduce_fusion, f32[8]{0:T(128)S(1)} %fusion.151, f32[8,2048]{1,0:T(8,128)S(1)} %copy-done.10, f32[8,8,2048]{2,1,0:T(8,128)S(1)} %reshape.117, f32[8]{0:T(128)S(1)} %copy-done.11, ...), kind=kOutput, calls=%fused_computation.345 | convolution fusion | flops 15204735 | bytes 6362628 | tf_op jit(solution)/shard_map/rs,ryx->syx/dot_general | solution.py:157
  154.5 3.0 %collective-permute-done.8 = f32[2,128]{1,0:T(2,128)S(1)} collective-permute-done((f32[2,128]{1,0:T(2,128)S(1)}, f32[2,128]{1,0:T(2,128)S(1)}, u32[]{:S(2)}, u32[]{:S(2)}) %collective-permute-start.8) | collective-permute-done | bytes 1056 | tf_op jit(solution)/shard_map/ppermute | solution.py:101
  158.7 4.0 %collective-permute-done.9 = f32[2,128]{1,0:T(2,128)S(1)} collective-permute-done((f32[2,128]{1,0:T(2,128)S(1)}, f32[2,128]{1,0:T(2,128)S(1)}, u32[]{:S(2)}, u32[]{:S(2)}) %collective-permute-start.9) | collective-permute-done | bytes 1056 | tf_op jit(solution)/shard_map/ppermute | solution.py:101
  162.7 3.6 %collective-permute-done.10 = f32[2,128]{1,0:T(2,128)S(1)} collective-permute-done((f32[2,128]{1,0:T(2,128)S(1)}, f32[2,128]{1,0:T(2,128)S(1)}, u32[]{:S(2)}, u32[]{:S(2)}) %collective-permute-start.10) | collective-permute-done | bytes 1056 | tf_op jit(solution)/shard_map/ppermute | solution.py:101
  167.4 4.0 %collective-permute-done.11 = f32[2,128]{1,0:T(2,128)S(1)} collective-permute-done((f32[2,128]{1,0:T(2,128)S(1)}, f32[2,128]{1,0:T(2,128)S(1)}, u32[]{:S(2)}, u32[]{:S(2)}) %collective-permute-start.11) | collective-permute-done | bytes 1056 | tf_op jit(solution)/shard_map/ppermute | solution.py:101
  173.1 3.0 %collective-permute-done.13 = f32[2,128]{1,0:T(2,128)S(1)} collective-permute-done((f32[2,128]{1,0:T(2,128)S(1)}, f32[2,128]{1,0:T(2,128)S(1)}, u32[]{:S(2)}, u32[]{:S(2)}) %collective-permute-start.13) | collective-permute-done | bytes 1056 | tf_op jit(solution)/shard_map/ppermute | solution.py:101
  176.5 4.1 %collective-permute-done.14 = f32[2,128]{1,0:T(2,128)S(1)} collective-permute-done((f32[2,128]{1,0:T(2,128)S(1)}, f32[2,128]{1,0:T(2,128)S(1)}, u32[]{:S(2)}, u32[]{:S(2)}) %collective-permute-start.14) | collective-permute-done | bytes 1056 | tf_op jit(solution)/shard_map/ppermute | solution.py:101
  180.6 5.0 %collective-permute-start.15 = (f32[2,128]{1,0:T(2,128)S(1)}, f32[2,128]{1,0:T(2,128)S(1)}, u32[]{:S(2)}, u32[]{:S(2)}) collective-permute-start(f32[2,128]{1,0:T(2,128)S(1)} %add.263), channel_id=1, source_target_pairs={{0,8},{1,9},{2,10},{3,11},{4,12},{5,13},{6,14},{7,15},{8,0},{9,1},... | collective-permute-start | bytes 3080 | tf_op jit(solution)/shard_map/ppermute | solution.py:101
  185.6 2.5 %collective-permute-done.15 = f32[2,128]{1,0:T(2,128)S(1)} collective-permute-done((f32[2,128]{1,0:T(2,128)S(1)}, f32[2,128]{1,0:T(2,128)S(1)}, u32[]{:S(2)}, u32[]{:S(2)}) %collective-permute-start.15) | collective-permute-done | bytes 1056 | tf_op jit(solution)/shard_map/ppermute | solution.py:101
  (128 shorter events, 80.6 us)
Async XLA Ops:
  0.0 9.1 %copy-start.4 = (f32[8,8,2048]{2,1,0:T(8,128)S(1)}, f32[8,8,2048]{2,1,0:T(8,128)}, u32[]{:S(2)}) copy-start(f32[8,8,2048]{2,1,0:T(8,128)} %param.9) | copy-start | bytes 1572868
  2.1 35.2 %all-to-all-start = ((f32[16,4,2048]{2,1,0:T(4,128)}), f32[16,4,2048]{2,1,0:T(4,128)S(1)}, u32[]{:S(2)}, u32[]{:S(2)}) async-start(f32[16,4,2048]{2,1,0:T(4,128)} %all_to_all.44), calls=%async_computation | async-start | bytes 1048576 | tf_op jit(solution)/shard_map/all_to_all | solution.py:150
  11.0 17.2 %collective-permute-start = (f32[3,8,8,1]{3,1,2,0:T(8,128)S(1)}, f32[3,8,8,1]{3,1,2,0:T(8,128)S(1)}, u32[]{:S(2)}, u32[]{:S(2)}) collective-permute-start(f32[3,8,8,1]{3,1,2,0:T(8,128)S(1)} %get-tuple-element.18), channel_id=1, source_target_pairs={{0,16},{16,32},{32,48},{48,64},{64,80},{80,96},{96,112},{112,128},... | collective-permute-start | bytes 2312 | tf_op jit(solution)/shard_map/ppermute | solution.py:21
  13.0 15.2 %collective-permute-start.1 = (f32[3,8,8,1]{3,1,2,0:T(8,128)S(1)}, f32[3,8,8,1]{3,1,2,0:T(8,128)}, u32[]{:S(2)}, u32[]{:S(2)}) collective-permute-start(f32[3,8,8,1]{3,1,2,0:T(8,128)S(1)} %get-tuple-element.17), channel_id=1, source_target_pairs={{16,0},{32,16},{48,32},{64,48},{80,64},{96,80},{112,96},{128,112},... | collective-permute-start | bytes 2312 | tf_op jit(solution)/shard_map/ppermute | solution.py:22
  30.5 5.2 %collective-permute-start.2 = (f32[3,8,1,2050]{3,1,2,0:T(8,128)S(1)}, f32[3,8,1,2050]{3,1,2,0:T(8,128)S(1)}, u32[]{:S(2)}, u32[]{:S(2)}) collective-permute-start(f32[3,8,1,2050]{3,1,2,0:T(8,128)S(1)} %get-tuple-element.13), channel_id=1, source_target_pairs={{0,1},{1,2},{2,3},{3,4},{4,5},{5,6},{6,7},{7,8},{8,9},{9,10},{10,1... | collective-permute-start | bytes 590408 | tf_op jit(solution)/shard_map/ppermute | solution.py:21
  30.6 5.2 %collective-permute-start.3 = (f32[3,8,1,2050]{3,1,2,0:T(8,128)S(1)}, f32[3,8,1,2050]{3,1,2,0:T(8,128)S(1)}, u32[]{:S(2)}, u32[]{:S(2)}) collective-permute-start(f32[3,8,1,2050]{3,1,2,0:T(8,128)S(1)} %get-tuple-element.14), channel_id=1, source_target_pairs={{1,0},{2,1},{3,2},{4,3},{5,4},{6,5},{7,6},{8,7},{9,8},{10,9},{11,1... | collective-permute-start | bytes 590408 | tf_op jit(solution)/shard_map/ppermute | solution.py:22
  59.3 15.9 %all-to-all-start.1 = ((f32[4,16,2048]{2,0,1:T(4,128)}), f32[4,16,2048]{2,0,1:T(4,128)}, u32[]{:S(2)}, u32[]{:S(2)}) async-start(f32[4,16,2048]{2,0,1:T(4,128)} %copy.58), calls=%async_computation.1 | async-start | bytes 1048576 | tf_op jit(solution)/shard_map/all_to_all | solution.py:158
  63.6 12.8 %copy-start.10 = (f32[8,2048]{1,0:T(8,128)S(1)}, f32[8,2048]{1,0:T(8,128)}, u32[]{:S(2)}) copy-start(f32[8,2048]{1,0:T(8,128)} %param.11) | copy-start | bytes 196612
  63.6 12.8 %copy-start.11 = (f32[8]{0:T(128)S(1)}, f32[8]{0:T(128)}, u32[]{:S(2)}) copy-start(f32[8]{0:T(128)} %param.13) | copy-start | bytes 100
  63.6 12.8 %copy-start.12 = (f32[8]{0:T(128)S(1)}, f32[8]{0:T(128)}, u32[]{:S(2)}) copy-start(f32[8]{0:T(128)} %param.12) | copy-start | bytes 100
  80.9 8.9 %collective-permute-start.4 = (f32[3,8,8,1]{3,1,2,0:T(8,128)S(1)}, f32[3,8,8,1]{3,1,2,0:T(8,128)S(1)}, u32[]{:S(2)}, u32[]{:S(2)}) collective-permute-start(f32[3,8,8,1]{3,1,2,0:T(8,128)S(1)} %get-tuple-element.16), channel_id=1, source_target_pairs={{0,16},{16,32},{32,48},{48,64},{64,80},{80,96},{96,112},{112,128},... | collective-permute-start | bytes 2312 | tf_op jit(solution)/shard_map/ppermute | solution.py:21
  81.5 8.3 %collective-permute-start.5 = (f32[3,8,8,1]{3,1,2,0:T(8,128)S(1)}, f32[3,8,8,1]{3,1,2,0:T(8,128)S(1)}, u32[]{:S(2)}, u32[]{:S(2)}) collective-permute-start(f32[3,8,8,1]{3,1,2,0:T(8,128)S(1)} %get-tuple-element.15), channel_id=1, source_target_pairs={{16,0},{32,16},{48,32},{64,48},{80,64},{96,80},{112,96},{128,112},... | collective-permute-start | bytes 2312 | tf_op jit(solution)/shard_map/ppermute | solution.py:22
  92.6 9.9 %collective-permute-start.6 = (f32[3,8,1,2050]{3,1,2,0:T(8,128)}, f32[3,8,1,2050]{3,1,2,0:T(8,128)}, u32[]{:S(2)}, u32[]{:S(2)}) collective-permute-start(f32[3,8,1,2050]{3,1,2,0:T(8,128)} %get-tuple-element.11), channel_id=1, source_target_pairs={{0,1},{1,2},{2,3},{3,4},{4,5},{5,6},{6,7},{7,8},{8,9},{9,10},{10,1... | collective-permute-start | bytes 590408 | tf_op jit(solution)/shard_map/ppermute | solution.py:21
  92.7 9.8 %collective-permute-start.7 = (f32[3,8,1,2050]{3,1,2,0:T(8,128)S(1)}, f32[3,8,1,2050]{3,1,2,0:T(8,128)}, u32[]{:S(2)}, u32[]{:S(2)}) collective-permute-start(f32[3,8,1,2050]{3,1,2,0:T(8,128)S(1)} %get-tuple-element.12), channel_id=1, source_target_pairs={{1,0},{2,1},{3,2},{4,3},{5,4},{6,5},{7,6},{8,7},{9,8},{10,9},{11,1... | collective-permute-start | bytes 590408 | tf_op jit(solution)/shard_map/ppermute | solution.py:22
  95.6 18.7 %all-to-all-start.2 = ((f32[16,4,2048]{2,1,0:T(4,128)}), f32[16,4,2048]{2,1,0:T(4,128)S(1)}, u32[]{:S(2)}, u32[]{:S(2)}) async-start(f32[16,4,2048]{2,1,0:T(4,128)} %all_to_all.49), calls=%async_computation.2 | async-start | bytes 1048576 | tf_op jit(solution)/shard_map/all_to_all | solution.py:150
  134.3 14.3 %all-to-all-start.3 = ((f32[4,16,2048]{2,0,1:T(4,128)}), f32[4,16,2048]{2,0,1:T(4,128)S(1)}, u32[]{:S(2)}, u32[]{:S(2)}) async-start(f32[4,16,2048]{2,0,1:T(4,128)} %copy.66), calls=%async_computation.3 | async-start | bytes 1048576 | tf_op jit(solution)/shard_map/all_to_all | solution.py:158
  153.9 3.6 %collective-permute-start.8 = (f32[2,128]{1,0:T(2,128)S(1)}, f32[2,128]{1,0:T(2,128)S(1)}, u32[]{:S(2)}, u32[]{:S(2)}) collective-permute-start(f32[2,128]{1,0:T(2,128)S(1)} %broadcast_in_dim.34), channel_id=1, source_target_pairs={{0,16},{16,0},{32,48},{48,32},{64,80},{80,64},{96,112},{112,96},{1... | collective-permute-start | bytes 3080 | tf_op jit(solution)/shard_map/ppermute | solution.py:101
  157.6 5.1 %collective-permute-start.9 = (f32[2,128]{1,0:T(2,128)S(1)}, f32[2,128]{1,0:T(2,128)S(1)}, u32[]{:S(2)}, u32[]{:S(2)}) collective-permute-start(f32[2,128]{1,0:T(2,128)S(1)} %broadcast_add_fusion), channel_id=1, source_target_pairs={{0,32},{16,48},{32,0},{48,16},{64,96},{80,112},{96,64},{112,80},{1... | collective-permute-start | bytes 3080 | tf_op jit(solution)/shard_map/ppermute | solution.py:101
  162.7 3.6 %collective-permute-start.10 = (f32[2,128]{1,0:T(2,128)S(1)}, f32[2,128]{1,0:T(2,128)S(1)}, u32[]{:S(2)}, u32[]{:S(2)}) collective-permute-start(f32[2,128]{1,0:T(2,128)S(1)} %fusion.308), channel_id=1, source_target_pairs={{0,64},{16,80},{32,96},{48,112},{64,0},{80,16},{96,32},{112,48},{1... | collective-permute-start | bytes 3080 | tf_op jit(solution)/shard_map/ppermute | solution.py:101
  166.3 5.1 %collective-permute-start.11 = (f32[2,128]{1,0:T(2,128)S(1)}, f32[2,128]{1,0:T(2,128)S(1)}, u32[]{:S(2)}, u32[]{:S(2)}) collective-permute-start(f32[2,128]{1,0:T(2,128)S(1)} %add.259), channel_id=1, source_target_pairs={{0,128},{16,144},{32,160},{48,176},{64,192},{80,208},{96,224},{112... | collective-permute-start | bytes 3080 | tf_op jit(solution)/shard_map/ppermute | solution.py:101
  171.4 1.2 collective-permute-start.12
  172.5 3.6 %collective-permute-start.13 = (f32[2,128]{1,0:T(2,128)S(1)}, f32[2,128]{1,0:T(2,128)S(1)}, u32[]{:S(2)}, u32[]{:S(2)}) collective-permute-start(f32[2,128]{1,0:T(2,128)S(1)} %add.261), channel_id=1, source_target_pairs={{0,2},{1,3},{2,0},{3,1},{4,6},{5,7},{6,4},{7,5},{8,10},{9,11},{10,... | collective-permute-start | bytes 3080 | tf_op jit(solution)/shard_map/ppermute | solution.py:101
  176.1 4.5 %collective-permute-start.14 = (f32[2,128]{1,0:T(2,128)S(1)}, f32[2,128]{1,0:T(2,128)S(1)}, u32[]{:S(2)}, u32[]{:S(2)}) collective-permute-start(f32[2,128]{1,0:T(2,128)S(1)} %add.262), channel_id=1, source_target_pairs={{0,4},{1,5},{2,6},{3,7},{4,0},{5,1},{6,2},{7,3},{8,12},{9,13},{10,... | collective-permute-start | bytes 3080 | tf_op jit(solution)/shard_map/ppermute | solution.py:101
  180.6 7.5 %collective-permute-start.15 = (f32[2,128]{1,0:T(2,128)S(1)}, f32[2,128]{1,0:T(2,128)S(1)}, u32[]{:S(2)}, u32[]{:S(2)}) collective-permute-start(f32[2,128]{1,0:T(2,128)S(1)} %add.263), channel_id=1, source_target_pairs={{0,8},{1,9},{2,10},{3,11},{4,12},{5,13},{6,14},{7,15},{8,0},{9,1},... | collective-permute-start | bytes 3080 | tf_op jit(solution)/shard_map/ppermute | solution.py:101
  (9 other events, 55.9 us)
where the time goes:
time: 196 us; the launch traced here: 192 us
  waiting for transfers between devices  60.8 us (31%)
  matrix products  49.5 us (25%)
  starting transfers between devices  44.8 us (23%)
  local copies, waits for them, and re-layouts  25.9 us (13%)
  other arithmetic  8.27 us (4%)
  between operations  2.88 us (1%)
    ppermute x8, waiting for transfers between devices, tree_sum(): values = values + lax.ppermute(values, axis, pairs)  25.3 us
    all_to_all x2, waiting for transfers between devices, local(): lax.all_to_all(jump_line, 'gx', split_axis=1, concat_axis=0, tiled=True)  19.5 us
    all_to_all x2, starting transfers between devices, local(): lax.all_to_all(field.reshape(regimes * y_rows, x_cols), 'gx', split_axis=...  13.9 us
    ppermute x4, starting transfers between devices, with_halo(): after = lax.ppermute(leading, axis, down)  11.6 us
    all_to_all x2, waiting for transfers between devices, local(): lax.all_to_all(field.reshape(regimes * y_rows, x_cols), 'gx', split_axis=...  9.25 us
    ppermute x8, starting transfers between devices, tree_sum(): values = values + lax.ppermute(values, axis, pairs)  8.68 us
    all_to_all x2, starting transfers between devices, local(): lax.all_to_all(jump_line, 'gx', split_axis=1, concat_axis=0, tiled=True)  7.81 us
    dot_general x2, matrix products, local(): jnp.einsum('rs,ryx->syx', generator_matrix, field, precision=HIGHEST_PREC...  7.03 us
  transfers between devices with their start and end apart: 20, of which 13 were waited for; matrix products, arithmetic and copies ran while one was open for 11% of the time, Pallas kernels for 0%

commit v1 on v0

--- a/solution.py
+++ b/solution.py
@@ -3,6 +3,8 @@
 import jax
 import jax.numpy as jnp
 from jax import lax
+from jax.experimental import pallas as pl
+from jax.experimental.pallas import tpu as pltpu
 from jax.sharding import PartitionSpec as P
 
 SWEEPS = 2
@@ -92,15 +94,64 @@
     return offdiag - jnp.diag(jnp.sum(offdiag, axis=1))
 
 
+def exchange_kernel(x_ref, o_ref, buf, send_sems, recv_sems, init_sem):
+    gx, gy = lax.axis_index("gx"), lax.axis_index("gy")
+    nx, ny = lax.axis_size("gx"), lax.axis_size("gy")
+    me = gx * ny + gy
+    partners = []
+    stride = 1
+    while stride < ny:
+        bit = (gy // stride) % 2
+        partners.append((gx, gy + stride - 2 * stride * bit))
+        stride *= 2
+    stride = 1
+    while stride < nx:
+        bit = (gx // stride) % 2
+        partners.append((gx + stride - 2 * stride * bit, gy))
+        stride *= 2
+    barrier = pltpu.get_barrier_semaphore()
+    for peer in partners:
+        pl.semaphore_signal(barrier, 1, device_id=peer, device_id_type=pl.DeviceIdType.MESH)
+    pl.semaphore_wait(barrier, len(partners))
+    own = pltpu.make_async_copy(x_ref, buf.at[pl.ds(me, 1)], init_sem)
+    own.start()
+    own.wait()
+    for stage, peer in enumerate(partners):
+        size = 1 << stage
+        start = (me // size) * size
+        block = buf.at[pl.ds(start, size)]
+        copy = pltpu.make_async_remote_copy(
+            src_ref=block,
+            dst_ref=block,
+            send_sem=send_sems.at[stage],
+            recv_sem=recv_sems.at[stage],
+            device_id=peer,
+            device_id_type=pl.DeviceIdType.MESH,
+        )
+        copy.start()
+        copy.wait()
+    o_ref[...] = jnp.sum(buf[...], axis=0)
+
+
 def tree_sum(values):
-    for axis in ("gx", "gy"):
-        peers = lax.axis_size(axis)
-        step = 1
-        while step < peers:
-            pairs = [(i, i ^ step) for i in range(peers)]
-            values = values + lax.ppermute(values, axis, pairs)
-            step *= 2
-    return values
+    count = values.shape[0]
+    peers = lax.axis_size("gx") * lax.axis_size("gy")
+    stages = peers.bit_length() - 1
+    slab = jnp.pad(values[None, :], ((0, 7), (0, 128 - count)))[None]
+    total = pl.pallas_call(
+        exchange_kernel,
+        out_shape=jax.ShapeDtypeStruct((8, 128), jnp.float32),
+        in_specs=[pl.BlockSpec(memory_space=pltpu.VMEM)],
+        out_specs=pl.BlockSpec(memory_space=pltpu.VMEM),
+        scratch_shapes=[
+            pltpu.VMEM((peers, 8, 128), jnp.float32),
+            pltpu.SemaphoreType.DMA((stages,)),
+            pltpu.SemaphoreType.DMA((stages,)),
+            pltpu.SemaphoreType.DMA,
+        ],
+        compiler_params=pltpu.CompilerParams(collective_id=0, has_side_effects=True),
+    )(slab)
+    return total[0, :count]
 
 
 def local(
@@ -185,7 +236,7 @@
         sums.append(jnp.sum(updated))
         field = updated
     cell_count = field.size * lax.axis_size("gx") * lax.axis_size("gy")
-    totals = tree_sum(jnp.broadcast_to(jnp.stack(sums)[:, None], (len(sums), 128)))[:, 0]
+    totals = tree_sum(jnp.stack(sums))
     scale = jnp.float32(1.0)
     for sweep_index in range(SWEEPS):
         mass_mean = totals[sweep_index] / scale / cell_count

time: 196 us -> 205 us (1.046)
  Pallas kernels: 0 us -> 42.7 us
  waiting for transfers between devices: 60.8 us -> 35.2 us
  starting transfers between devices: 44.8 us -> 36.3 us
    pallas_call x0 -> x1, Pallas kernels: none -> 42.7 us  [tree_sum(): pl.pallas_call(exchange_kernel, out_shape=jax.ShapeDtypeStruct((8, 128),...]
    ppermute x8 -> x0, waiting for transfers between devices: 25.3 us -> none  [tree_sum(): values = values + lax.ppermute(values, axis, pairs)]
    ppermute x8 -> x0, starting transfers between devices: 8.68 us -> none  [tree_sum(): values = values + lax.ppermute(values, axis, pairs)]
  transfers between devices with their start and end apart: 20 -> 12, of which waited for: 13 -> 5; matrix products, arithmetic and copies ran while one was open for 11% -> 11% of each run, Pallas kernels for 0% -> 0%
where the time goes in v1:
time: 205 us; the launch traced here: 202 us
  matrix products  49.4 us (24%)
  Pallas kernels  42.7 us (21%)
  starting transfers between devices  36.3 us (18%)
  waiting for transfers between devices  35.2 us (17%)
  local copies, waits for them, and re-layouts  27.4 us (13%)
  other arithmetic  8.01 us (4%)
  between operations  2.71 us (1%)
    pallas_call x1, Pallas kernels, tree_sum(): pl.pallas_call(exchange_kernel, out_shape=jax.ShapeDtypeStruct((8, 128),...  42.7 us
    all_to_all x2, waiting for transfers between devices, local(): lax.all_to_all(jump_line, 'gx', split_axis=1, concat_axis=0, tiled=True)  19.5 us
    all_to_all x2, starting transfers between devices, local(): lax.all_to_all(field.reshape(regimes * y_rows, x_cols), 'gx', split_axis=...  14.2 us
    ppermute x4, starting transfers between devices, with_halo(): after = lax.ppermute(leading, axis, down)  11.6 us
    all_to_all x2, waiting for transfers between devices, local(): lax.all_to_all(field.reshape(regimes * y_rows, x_cols), 'gx', split_axis=...  9 us
    all_to_all x2, starting transfers between devices, local(): lax.all_to_all(jump_line, 'gx', split_axis=1, concat_axis=0, tiled=True)  7.81 us
    dot_general x2, matrix products, local(): jnp.einsum('rs,ryx->syx', generator_matrix, field, precision=HIGHEST_PREC...  7.11 us
    ppermute x4, waiting for transfers between devices, with_halo(): before = lax.ppermute(last, axis, up)  6.71 us
  transfers between devices with their start and end apart: 12, of which 5 were waited for; matrix products, arithmetic and copies ran while one was open for 11% of the time, Pallas kernels for 0%

profile of v1, /device:TPU:32, one launch (start us, length us, event | category | flops | bytes accessed | tf_op | source)
XLA Modules:
  0.0 201.7 jit_solution(11486620652716710976)
XLA Ops:
  0.0 2.0 %all_to_all.44 = f32[16,4,2048]{2,1,0:T(4,128)} reshape(f32[8,8,2048]{2,1,0:T(8,128)} %param.9) | data formatting | bytes 1048576 | tf_op jit(solution)/shard_map/all_to_all | solution.py:201
  2.1 7.0 %all-to-all-start = ((f32[16,4,2048]{2,1,0:T(4,128)}), f32[16,4,2048]{2,1,0:T(4,128)S(1)}, u32[]{:S(2)}, u32[]{:S(2)}) async-start(f32[16,4,2048]{2,1,0:T(4,128)} %all_to_all.44), calls=%async_computation | async-start | bytes 1048576 | tf_op jit(solution)/shard_map/all_to_all | solution.py:201
  10.9 2.0 collective-permute-start
  12.9 3.4 %collective-permute-start.1 = (f32[3,8,8,1]{3,1,2,0:T(8,128)S(1)}, f32[3,8,8,1]{3,1,2,0:T(8,128)}, u32[]{:S(2)}, u32[]{:S(2)}) collective-permute-start(f32[3,8,8,1]{3,1,2,0:T(8,128)S(1)} %get-tuple-element.17), channel_id=1, source_target_pairs={{16,0},{32,16},{48,32},{64,48},{80,64},{96,80},{112,96},{128,112},... | collective-permute-start | bytes 2312 | tf_op jit(solution)/shard_map/ppermute | solution.py:24
  24.4 1.8 convolution_add_fusion.6
  26.2 1.8 convolution_subtract_fusion.6
  28.5 2.3 %concatenate.15 = f32[3,8,8,2050]{3,1,2,0:T(8,128)S(1)} concatenate(f32[3,8,8,1]{3,1,2,0:T(8,128)S(1)} %collective-permute-done, f32[3,8,8,2048]{3,1,2,0:T(8,128)} %copy-done.2, f32[3,8,8,1]{3,1,2,0:T(8,128)} %collective-permute-done.1), dimensions={3} | concatenate | bytes 3148800 | tf_op jit(solution)/shard_map/concatenate | solution.py:25
  32.9 3.2 %collective-permute-done.2 = f32[3,8,1,2050]{3,1,2,0:T(8,128)S(1)} collective-permute-done((f32[3,8,1,2050]{3,1,2,0:T(8,128)S(1)}, f32[3,8,1,2050]{3,1,2,0:T(8,128)S(1)}, u32[]{:S(2)}, u32[]{:S(2)}) %collective-permute-start.2) | collective-permute-done | bytes 196832 | tf_op jit(solution)/shard_map/ppermute | solution.py:23
  47.6 1.8 fusion.59
  55.1 2.1 %div.53 = f32[4,16,2048]{2,1,0:T(8,128)} reshape(f32[4,128,256]{2,1,0:T(8,128)} %fusion.3) | data formatting | bytes 1048576 | tf_op jit(solution)/shard_map/div | solution.py:82
  57.2 2.2 %copy.58 = f32[4,16,2048]{2,0,1:T(4,128)} copy(f32[4,16,2048]{2,1,0:T(8,128)} %div.53) | data formatting | bytes 1048576 | tf_op jit(solution)/shard_map/div | solution.py:82
  59.4 4.2 %all-to-all-start.1 = ((f32[4,16,2048]{2,0,1:T(4,128)}), f32[4,16,2048]{2,0,1:T(4,128)}, u32[]{:S(2)}, u32[]{:S(2)}) async-start(f32[4,16,2048]{2,0,1:T(4,128)} %copy.58), calls=%async_computation.1 | async-start | bytes 1048576 | tf_op jit(solution)/shard_map/all_to_all | solution.py:209
  65.1 10.2 %all-to-all-done.1 = f32[4,16,2048]{2,0,1:T(4,128)} async-done(((f32[4,16,2048]{2,0,1:T(4,128)}), f32[4,16,2048]{2,0,1:T(4,128)}, u32[]{:S(2)}, u32[]{:S(2)}) %all-to-all-start.1) | async-done | bytes 524320 | tf_op jit(solution)/shard_map/all_to_all | solution.py:209
  76.5 3.3 %convolution_add_fusion.1 = f32[8,8,2048]{2,0,1:T(8,128)S(1)} fusion(f32[8,10,2050]{2,0,1:T(8,128)} %get-tuple-element.9, f32[8,10,2050]{2,0,1:T(8,128)} %get-tuple-element.10, f32[8,10,2050]{2,0,1:T(8,128)} %get-tuple-element.8, f32[8,8,2048]{2,1,0:T(8,128)S(1)} %reshape.114, f32[8,8,2048]{2,1,0:T(8,128)S(1)} %copy-done.4, f32[8,2048]{1,0:T(8,128)S(1)} %copy-done.10, ...), kind=kOutput, calls=%fused_computation.1 | convolution fusion | flops 15073664 | bytes 6362624 | tf_op jit(solution)/shard_map/rs,ryx->syx/dot_general | solution.py:208
  81.5 4.8 %collective-permute-start.5 = (f32[3,8,8,1]{3,1,2,0:T(8,128)S(1)}, f32[3,8,8,1]{3,1,2,0:T(8,128)S(1)}, u32[]{:S(2)}, u32[]{:S(2)}) collective-permute-start(f32[3,8,8,1]{3,1,2,0:T(8,128)S(1)} %get-tuple-element.15), channel_id=1, source_target_pairs={{16,0},{32,16},{48,32},{64,48},{80,64},{96,80},{112,96},{128,112},... | collective-permute-start | bytes 2312 | tf_op jit(solution)/shard_map/ppermute | solution.py:24
  86.3 3.5 %collective-permute-done.4 = f32[3,8,8,1]{3,1,2,0:T(8,128)S(1)} collective-permute-done((f32[3,8,8,1]{3,1,2,0:T(8,128)S(1)}, f32[3,8,8,1]{3,1,2,0:T(8,128)S(1)}, u32[]{:S(2)}, u32[]{:S(2)}) %collective-permute-start.4) | collective-permute-done | bytes 800 | tf_op jit(solution)/shard_map/ppermute | solution.py:23
  89.8 2.1 %concatenate.18 = f32[3,8,8,2050]{3,1,2,0:T(8,128)S(1)} concatenate(f32[3,8,8,1]{3,1,2,0:T(8,128)S(1)} %collective-permute-done.4, f32[3,8,8,2048]{3,1,2,0:T(8,128)} %copy-done.3, f32[3,8,8,1]{3,1,2,0:T(8,128)S(1)} %collective-permute-done.5), dimensions={3} | concatenate | bytes 3148800 | tf_op jit(solution)/shard_map/concatenate | solution.py:25
  95.6 7.1 %all-to-all-start.2 = ((f32[16,4,2048]{2,1,0:T(4,128)}), f32[16,4,2048]{2,1,0:T(4,128)S(1)}, u32[]{:S(2)}, u32[]{:S(2)}) async-start(f32[16,4,2048]{2,1,0:T(4,128)} %all_to_all.49), calls=%async_computation.2 | async-start | bytes 1048576 | tf_op jit(solution)/shard_map/all_to_all | solution.py:201
  102.8 2.5 %pad_maximum_fusion.1 = f32[3,8,10,2050]{3,1,2,0:T(8,128)} fusion(f32[3,8,1,2050]{3,1,2,0:T(8,128)} %collective-permute-done.7, f32[3,8,8,2050]{3,1,2,0:T(8,128)S(1)} %concatenate.18, f32[3,8,1,2050]{3,1,2,0:T(8,128)} %collective-permute-done.6), kind=kLoop, calls=%fused_computation.3 | loop fusion | flops 984000 | bytes 3936000 | tf_op jit(solution)/shard_map/concatenate | solution.py:25
  105.3 9.0 %all-to-all-done.2 = f32[16,4,2048]{2,1,0:T(4,128)S(1)} async-done(((f32[16,4,2048]{2,1,0:T(4,128)}), f32[16,4,2048]{2,1,0:T(4,128)S(1)}, u32[]{:S(2)}, u32[]{:S(2)}) %all-to-all-start.2) | async-done | bytes 524320 | tf_op jit(solution)/shard_map/all_to_all | solution.py:201
  134.2 3.6 %all-to-all-start.3 = ((f32[4,16,2048]{2,0,1:T(4,128)}), f32[4,16,2048]{2,0,1:T(4,128)S(1)}, u32[]{:S(2)}, u32[]{:S(2)}) async-start(f32[4,16,2048]{2,0,1:T(4,128)} %copy.66), calls=%async_computation.3 | async-start | bytes 1048576 | tf_op jit(solution)/shard_map/all_to_all | solution.py:209
  139.2 9.3 %all-to-all-done.3 = f32[4,16,2048]{2,0,1:T(4,128)S(1)} async-done(((f32[4,16,2048]{2,0,1:T(4,128)}), f32[4,16,2048]{2,0,1:T(4,128)S(1)}, u32[]{:S(2)}, u32[]{:S(2)}) %all-to-all-start.3) | async-done | bytes 524320 | tf_op jit(solution)/shard_map/all_to_all | solution.py:209
  148.7 3.9 %fusion.300 = (f32[]{:T(128)}, f32[8,8,2048]{2,0,1:T(8,128)S(1)}) fusion(f32[8,8,2048]{2,0,1:T(8,128)S(1)} %convolution_add_fusion.1, f32[8,8]{1,0:T(8,128)S(1)} %select_reduce_fusion, f32[8]{0:T(128)S(1)} %fusion.151, f32[8,2048]{1,0:T(8,128)S(1)} %copy-done.10, f32[8,8,2048]{2,1,0:T(8,128)S(1)} %reshape.116, f32[8]{0:T(128)S(1)} %copy-done.11, ...), kind=kOutput, calls=%fused_computation.345 | convolution fusion | flops 15204735 | bytes 6362628 | tf_op jit(solution)/shard_map/rs,ryx->syx/dot_general | solution.py:208
  154.4 42.7 %shard_map.91 = f32[8,128]{1,0:T(8,128)} custom-call(f32[1,8,128]{2,1,0:T(8,128)} %pad_bitcast_fusion.x_ref), custom_call_target="tpu_custom_call" | custom-call | tf_op jit(solution)/shard_map/pallas_call | solution.py:141
  (105 shorter events, 63.3 us)
Async XLA Ops:
  0.0 9.1 %copy-start.4 = (f32[8,8,2048]{2,1,0:T(8,128)S(1)}, f32[8,8,2048]{2,1,0:T(8,128)}, u32[]{:S(2)}) copy-start(f32[8,8,2048]{2,1,0:T(8,128)} %param.9) | copy-start | bytes 1572868
  0.0 9.1 %copy-start.6 = (f32[2,8,2048]{2,1,0:T(8,128)S(1)}, f32[2,8,2048]{2,1,0:T(8,128)}, u32[]{:S(2)}) copy-start(f32[2,8,2048]{2,1,0:T(8,128)} %param.10) | copy-start | bytes 393220
  2.1 35.5 %all-to-all-start = ((f32[16,4,2048]{2,1,0:T(4,128)}), f32[16,4,2048]{2,1,0:T(4,128)S(1)}, u32[]{:S(2)}, u32[]{:S(2)}) async-start(f32[16,4,2048]{2,1,0:T(4,128)} %all_to_all.44), calls=%async_computation | async-start | bytes 1048576 | tf_op jit(solution)/shard_map/all_to_all | solution.py:201
  9.5 6.9 %copy-start.5 = (f32[8,8192]{1,0:T(8,128)S(1)}, f32[8,8192]{1,0:T(8,128)}, u32[]{:S(2)}) copy-start(f32[8,8192]{1,0:T(8,128)} %param.14) | copy-start | bytes 786436
  9.5 6.9 %copy-start.8 = (s32[8]{0:T(128)S(1)}, s32[8]{0:T(128)}, u32[]{:S(2)}) copy-start(s32[8]{0:T(128)} %param.15) | copy-start | bytes 100
  10.9 17.6 %collective-permute-start = (f32[3,8,8,1]{3,1,2,0:T(8,128)S(1)}, f32[3,8,8,1]{3,1,2,0:T(8,128)S(1)}, u32[]{:S(2)}, u32[]{:S(2)}) collective-permute-start(f32[3,8,8,1]{3,1,2,0:T(8,128)S(1)} %get-tuple-element.18), channel_id=1, source_target_pairs={{0,16},{16,32},{32,48},{48,64},{64,80},{80,96},{96,112},{112,128},... | collective-permute-start | bytes 2312 | tf_op jit(solution)/shard_map/ppermute | solution.py:23
  12.9 15.6 %collective-permute-start.1 = (f32[3,8,8,1]{3,1,2,0:T(8,128)S(1)}, f32[3,8,8,1]{3,1,2,0:T(8,128)}, u32[]{:S(2)}, u32[]{:S(2)}) collective-permute-start(f32[3,8,8,1]{3,1,2,0:T(8,128)S(1)} %get-tuple-element.17), channel_id=1, source_target_pairs={{16,0},{32,16},{48,32},{64,48},{80,64},{96,80},{112,96},{128,112},... | collective-permute-start | bytes 2312 | tf_op jit(solution)/shard_map/ppermute | solution.py:24
  28.5 4.1 %copy-start.7 = (s32[8,8]{1,0:T(8,128)S(1)}, s32[8,8]{1,0:T(8,128)}, u32[]{:S(2)}) copy-start(s32[8,8]{1,0:T(8,128)} %param.17) | copy-start | bytes 772
  28.5 4.1 %copy-start.9 = (f32[64]{0:T(128)S(1)}, f32[64]{0:T(128)}, u32[]{:S(2)}) copy-start(f32[64]{0:T(128)} %param.16) | copy-start | bytes 772
  30.8 5.2 %collective-permute-start.2 = (f32[3,8,1,2050]{3,1,2,0:T(8,128)S(1)}, f32[3,8,1,2050]{3,1,2,0:T(8,128)S(1)}, u32[]{:S(2)}, u32[]{:S(2)}) collective-permute-start(f32[3,8,1,2050]{3,1,2,0:T(8,128)S(1)} %get-tuple-element.13), channel_id=1, source_target_pairs={{0,1},{1,2},{2,3},{3,4},{4,5},{5,6},{6,7},{7,8},{8,9},{9,10},{10,1... | collective-permute-start | bytes 590408 | tf_op jit(solution)/shard_map/ppermute | solution.py:23
  30.9 5.2 %collective-permute-start.3 = (f32[3,8,1,2050]{3,1,2,0:T(8,128)S(1)}, f32[3,8,1,2050]{3,1,2,0:T(8,128)S(1)}, u32[]{:S(2)}, u32[]{:S(2)}) collective-permute-start(f32[3,8,1,2050]{3,1,2,0:T(8,128)S(1)} %get-tuple-element.14), channel_id=1, source_target_pairs={{1,0},{2,1},{3,2},{4,3},{5,4},{6,5},{7,6},{8,7},{9,8},{10,9},{11,1... | collective-permute-start | bytes 590408 | tf_op jit(solution)/shard_map/ppermute | solution.py:24
  55.1 8.5 %copy-start.1 = (f32[3,8,10,2050]{3,1,2,0:T(8,128)S(1)}, f32[3,8,10,2050]{3,1,2,0:T(8,128)}, u32[]{:S(2)}) copy-start(f32[3,8,10,2050]{3,1,2,0:T(8,128)} %pad_maximum_fusion) | copy-start | bytes 5904004
  59.4 15.9 %all-to-all-start.1 = ((f32[4,16,2048]{2,0,1:T(4,128)}), f32[4,16,2048]{2,0,1:T(4,128)}, u32[]{:S(2)}, u32[]{:S(2)}) async-start(f32[4,16,2048]{2,0,1:T(4,128)} %copy.58), calls=%async_computation.1 | async-start | bytes 1048576 | tf_op jit(solution)/shard_map/all_to_all | solution.py:209
  63.6 12.8 %copy-start.10 = (f32[8,2048]{1,0:T(8,128)S(1)}, f32[8,2048]{1,0:T(8,128)}, u32[]{:S(2)}) copy-start(f32[8,2048]{1,0:T(8,128)} %param.11) | copy-start | bytes 196612
  63.7 12.8 %copy-start.11 = (f32[8]{0:T(128)S(1)}, f32[8]{0:T(128)}, u32[]{:S(2)}) copy-start(f32[8]{0:T(128)} %param.13) | copy-start | bytes 100
  63.7 12.8 %copy-start.12 = (f32[8]{0:T(128)S(1)}, f32[8]{0:T(128)}, u32[]{:S(2)}) copy-start(f32[8]{0:T(128)} %param.12) | copy-start | bytes 100
  80.8 9.0 %copy-start.3 = (f32[3,8,8,2048]{3,1,2,0:T(8,128)}, f32[3,8,8,2048]{3,1,2,0:T(8,128)S(1)}, u32[]{:S(2)}) copy-start(f32[3,8,8,2048]{3,1,2,0:T(8,128)S(1)} %pad_maximum_fusion.3) | copy-start | bytes 4718596
  80.8 8.9 %collective-permute-start.4 = (f32[3,8,8,1]{3,1,2,0:T(8,128)S(1)}, f32[3,8,8,1]{3,1,2,0:T(8,128)S(1)}, u32[]{:S(2)}, u32[]{:S(2)}) collective-permute-start(f32[3,8,8,1]{3,1,2,0:T(8,128)S(1)} %get-tuple-element.16), channel_id=1, source_target_pairs={{0,16},{16,32},{32,48},{48,64},{64,80},{80,96},{96,112},{112,128},... | collective-permute-start | bytes 2312 | tf_op jit(solution)/shard_map/ppermute | solution.py:23
  81.5 8.3 %collective-permute-start.5 = (f32[3,8,8,1]{3,1,2,0:T(8,128)S(1)}, f32[3,8,8,1]{3,1,2,0:T(8,128)S(1)}, u32[]{:S(2)}, u32[]{:S(2)}) collective-permute-start(f32[3,8,8,1]{3,1,2,0:T(8,128)S(1)} %get-tuple-element.15), channel_id=1, source_target_pairs={{16,0},{32,16},{48,32},{64,48},{80,64},{96,80},{112,96},{128,112},... | collective-permute-start | bytes 2312 | tf_op jit(solution)/shard_map/ppermute | solution.py:24
  92.6 10.1 %collective-permute-start.6 = (f32[3,8,1,2050]{3,1,2,0:T(8,128)}, f32[3,8,1,2050]{3,1,2,0:T(8,128)}, u32[]{:S(2)}, u32[]{:S(2)}) collective-permute-start(f32[3,8,1,2050]{3,1,2,0:T(8,128)} %get-tuple-element.11), channel_id=1, source_target_pairs={{0,1},{1,2},{2,3},{3,4},{4,5},{5,6},{6,7},{7,8},{8,9},{9,10},{10,1... | collective-permute-start | bytes 590408 | tf_op jit(solution)/shard_map/ppermute | solution.py:23
  92.7 10.0 %collective-permute-start.7 = (f32[3,8,1,2050]{3,1,2,0:T(8,128)S(1)}, f32[3,8,1,2050]{3,1,2,0:T(8,128)}, u32[]{:S(2)}, u32[]{:S(2)}) collective-permute-start(f32[3,8,1,2050]{3,1,2,0:T(8,128)S(1)} %get-tuple-element.12), channel_id=1, source_target_pairs={{1,0},{2,1},{3,2},{4,3},{5,4},{6,5},{7,6},{8,7},{9,8},{10,9},{11,1... | collective-permute-start | bytes 590408 | tf_op jit(solution)/shard_map/ppermute | solution.py:24
  95.6 18.7 %all-to-all-start.2 = ((f32[16,4,2048]{2,1,0:T(4,128)}), f32[16,4,2048]{2,1,0:T(4,128)S(1)}, u32[]{:S(2)}, u32[]{:S(2)}) async-start(f32[16,4,2048]{2,1,0:T(4,128)} %all_to_all.49), calls=%async_computation.2 | async-start | bytes 1048576 | tf_op jit(solution)/shard_map/all_to_all | solution.py:201
  131.8 6.0 %copy-start = (f32[3,8,10,2050]{3,1,2,0:T(8,128)S(1)}, f32[3,8,10,2050]{3,1,2,0:T(8,128)}, u32[]{:S(2)}) copy-start(f32[3,8,10,2050]{3,1,2,0:T(8,128)} %pad_maximum_fusion.1) | copy-start | bytes 5904004
  134.2 14.2 %all-to-all-start.3 = ((f32[4,16,2048]{2,0,1:T(4,128)}), f32[4,16,2048]{2,0,1:T(4,128)S(1)}, u32[]{:S(2)}, u32[]{:S(2)}) async-start(f32[4,16,2048]{2,0,1:T(4,128)} %copy.66), calls=%async_computation.3 | async-start | bytes 1048576 | tf_op jit(solution)/shard_map/all_to_all | solution.py:209
  (1 other events, 1.2 us)

commit v2 on v0

--- a/solution.py
+++ b/solution.py
@@ -8,7 +8,7 @@
 SWEEPS = 2
 
 
-HIGHEST_PRECISION = lax.Precision.HIGHEST
+HIGHEST_PRECISION = lax.Precision.HIGH
 
 
 def with_halo(array, sides, width):

time: 196 us -> 191 us (0.974)
  matrix products: 49.5 us -> 44.5 us
  transfers between devices with their start and end apart: 20 -> 20, of which waited for: 13 -> 13; matrix products, arithmetic and copies ran while one was open for 11% -> 12% of each run, Pallas kernels for 0% -> 0%
where the time goes in v2:
time: 191 us; the launch traced here: 187 us
  waiting for transfers between devices  60.5 us (32%)
  starting transfers between devices  45 us (24%)
  matrix products  44.5 us (23%)
  local copies, waits for them, and re-layouts  26.2 us (14%)
  other arithmetic  8.27 us (4%)
  between operations  2.85 us (1%)
    ppermute x8, waiting for transfers between devices, tree_sum(): values = values + lax.ppermute(values, axis, pairs)  25.3 us
    all_to_all x2, waiting for transfers between devices, local(): lax.all_to_all(jump_line, 'gx', split_axis=1, concat_axis=0, tiled=True)  19.5 us
    all_to_all x2, starting transfers between devices, local(): lax.all_to_all(field.reshape(regimes * y_rows, x_cols), 'gx', split_axis=...  14.2 us
    ppermute x4, starting transfers between devices, with_halo(): after = lax.ppermute(leading, axis, down)  11.6 us
    all_to_all x2, waiting for transfers between devices, local(): lax.all_to_all(field.reshape(regimes * y_rows, x_cols), 'gx', split_axis=...  9.01 us
    ppermute x8, starting transfers between devices, tree_sum(): values = values + lax.ppermute(values, axis, pairs)  8.68 us
    dot_general x2, matrix products, local(): jnp.einsum('rs,ryx->syx', generator_matrix, field, precision=HIGHEST_PREC...  7.97 us
    all_to_all x2, starting transfers between devices, local(): lax.all_to_all(jump_line, 'gx', split_axis=1, concat_axis=0, tiled=True)  7.81 us
  transfers between devices with their start and end apart: 20, of which 13 were waited for; matrix products, arithmetic and copies ran while one was open for 12% of the time, Pallas kernels for 0%

profile of v2, /device:TPU:32, one launch (start us, length us, event | category | flops | bytes accessed | tf_op | source)
XLA Modules:
  0.0 187.3 jit_solution(6126380104799057140)
XLA Ops:
  2.1 7.0 %all-to-all-start = ((f32[16,4,2048]{2,1,0:T(4,128)}), f32[16,4,2048]{2,1,0:T(4,128)S(1)}, u32[]{:S(2)}, u32[]{:S(2)}) async-start(f32[16,4,2048]{2,1,0:T(4,128)} %all_to_all.44), calls=%async_computation | async-start | bytes 1048576 | tf_op jit(solution)/shard_map/all_to_all | solution.py:150
  13.0 3.4 %collective-permute-start.1 = (f32[3,8,8,1]{3,1,2,0:T(8,128)S(1)}, f32[3,8,8,1]{3,1,2,0:T(8,128)}, u32[]{:S(2)}, u32[]{:S(2)}) collective-permute-start(f32[3,8,8,1]{3,1,2,0:T(8,128)S(1)} %get-tuple-element.17), channel_id=1, source_target_pairs={{16,0},{32,16},{48,32},{64,48},{80,64},{96,80},{112,96},{128,112},... | collective-permute-start | bytes 2312 | tf_op jit(solution)/shard_map/ppermute | solution.py:22
  28.0 2.3 %concatenate.15 = f32[3,8,8,2050]{3,1,2,0:T(8,128)S(1)} concatenate(f32[3,8,8,1]{3,1,2,0:T(8,128)S(1)} %collective-permute-done, f32[3,8,8,2048]{3,1,2,0:T(8,128)} %copy-done.2, f32[3,8,8,1]{3,1,2,0:T(8,128)} %collective-permute-done.1), dimensions={3} | concatenate | bytes 3148800 | tf_op jit(solution)/shard_map/concatenate | solution.py:23
  32.4 3.2 %collective-permute-done.2 = f32[3,8,1,2050]{3,1,2,0:T(8,128)S(1)} collective-permute-done((f32[3,8,1,2050]{3,1,2,0:T(8,128)S(1)}, f32[3,8,1,2050]{3,1,2,0:T(8,128)S(1)}, u32[]{:S(2)}, u32[]{:S(2)}) %collective-permute-start.2) | collective-permute-done | bytes 196832 | tf_op jit(solution)/shard_map/ppermute | solution.py:21
  54.1 2.2 %copy.58 = f32[4,16,2048]{2,0,1:T(4,128)} copy(f32[4,16,2048]{2,1,0:T(8,128)} %div.53) | data formatting | bytes 1048576 | tf_op jit(solution)/shard_map/div | solution.py:80
  56.3 4.2 %all-to-all-start.1 = ((f32[4,16,2048]{2,0,1:T(4,128)}), f32[4,16,2048]{2,0,1:T(4,128)}, u32[]{:S(2)}, u32[]{:S(2)}) async-start(f32[4,16,2048]{2,0,1:T(4,128)} %copy.58), calls=%async_computation.1 | async-start | bytes 1048576 | tf_op jit(solution)/shard_map/all_to_all | solution.py:158
  62.0 10.2 %all-to-all-done.1 = f32[4,16,2048]{2,0,1:T(4,128)} async-done(((f32[4,16,2048]{2,0,1:T(4,128)}), f32[4,16,2048]{2,0,1:T(4,128)}, u32[]{:S(2)}, u32[]{:S(2)}) %all-to-all-start.1) | async-done | bytes 524320 | tf_op jit(solution)/shard_map/all_to_all | solution.py:158
  73.4 3.8 %convolution_add_fusion.1 = f32[8,8,2048]{2,0,1:T(8,128)S(1)} fusion(f32[8,10,2050]{2,0,1:T(8,128)} %get-tuple-element.9, f32[8,10,2050]{2,0,1:T(8,128)} %get-tuple-element.10, f32[8,10,2050]{2,0,1:T(8,128)} %get-tuple-element.8, f32[8,8,2048]{2,1,0:T(8,128)S(1)} %reshape.115, f32[8,8,2048]{2,1,0:T(8,128)S(1)} %copy-done.4, f32[8,2048]{1,0:T(8,128)S(1)} %copy-done.10, ...), kind=kOutput, calls=%fused_computation.1 | convolution fusion | flops 8782208 | bytes 6362624 | tf_op jit(solution)/shard_map/rs,ryx->syx/dot_general | solution.py:157
  79.0 4.8 %collective-permute-start.5 = (f32[3,8,8,1]{3,1,2,0:T(8,128)S(1)}, f32[3,8,8,1]{3,1,2,0:T(8,128)S(1)}, u32[]{:S(2)}, u32[]{:S(2)}) collective-permute-start(f32[3,8,8,1]{3,1,2,0:T(8,128)S(1)} %get-tuple-element.15), channel_id=1, source_target_pairs={{16,0},{32,16},{48,32},{64,48},{80,64},{96,80},{112,96},{128,112},... | collective-permute-start | bytes 2312 | tf_op jit(solution)/shard_map/ppermute | solution.py:22
  83.7 3.5 %collective-permute-done.4 = f32[3,8,8,1]{3,1,2,0:T(8,128)S(1)} collective-permute-done((f32[3,8,8,1]{3,1,2,0:T(8,128)S(1)}, f32[3,8,8,1]{3,1,2,0:T(8,128)S(1)}, u32[]{:S(2)}, u32[]{:S(2)}) %collective-permute-start.4) | collective-permute-done | bytes 800 | tf_op jit(solution)/shard_map/ppermute | solution.py:21
  93.1 7.1 %all-to-all-start.2 = ((f32[16,4,2048]{2,1,0:T(4,128)}), f32[16,4,2048]{2,1,0:T(4,128)S(1)}, u32[]{:S(2)}, u32[]{:S(2)}) async-start(f32[16,4,2048]{2,1,0:T(4,128)} %all_to_all.49), calls=%async_computation.2 | async-start | bytes 1048576 | tf_op jit(solution)/shard_map/all_to_all | solution.py:150
  100.2 2.5 %pad_maximum_fusion.1 = f32[3,8,10,2050]{3,1,2,0:T(8,128)} fusion(f32[3,8,1,2050]{3,1,2,0:T(8,128)} %collective-permute-done.7, f32[3,8,8,2050]{3,1,2,0:T(8,128)S(1)} %concatenate.18, f32[3,8,1,2050]{3,1,2,0:T(8,128)} %collective-permute-done.6), kind=kLoop, calls=%fused_computation.3 | loop fusion | flops 984000 | bytes 3936000 | tf_op jit(solution)/shard_map/concatenate | solution.py:23
  102.7 9.0 %all-to-all-done.2 = f32[16,4,2048]{2,1,0:T(4,128)S(1)} async-done(((f32[16,4,2048]{2,1,0:T(4,128)}), f32[16,4,2048]{2,1,0:T(4,128)S(1)}, u32[]{:S(2)}, u32[]{:S(2)}) %all-to-all-start.2) | async-done | bytes 524320 | tf_op jit(solution)/shard_map/all_to_all | solution.py:150
  129.1 3.6 %all-to-all-start.3 = ((f32[4,16,2048]{2,0,1:T(4,128)}), f32[4,16,2048]{2,0,1:T(4,128)S(1)}, u32[]{:S(2)}, u32[]{:S(2)}) async-start(f32[4,16,2048]{2,0,1:T(4,128)} %copy.66), calls=%async_computation.3 | async-start | bytes 1048576 | tf_op jit(solution)/shard_map/all_to_all | solution.py:158
  134.0 9.3 %all-to-all-done.3 = f32[4,16,2048]{2,0,1:T(4,128)S(1)} async-done(((f32[4,16,2048]{2,0,1:T(4,128)}), f32[4,16,2048]{2,0,1:T(4,128)S(1)}, u32[]{:S(2)}, u32[]{:S(2)}) %all-to-all-start.3) | async-done | bytes 524320 | tf_op jit(solution)/shard_map/all_to_all | solution.py:158
  143.5 4.2 %fusion.300 = (f32[]{:T(128)}, f32[8,8,2048]{2,0,1:T(8,128)S(1)}) fusion(f32[8,8,2048]{2,0,1:T(8,128)S(1)} %convolution_add_fusion.1, f32[8,8]{1,0:T(8,128)S(1)} %select_reduce_fusion, f32[8]{0:T(128)S(1)} %fusion.151, f32[8,2048]{1,0:T(8,128)S(1)} %copy-done.10, f32[8,8,2048]{2,1,0:T(8,128)S(1)} %reshape.117, f32[8]{0:T(128)S(1)} %copy-done.11, ...), kind=kOutput, calls=%fused_computation.345 | convolution fusion | flops 8913279 | bytes 6362628 | tf_op jit(solution)/shard_map/rs,ryx->syx/dot_general | solution.py:157
  149.7 3.0 %collective-permute-done.8 = f32[2,128]{1,0:T(2,128)S(1)} collective-permute-done((f32[2,128]{1,0:T(2,128)S(1)}, f32[2,128]{1,0:T(2,128)S(1)}, u32[]{:S(2)}, u32[]{:S(2)}) %collective-permute-start.8) | collective-permute-done | bytes 1056 | tf_op jit(solution)/shard_map/ppermute | solution.py:101
  153.9 4.0 %collective-permute-done.9 = f32[2,128]{1,0:T(2,128)S(1)} collective-permute-done((f32[2,128]{1,0:T(2,128)S(1)}, f32[2,128]{1,0:T(2,128)S(1)}, u32[]{:S(2)}, u32[]{:S(2)}) %collective-permute-start.9) | collective-permute-done | bytes 1056 | tf_op jit(solution)/shard_map/ppermute | solution.py:101
  157.9 3.6 %collective-permute-done.10 = f32[2,128]{1,0:T(2,128)S(1)} collective-permute-done((f32[2,128]{1,0:T(2,128)S(1)}, f32[2,128]{1,0:T(2,128)S(1)}, u32[]{:S(2)}, u32[]{:S(2)}) %collective-permute-start.10) | collective-permute-done | bytes 1056 | tf_op jit(solution)/shard_map/ppermute | solution.py:101
  162.6 4.0 %collective-permute-done.11 = f32[2,128]{1,0:T(2,128)S(1)} collective-permute-done((f32[2,128]{1,0:T(2,128)S(1)}, f32[2,128]{1,0:T(2,128)S(1)}, u32[]{:S(2)}, u32[]{:S(2)}) %collective-permute-start.11) | collective-permute-done | bytes 1056 | tf_op jit(solution)/shard_map/ppermute | solution.py:101
  168.4 3.0 %collective-permute-done.13 = f32[2,128]{1,0:T(2,128)S(1)} collective-permute-done((f32[2,128]{1,0:T(2,128)S(1)}, f32[2,128]{1,0:T(2,128)S(1)}, u32[]{:S(2)}, u32[]{:S(2)}) %collective-permute-start.13) | collective-permute-done | bytes 1056 | tf_op jit(solution)/shard_map/ppermute | solution.py:101
  171.7 4.1 %collective-permute-done.14 = f32[2,128]{1,0:T(2,128)S(1)} collective-permute-done((f32[2,128]{1,0:T(2,128)S(1)}, f32[2,128]{1,0:T(2,128)S(1)}, u32[]{:S(2)}, u32[]{:S(2)}) %collective-permute-start.14) | collective-permute-done | bytes 1056 | tf_op jit(solution)/shard_map/ppermute | solution.py:101
  175.8 5.0 %collective-permute-start.15 = (f32[2,128]{1,0:T(2,128)S(1)}, f32[2,128]{1,0:T(2,128)S(1)}, u32[]{:S(2)}, u32[]{:S(2)}) collective-permute-start(f32[2,128]{1,0:T(2,128)S(1)} %add.263), channel_id=1, source_target_pairs={{0,8},{1,9},{2,10},{3,11},{4,12},{5,13},{6,14},{7,15},{8,0},{9,1},... | collective-permute-start | bytes 3080 | tf_op jit(solution)/shard_map/ppermute | solution.py:101
  180.8 2.5 %collective-permute-done.15 = f32[2,128]{1,0:T(2,128)S(1)} collective-permute-done((f32[2,128]{1,0:T(2,128)S(1)}, f32[2,128]{1,0:T(2,128)S(1)}, u32[]{:S(2)}, u32[]{:S(2)}) %collective-permute-start.15) | collective-permute-done | bytes 1056 | tf_op jit(solution)/shard_map/ppermute | solution.py:101
  (128 shorter events, 75.0 us)
Async XLA Ops:
  0.0 9.1 %copy-start.4 = (f32[8,8,2048]{2,1,0:T(8,128)S(1)}, f32[8,8,2048]{2,1,0:T(8,128)}, u32[]{:S(2)}) copy-start(f32[8,8,2048]{2,1,0:T(8,128)} %param.9) | copy-start | bytes 1572868
  2.1 35.0 %all-to-all-start = ((f32[16,4,2048]{2,1,0:T(4,128)}), f32[16,4,2048]{2,1,0:T(4,128)S(1)}, u32[]{:S(2)}, u32[]{:S(2)}) async-start(f32[16,4,2048]{2,1,0:T(4,128)} %all_to_all.44), calls=%async_computation | async-start | bytes 1048576 | tf_op jit(solution)/shard_map/all_to_all | solution.py:150
  11.0 17.0 %collective-permute-start = (f32[3,8,8,1]{3,1,2,0:T(8,128)S(1)}, f32[3,8,8,1]{3,1,2,0:T(8,128)S(1)}, u32[]{:S(2)}, u32[]{:S(2)}) collective-permute-start(f32[3,8,8,1]{3,1,2,0:T(8,128)S(1)} %get-tuple-element.18), channel_id=1, source_target_pairs={{0,16},{16,32},{32,48},{48,64},{64,80},{80,96},{96,112},{112,128},... | collective-permute-start | bytes 2312 | tf_op jit(solution)/shard_map/ppermute | solution.py:21
  13.0 15.0 %collective-permute-start.1 = (f32[3,8,8,1]{3,1,2,0:T(8,128)S(1)}, f32[3,8,8,1]{3,1,2,0:T(8,128)}, u32[]{:S(2)}, u32[]{:S(2)}) collective-permute-start(f32[3,8,8,1]{3,1,2,0:T(8,128)S(1)} %get-tuple-element.17), channel_id=1, source_target_pairs={{16,0},{32,16},{48,32},{64,48},{80,64},{96,80},{112,96},{128,112},... | collective-permute-start | bytes 2312 | tf_op jit(solution)/shard_map/ppermute | solution.py:22
  30.3 5.2 %collective-permute-start.2 = (f32[3,8,1,2050]{3,1,2,0:T(8,128)S(1)}, f32[3,8,1,2050]{3,1,2,0:T(8,128)S(1)}, u32[]{:S(2)}, u32[]{:S(2)}) collective-permute-start(f32[3,8,1,2050]{3,1,2,0:T(8,128)S(1)} %get-tuple-element.13), channel_id=1, source_target_pairs={{0,1},{1,2},{2,3},{3,4},{4,5},{5,6},{6,7},{7,8},{8,9},{9,10},{10,1... | collective-permute-start | bytes 590408 | tf_op jit(solution)/shard_map/ppermute | solution.py:21
  30.4 5.2 %collective-permute-start.3 = (f32[3,8,1,2050]{3,1,2,0:T(8,128)S(1)}, f32[3,8,1,2050]{3,1,2,0:T(8,128)S(1)}, u32[]{:S(2)}, u32[]{:S(2)}) collective-permute-start(f32[3,8,1,2050]{3,1,2,0:T(8,128)S(1)} %get-tuple-element.14), channel_id=1, source_target_pairs={{1,0},{2,1},{3,2},{4,3},{5,4},{6,5},{7,6},{8,7},{9,8},{10,9},{11,1... | collective-permute-start | bytes 590408 | tf_op jit(solution)/shard_map/ppermute | solution.py:22
  56.3 15.9 %all-to-all-start.1 = ((f32[4,16,2048]{2,0,1:T(4,128)}), f32[4,16,2048]{2,0,1:T(4,128)}, u32[]{:S(2)}, u32[]{:S(2)}) async-start(f32[4,16,2048]{2,0,1:T(4,128)} %copy.58), calls=%async_computation.1 | async-start | bytes 1048576 | tf_op jit(solution)/shard_map/all_to_all | solution.py:158
  60.6 12.8 %copy-start.10 = (f32[8,2048]{1,0:T(8,128)S(1)}, f32[8,2048]{1,0:T(8,128)}, u32[]{:S(2)}) copy-start(f32[8,2048]{1,0:T(8,128)} %param.11) | copy-start | bytes 196612
  60.6 12.8 %copy-start.11 = (f32[8]{0:T(128)S(1)}, f32[8]{0:T(128)}, u32[]{:S(2)}) copy-start(f32[8]{0:T(128)} %param.13) | copy-start | bytes 100
  60.6 12.8 %copy-start.12 = (f32[8]{0:T(128)S(1)}, f32[8]{0:T(128)}, u32[]{:S(2)}) copy-start(f32[8]{0:T(128)} %param.12) | copy-start | bytes 100
  78.3 8.9 %collective-permute-start.4 = (f32[3,8,8,1]{3,1,2,0:T(8,128)S(1)}, f32[3,8,8,1]{3,1,2,0:T(8,128)S(1)}, u32[]{:S(2)}, u32[]{:S(2)}) collective-permute-start(f32[3,8,8,1]{3,1,2,0:T(8,128)S(1)} %get-tuple-element.16), channel_id=1, source_target_pairs={{0,16},{16,32},{32,48},{48,64},{64,80},{80,96},{96,112},{112,128},... | collective-permute-start | bytes 2312 | tf_op jit(solution)/shard_map/ppermute | solution.py:21
  79.0 8.3 %collective-permute-start.5 = (f32[3,8,8,1]{3,1,2,0:T(8,128)S(1)}, f32[3,8,8,1]{3,1,2,0:T(8,128)S(1)}, u32[]{:S(2)}, u32[]{:S(2)}) collective-permute-start(f32[3,8,8,1]{3,1,2,0:T(8,128)S(1)} %get-tuple-element.15), channel_id=1, source_target_pairs={{16,0},{32,16},{48,32},{64,48},{80,64},{96,80},{112,96},{128,112},... | collective-permute-start | bytes 2312 | tf_op jit(solution)/shard_map/ppermute | solution.py:22
  90.1 10.1 %collective-permute-start.6 = (f32[3,8,1,2050]{3,1,2,0:T(8,128)}, f32[3,8,1,2050]{3,1,2,0:T(8,128)}, u32[]{:S(2)}, u32[]{:S(2)}) collective-permute-start(f32[3,8,1,2050]{3,1,2,0:T(8,128)} %get-tuple-element.11), channel_id=1, source_target_pairs={{0,1},{1,2},{2,3},{3,4},{4,5},{5,6},{6,7},{7,8},{8,9},{9,10},{10,1... | collective-permute-start | bytes 590408 | tf_op jit(solution)/shard_map/ppermute | solution.py:21
  90.2 10.0 %collective-permute-start.7 = (f32[3,8,1,2050]{3,1,2,0:T(8,128)S(1)}, f32[3,8,1,2050]{3,1,2,0:T(8,128)}, u32[]{:S(2)}, u32[]{:S(2)}) collective-permute-start(f32[3,8,1,2050]{3,1,2,0:T(8,128)S(1)} %get-tuple-element.12), channel_id=1, source_target_pairs={{1,0},{2,1},{3,2},{4,3},{5,4},{6,5},{7,6},{8,7},{9,8},{10,9},{11,1... | collective-permute-start | bytes 590408 | tf_op jit(solution)/shard_map/ppermute | solution.py:22
  93.1 18.7 %all-to-all-start.2 = ((f32[16,4,2048]{2,1,0:T(4,128)}), f32[16,4,2048]{2,1,0:T(4,128)S(1)}, u32[]{:S(2)}, u32[]{:S(2)}) async-start(f32[16,4,2048]{2,1,0:T(4,128)} %all_to_all.49), calls=%async_computation.2 | async-start | bytes 1048576 | tf_op jit(solution)/shard_map/all_to_all | solution.py:150
  129.1 14.2 %all-to-all-start.3 = ((f32[4,16,2048]{2,0,1:T(4,128)}), f32[4,16,2048]{2,0,1:T(4,128)S(1)}, u32[]{:S(2)}, u32[]{:S(2)}) async-start(f32[4,16,2048]{2,0,1:T(4,128)} %copy.66), calls=%async_computation.3 | async-start | bytes 1048576 | tf_op jit(solution)/shard_map/all_to_all | solution.py:158
  149.1 3.6 %collective-permute-start.8 = (f32[2,128]{1,0:T(2,128)S(1)}, f32[2,128]{1,0:T(2,128)S(1)}, u32[]{:S(2)}, u32[]{:S(2)}) collective-permute-start(f32[2,128]{1,0:T(2,128)S(1)} %broadcast_in_dim.34), channel_id=1, source_target_pairs={{0,16},{16,0},{32,48},{48,32},{64,80},{80,64},{96,112},{112,96},{1... | collective-permute-start | bytes 3080 | tf_op jit(solution)/shard_map/ppermute | solution.py:101
  152.8 5.1 %collective-permute-start.9 = (f32[2,128]{1,0:T(2,128)S(1)}, f32[2,128]{1,0:T(2,128)S(1)}, u32[]{:S(2)}, u32[]{:S(2)}) collective-permute-start(f32[2,128]{1,0:T(2,128)S(1)} %broadcast_add_fusion), channel_id=1, source_target_pairs={{0,32},{16,48},{32,0},{48,16},{64,96},{80,112},{96,64},{112,80},{1... | collective-permute-start | bytes 3080 | tf_op jit(solution)/shard_map/ppermute | solution.py:101
  157.9 3.6 %collective-permute-start.10 = (f32[2,128]{1,0:T(2,128)S(1)}, f32[2,128]{1,0:T(2,128)S(1)}, u32[]{:S(2)}, u32[]{:S(2)}) collective-permute-start(f32[2,128]{1,0:T(2,128)S(1)} %fusion.308), channel_id=1, source_target_pairs={{0,64},{16,80},{32,96},{48,112},{64,0},{80,16},{96,32},{112,48},{1... | collective-permute-start | bytes 3080 | tf_op jit(solution)/shard_map/ppermute | solution.py:101
  161.5 5.1 %collective-permute-start.11 = (f32[2,128]{1,0:T(2,128)S(1)}, f32[2,128]{1,0:T(2,128)S(1)}, u32[]{:S(2)}, u32[]{:S(2)}) collective-permute-start(f32[2,128]{1,0:T(2,128)S(1)} %add.259), channel_id=1, source_target_pairs={{0,128},{16,144},{32,160},{48,176},{64,192},{80,208},{96,224},{112... | collective-permute-start | bytes 3080 | tf_op jit(solution)/shard_map/ppermute | solution.py:101
  166.6 1.2 collective-permute-start.12
  167.8 3.6 %collective-permute-start.13 = (f32[2,128]{1,0:T(2,128)S(1)}, f32[2,128]{1,0:T(2,128)S(1)}, u32[]{:S(2)}, u32[]{:S(2)}) collective-permute-start(f32[2,128]{1,0:T(2,128)S(1)} %add.261), channel_id=1, source_target_pairs={{0,2},{1,3},{2,0},{3,1},{4,6},{5,7},{6,4},{7,5},{8,10},{9,11},{10,... | collective-permute-start | bytes 3080 | tf_op jit(solution)/shard_map/ppermute | solution.py:101
  171.3 4.5 %collective-permute-start.14 = (f32[2,128]{1,0:T(2,128)S(1)}, f32[2,128]{1,0:T(2,128)S(1)}, u32[]{:S(2)}, u32[]{:S(2)}) collective-permute-start(f32[2,128]{1,0:T(2,128)S(1)} %add.262), channel_id=1, source_target_pairs={{0,4},{1,5},{2,6},{3,7},{4,0},{5,1},{6,2},{7,3},{8,12},{9,13},{10,... | collective-permute-start | bytes 3080 | tf_op jit(solution)/shard_map/ppermute | solution.py:101
  175.8 7.5 %collective-permute-start.15 = (f32[2,128]{1,0:T(2,128)S(1)}, f32[2,128]{1,0:T(2,128)S(1)}, u32[]{:S(2)}, u32[]{:S(2)}) collective-permute-start(f32[2,128]{1,0:T(2,128)S(1)} %add.263), channel_id=1, source_target_pairs={{0,8},{1,9},{2,10},{3,11},{4,12},{5,13},{6,14},{7,15},{8,0},{9,1},... | collective-permute-start | bytes 3080 | tf_op jit(solution)/shard_map/ppermute | solution.py:101
  (9 other events, 55.8 us)

commit v3 on v2

--- a/solution.py
+++ b/solution.py
@@ -50,34 +50,38 @@
     width_b = cos_b.shape[0]
     line_count = line_data.shape[0]
     blocks = line_data.reshape(line_count, width_a, width_b)
-    first_re = jnp.einsum("mab,ak->mkb", blocks, cos_a, precision=HIGHEST_PRECISION)
-    first_im = -jnp.einsum("mab,ak->mkb", blocks, sin_a, precision=HIGHEST_PRECISION)
+    table_a = jnp.concatenate([cos_a, -sin_a], axis=1)
+    first = jnp.einsum("mab,ak->mkb", blocks, table_a, precision=HIGHEST_PRECISION)
+    first_re, first_im = first[:, :width_a], first[:, width_a:]
     turned_re = first_re * cos_t + first_im * sin_t
     turned_im = first_im * cos_t - first_re * sin_t
-    final_re = jnp.einsum(
-        "mkb,bj->mkj", turned_re, cos_b, precision=HIGHEST_PRECISION
-    ) + jnp.einsum("mkb,bj->mkj", turned_im, sin_b, precision=HIGHEST_PRECISION)
-    final_im = jnp.einsum(
-        "mkb,bj->mkj", turned_im, cos_b, precision=HIGHEST_PRECISION
-    ) - jnp.einsum("mkb,bj->mkj", turned_re, sin_b, precision=HIGHEST_PRECISION)
-    return (final_re, final_im)
+    table_b = jnp.concatenate(
+        [jnp.concatenate([cos_b, -sin_b], axis=1), jnp.concatenate([sin_b, cos_b], axis=1)], axis=0
+    )
+    turned = jnp.concatenate([turned_re, turned_im], axis=2)
+    final = jnp.einsum("mkb,bj->mkj", turned, table_b, precision=HIGHEST_PRECISION)
+    return (final[:, :, :width_b], final[:, :, width_b:])
 
 
 def inverse_lines(spec_re, spec_im, tables):
     (cos_a, sin_a), (cos_b, sin_b), (cos_t, sin_t) = tables
     line_count, width_a, width_b = spec_re.shape
-    back_re = jnp.einsum("mkj,jb->mkb", spec_re, cos_b, precision=HIGHEST_PRECISION) - jnp.einsum(
-        "mkj,jb->mkb", spec_im, sin_b, precision=HIGHEST_PRECISION
-    )
-    back_im = jnp.einsum("mkj,jb->mkb", spec_re, sin_b, precision=HIGHEST_PRECISION) + jnp.einsum(
-        "mkj,jb->mkb", spec_im, cos_b, precision=HIGHEST_PRECISION
-    )
+    table_b = jnp.concatenate(
+        [jnp.concatenate([cos_b, sin_b], axis=1), jnp.concatenate([-sin_b, cos_b], axis=1)], axis=0
+    )
+    back = jnp.einsum(
+        "mkj,jb->mkb", jnp.concatenate([spec_re, spec_im], axis=2), table_b,
+        precision=HIGHEST_PRECISION,
+    )
+    back_re, back_im = back[:, :, :width_b], back[:, :, width_b:]
     turned_re = back_re * cos_t - back_im * sin_t
     turned_im = back_re * sin_t + back_im * cos_t
-    result = jnp.einsum("mkb,ka->mab", turned_re, cos_a, precision=HIGHEST_PRECISION) - jnp.einsum(
-        "mkb,ka->mab", turned_im, sin_a, precision=HIGHEST_PRECISION
-    )
-    return result.reshape(line_count, width_a * width_b) / (width_a * width_b)
+    table_a = jnp.concatenate([cos_a, -sin_a], axis=0)
+    result = jnp.einsum(
+        "mkb,ka->mab", jnp.concatenate([turned_re, turned_im], axis=1), table_a,
+        precision=HIGHEST_PRECISION,
+    )
+    return result.reshape(line_count, width_a * width_b)
 
 
 def generator(rate_table, rate_index):
@@ -132,15 +136,15 @@
     if y_rows % per_dev == 0:
         own = lax.dynamic_slice_in_dim(padded, first_line // y_rows, 1, axis=0)
         own_re, own_im = forward_lines(own, tables)
-        line_re = jnp.broadcast_to(own_re, (per_dev,) + own_re.shape[1:])
-        line_im = jnp.broadcast_to(own_im, (per_dev,) + own_im.shape[1:])
+        line_re = jnp.broadcast_to(own_re / length, (per_dev,) + own_re.shape[1:])
+        line_im = jnp.broadcast_to(own_im / length, (per_dev,) + own_im.shape[1:])
     else:
         kern_re, kern_im = forward_lines(padded, tables)
         line_ids = first_line + lax.iota(jnp.int32, per_dev)
         owner_mask = (line_ids // y_rows)[:, None] == lax.iota(jnp.int32, regimes)[None, :]
         select = owner_mask.astype(jnp.float32)
-        line_re = jnp.einsum("lr,rkj->lkj", select, kern_re, precision=HIGHEST_PRECISION)
-        line_im = jnp.einsum("lr,rkj->lkj", select, kern_im, precision=HIGHEST_PRECISION)
+        line_re = jnp.einsum("lr,rkj->lkj", select, kern_re / length, precision=HIGHEST_PRECISION)
+        line_im = jnp.einsum("lr,rkj->lkj", select, kern_im / length, precision=HIGHEST_PRECISION)
     generator_matrix = generator(rate_table, rate_index)
     scale_diff = diffusion[:, None, None]
     scale_jump = jump_rate[:, None, None]

time: 191 us -> 163 us (0.85); the launches traced: 187 us -> 162 us
  matrix products: 44.5 us -> 15.6 us
  other arithmetic: 8.27 us -> 11.3 us
    dot_general x30 -> x10, matrix products: 36.5 us -> 7.54 us  [the longest x3 2.55 us: forward_lines(): jnp.einsum('mkb,bj->mkj', turned, table_b, precision=HIGHEST_PRECISION)]
    div x4 -> x0, local copies, waits for them, and re-layouts: 6.66 us -> none  [inverse_lines(): return result.reshape(line_count, width_a * width_b) / (width_a * width_b)]
    all_to_all x0 -> x4, local copies, waits for them, and re-layouts: none -> 2.43 us  [local(): lax.all_to_all(jump_line, 'gx', split_axis=1, concat_axis=0, tiled=True)]
    unnamed x28 -> x80, local copies, waits for them, and re-layouts: 2.52 us -> 4.83 us
  transfers between devices with their start and end apart: 20 -> 20, of which waited for: 13 -> 13; matrix products, arithmetic and copies ran while one was open for 12% -> 15% of each run, Pallas kernels for 0% -> 0%
where the time goes in v3:
time: 163 us; the launch traced here: 162 us
  waiting for transfers between devices  60.4 us (37%)
  starting transfers between devices  44.7 us (27%)
  local copies, waits for them, and re-layouts  27.6 us (17%)
  matrix products  15.6 us (10%)
  other arithmetic  11.3 us (7%)
  between operations  2.69 us (2%)
    ppermute x8, waiting for transfers between devices, tree_sum(): values = values + lax.ppermute(values, axis, pairs)  24.5 us
    all_to_all x2, waiting for transfers between devices, local(): lax.all_to_all(jump_line, 'gx', split_axis=1, concat_axis=0, tiled=True)  19.1 us
    all_to_all x2, starting transfers between devices, local(): lax.all_to_all(field.reshape(regimes * y_rows, x_cols), 'gx', split_axis=...  13.6 us
    ppermute x4, starting transfers between devices, with_halo(): after = lax.ppermute(leading, axis, down)  11.5 us
    all_to_all x2, waiting for transfers between devices, local(): lax.all_to_all(field.reshape(regimes * y_rows, x_cols), 'gx', split_axis=...  10.4 us
    ppermute x8, starting transfers between devices, tree_sum(): values = values + lax.ppermute(values, axis, pairs)  9.47 us
    dot_general x2, matrix products, local(): jnp.einsum('rs,ryx->syx', generator_matrix, field, precision=HIGHEST_PREC...  8.04 us
    all_to_all x2, starting transfers between devices, local(): lax.all_to_all(jump_line, 'gx', split_axis=1, concat_axis=0, tiled=True)  7.41 us
  transfers between devices with their start and end apart: 20, of which 13 were waited for; matrix products, arithmetic and copies ran while one was open for 15% of the time, Pallas kernels for 0%

profile of v3, /device:TPU:32, one launch (start us, length us, event | category | flops | bytes accessed | tf_op | source)
XLA Modules:
  0.0 162.3 jit_solution(4827833760998354272)
XLA Ops:
  0.0 2.0 %all_to_all.48 = f32[16,4,2048]{2,1,0:T(4,128)} reshape(f32[8,8,2048]{2,1,0:T(8,128)} %param.9) | data formatting | bytes 1048576 | tf_op jit(solution)/shard_map/all_to_all | solution.py:154
  2.1 7.1 %all-to-all-start = ((f32[16,4,2048]{2,1,0:T(4,128)}), f32[16,4,2048]{2,1,0:T(4,128)}, u32[]{:S(2)}, u32[]{:S(2)}) async-start(f32[16,4,2048]{2,1,0:T(4,128)} %all_to_all.48), calls=%async_computation | async-start | bytes 1048576 | tf_op jit(solution)/shard_map/all_to_all | solution.py:154
  12.4 3.5 %collective-permute-start.1 = (f32[3,8,8,1]{3,1,2,0:T(8,128)}, f32[3,8,8,1]{3,1,2,0:T(8,128)}, u32[]{:S(2)}, u32[]{:S(2)}) collective-permute-start(f32[3,8,8,1]{3,1,2,0:T(8,128)} %get-tuple-element.17), channel_id=1, source_target_pairs={{16,0},{32,16},{48,32},{64,48},{80,64},{96,80},{112,96},{128,112},... | collective-permute-start | bytes 2312 | tf_op jit(solution)/shard_map/ppermute | solution.py:22
  20.0 2.1 %dynamic-update-slice.1 = f32[8,32768]{1,0:T(8,128)} dynamic-update-slice(f32[8,32768]{1,0:T(8,128)} %dynamic-update-slice, f32[8,8192]{1,0:T(8,128)S(1)} %fusion.62, s32[]{} %constant.113, s32[]{} %constant.114) | dynamic-update-slice | bytes 524292
  22.1 3.1 %dynamic-update-slice.2 = f32[8,32768]{1,0:T(8,128)} dynamic-update-slice(f32[8,32768]{1,0:T(8,128)} %dynamic-update-slice.1, f32[8,24575]{1,0:T(8,128)S(1)} %broadcast_in_dim.33, s32[]{} %constant.113, s32[]{} %constant.115) | dynamic-update-slice | bytes 1572804 | tf_op jit(solution)/shard_map/concatenate | solution.py:127
  33.4 3.2 %collective-permute-done.2 = f32[3,8,1,2050]{3,1,2,0:T(8,128)S(1)} collective-permute-done((f32[3,8,1,2050]{3,1,2,0:T(8,128)S(1)}, f32[3,8,1,2050]{3,1,2,0:T(8,128)S(1)}, u32[]{:S(2)}, u32[]{:S(2)}) %collective-permute-start.2) | collective-permute-done | bytes 196832 | tf_op jit(solution)/shard_map/ppermute | solution.py:21
  45.0 3.8 %all-to-all-start.1 = ((f32[4,16,2048]{2,0,1:T(4,128)}), f32[4,16,2048]{2,0,1:T(4,128)S(1)}, u32[]{:S(2)}, u32[]{:S(2)}) async-start(f32[4,16,2048]{2,0,1:T(4,128)} %copy.97), calls=%async_computation.1 | async-start | bytes 1048576 | tf_op jit(solution)/shard_map/all_to_all | solution.py:162
  50.3 9.8 %all-to-all-done.1 = f32[4,16,2048]{2,0,1:T(4,128)S(1)} async-done(((f32[4,16,2048]{2,0,1:T(4,128)}), f32[4,16,2048]{2,0,1:T(4,128)S(1)}, u32[]{:S(2)}, u32[]{:S(2)}) %all-to-all-start.1) | async-done | bytes 524320 | tf_op jit(solution)/shard_map/all_to_all | solution.py:162
  60.4 3.9 %convolution_add_fusion.1 = f32[8,8,2048]{2,0,1:T(8,128)S(1)} fusion(f32[8,10,2050]{2,0,1:T(8,128)} %get-tuple-element.9, f32[8,10,2050]{2,0,1:T(8,128)} %get-tuple-element.10, f32[8,10,2050]{2,0,1:T(8,128)} %get-tuple-element.8, f32[8,8,2048]{2,1,0:T(8,128)S(1)} %reshape.125, f32[8,8,2048]{2,1,0:T(8,128)S(1)} %copy-done.11, f32[8,2048]{1,0:T(8,128)S(1)} %copy-done.35, ...), kind=kOutput, calls=%fused_computation.1 | convolution fusion | flops 8782208 | bytes 6362624 | tf_op jit(solution)/shard_map/rs,ryx->syx/dot_general | solution.py:161
  65.8 4.9 %collective-permute-start.5 = (f32[3,8,8,1]{3,1,2,0:T(8,128)S(1)}, f32[3,8,8,1]{3,1,2,0:T(8,128)}, u32[]{:S(2)}, u32[]{:S(2)}) collective-permute-start(f32[3,8,8,1]{3,1,2,0:T(8,128)S(1)} %get-tuple-element.15), channel_id=1, source_target_pairs={{16,0},{32,16},{48,32},{64,48},{80,64},{96,80},{112,96},{128,112},... | collective-permute-start | bytes 2312 | tf_op jit(solution)/shard_map/ppermute | solution.py:22
  70.7 3.2 %collective-permute-done.4 = f32[3,8,8,1]{3,1,2,0:T(8,128)S(1)} collective-permute-done((f32[3,8,8,1]{3,1,2,0:T(8,128)S(1)}, f32[3,8,8,1]{3,1,2,0:T(8,128)S(1)}, u32[]{:S(2)}, u32[]{:S(2)}) %collective-permute-start.4) | collective-permute-done | bytes 800 | tf_op jit(solution)/shard_map/ppermute | solution.py:21
  80.4 6.5 %all-to-all-start.2 = ((f32[16,4,2048]{2,1,0:T(4,128)}), f32[16,4,2048]{2,1,0:T(4,128)S(1)}, u32[]{:S(2)}, u32[]{:S(2)}) async-start(f32[16,4,2048]{2,1,0:T(4,128)} %all_to_all.54), calls=%async_computation.2 | async-start | bytes 1048576 | tf_op jit(solution)/shard_map/all_to_all | solution.py:154
  88.4 10.4 %all-to-all-done.2 = f32[16,4,2048]{2,1,0:T(4,128)S(1)} async-done(((f32[16,4,2048]{2,1,0:T(4,128)}), f32[16,4,2048]{2,1,0:T(4,128)S(1)}, u32[]{:S(2)}, u32[]{:S(2)}) %all-to-all-start.2) | async-done | bytes 524320 | tf_op jit(solution)/shard_map/all_to_all | solution.py:154
  104.7 3.6 %all-to-all-start.3 = ((f32[4,16,2048]{2,0,1:T(4,128)}), f32[4,16,2048]{2,0,1:T(4,128)S(1)}, u32[]{:S(2)}, u32[]{:S(2)}) async-start(f32[4,16,2048]{2,0,1:T(4,128)} %copy.111), calls=%async_computation.3 | async-start | bytes 1048576 | tf_op jit(solution)/shard_map/all_to_all | solution.py:162
  109.7 9.3 %all-to-all-done.3 = f32[4,16,2048]{2,0,1:T(4,128)S(1)} async-done(((f32[4,16,2048]{2,0,1:T(4,128)}), f32[4,16,2048]{2,0,1:T(4,128)S(1)}, u32[]{:S(2)}, u32[]{:S(2)}) %all-to-all-start.3) | async-done | bytes 524320 | tf_op jit(solution)/shard_map/all_to_all | solution.py:162
  119.1 4.2 %fusion.123 = (f32[]{:T(128)}, f32[8,8,2048]{2,0,1:T(8,128)S(1)}) fusion(f32[8,8,2048]{2,0,1:T(8,128)S(1)} %copy-done.3, f32[8,8]{1,0:T(8,128)S(1)} %select_reduce_fusion, f32[8]{0:T(128)S(1)} %fusion.96, f32[8,2048]{1,0:T(8,128)S(1)} %copy-done.36, f32[8,8,2048]{2,1,0:T(8,128)S(1)} %reshape.127, f32[8]{0:T(128)S(1)} %copy-done.37, ...), kind=kOutput, calls=%fused_computation.201 | convolution fusion | flops 8913279 | bytes 6362628 | tf_op jit(solution)/shard_map/rs,ryx->syx/dot_general | solution.py:161
  125.2 3.0 %collective-permute-done.8 = f32[2,128]{1,0:T(2,128)S(1)} collective-permute-done((f32[2,128]{1,0:T(2,128)S(1)}, f32[2,128]{1,0:T(2,128)S(1)}, u32[]{:S(2)}, u32[]{:S(2)}) %collective-permute-start.8) | collective-permute-done | bytes 1056 | tf_op jit(solution)/shard_map/ppermute | solution.py:105
  129.4 4.0 %collective-permute-done.9 = f32[2,128]{1,0:T(2,128)S(1)} collective-permute-done((f32[2,128]{1,0:T(2,128)S(1)}, f32[2,128]{1,0:T(2,128)S(1)}, u32[]{:S(2)}, u32[]{:S(2)}) %collective-permute-start.9) | collective-permute-done | bytes 1056 | tf_op jit(solution)/shard_map/ppermute | solution.py:105
  133.5 3.6 %collective-permute-done.10 = f32[2,128]{1,0:T(2,128)S(1)} collective-permute-done((f32[2,128]{1,0:T(2,128)S(1)}, f32[2,128]{1,0:T(2,128)S(1)}, u32[]{:S(2)}, u32[]{:S(2)}) %collective-permute-start.10) | collective-permute-done | bytes 1056 | tf_op jit(solution)/shard_map/ppermute | solution.py:105
  138.1 4.0 %collective-permute-done.11 = f32[2,128]{1,0:T(2,128)S(1)} collective-permute-done((f32[2,128]{1,0:T(2,128)S(1)}, f32[2,128]{1,0:T(2,128)S(1)}, u32[]{:S(2)}, u32[]{:S(2)}) %collective-permute-start.11) | collective-permute-done | bytes 1056 | tf_op jit(solution)/shard_map/ppermute | solution.py:105
  144.0 2.9 %collective-permute-done.13 = f32[2,128]{1,0:T(2,128)S(1)} collective-permute-done((f32[2,128]{1,0:T(2,128)S(1)}, f32[2,128]{1,0:T(2,128)S(1)}, u32[]{:S(2)}, u32[]{:S(2)}) %collective-permute-start.13) | collective-permute-done | bytes 1056 | tf_op jit(solution)/shard_map/ppermute | solution.py:105
  147.5 3.9 %collective-permute-done.14 = f32[2,128]{1,0:T(2,128)S(1)} collective-permute-done((f32[2,128]{1,0:T(2,128)S(1)}, f32[2,128]{1,0:T(2,128)S(1)}, u32[]{:S(2)}, u32[]{:S(2)}) %collective-permute-start.14) | collective-permute-done | bytes 1056 | tf_op jit(solution)/shard_map/ppermute | solution.py:105
  151.3 5.4 %collective-permute-start.15 = (f32[2,128]{1,0:T(2,128)S(1)}, f32[2,128]{1,0:T(2,128)S(1)}, u32[]{:S(2)}, u32[]{:S(2)}) collective-permute-start(f32[2,128]{1,0:T(2,128)S(1)} %add.204), channel_id=1, source_target_pairs={{0,8},{1,9},{2,10},{3,11},{4,12},{5,13},{6,14},{7,15},{8,0},{9,1},... | collective-permute-start | bytes 3080 | tf_op jit(solution)/shard_map/ppermute | solution.py:105
  156.7 2.1 %collective-permute-done.15 = f32[2,128]{1,0:T(2,128)S(1)} collective-permute-done((f32[2,128]{1,0:T(2,128)S(1)}, f32[2,128]{1,0:T(2,128)S(1)}, u32[]{:S(2)}, u32[]{:S(2)}) %collective-permute-start.15) | collective-permute-done | bytes 1056 | tf_op jit(solution)/shard_map/ppermute | solution.py:105
  (171 shorter events, 50.3 us)
Async XLA Ops:
  2.1 36.0 %all-to-all-start = ((f32[16,4,2048]{2,1,0:T(4,128)}), f32[16,4,2048]{2,1,0:T(4,128)}, u32[]{:S(2)}, u32[]{:S(2)}) async-start(f32[16,4,2048]{2,1,0:T(4,128)} %all_to_all.48), calls=%async_computation | async-start | bytes 1048576 | tf_op jit(solution)/shard_map/all_to_all | solution.py:154
  10.6 18.9 %collective-permute-start = (f32[3,8,8,1]{3,1,2,0:T(8,128)}, f32[3,8,8,1]{3,1,2,0:T(8,128)}, u32[]{:S(2)}, u32[]{:S(2)}) collective-permute-start(f32[3,8,8,1]{3,1,2,0:T(8,128)} %get-tuple-element.18), channel_id=1, source_target_pairs={{0,16},{16,32},{32,48},{48,64},{64,80},{80,96},{96,112},{112,128},... | collective-permute-start | bytes 2312 | tf_op jit(solution)/shard_map/ppermute | solution.py:21
  12.4 17.1 %collective-permute-start.1 = (f32[3,8,8,1]{3,1,2,0:T(8,128)}, f32[3,8,8,1]{3,1,2,0:T(8,128)}, u32[]{:S(2)}, u32[]{:S(2)}) collective-permute-start(f32[3,8,8,1]{3,1,2,0:T(8,128)} %get-tuple-element.17), channel_id=1, source_target_pairs={{16,0},{32,16},{48,32},{64,48},{80,64},{96,80},{112,96},{128,112},... | collective-permute-start | bytes 2312 | tf_op jit(solution)/shard_map/ppermute | solution.py:22
  31.4 5.2 %collective-permute-start.2 = (f32[3,8,1,2050]{3,1,2,0:T(8,128)S(1)}, f32[3,8,1,2050]{3,1,2,0:T(8,128)S(1)}, u32[]{:S(2)}, u32[]{:S(2)}) collective-permute-start(f32[3,8,1,2050]{3,1,2,0:T(8,128)S(1)} %get-tuple-element.13), channel_id=1, source_target_pairs={{0,1},{1,2},{2,3},{3,4},{4,5},{5,6},{6,7},{7,8},{8,9},{9,10},{10,1... | collective-permute-start | bytes 590408 | tf_op jit(solution)/shard_map/ppermute | solution.py:21
  31.4 5.2 %collective-permute-start.3 = (f32[3,8,1,2050]{3,1,2,0:T(8,128)S(1)}, f32[3,8,1,2050]{3,1,2,0:T(8,128)S(1)}, u32[]{:S(2)}, u32[]{:S(2)}) collective-permute-start(f32[3,8,1,2050]{3,1,2,0:T(8,128)S(1)} %get-tuple-element.14), channel_id=1, source_target_pairs={{1,0},{2,1},{3,2},{4,3},{5,4},{6,5},{7,6},{8,7},{9,8},{10,9},{11,1... | collective-permute-start | bytes 590408 | tf_op jit(solution)/shard_map/ppermute | solution.py:22
  45.0 15.1 %all-to-all-start.1 = ((f32[4,16,2048]{2,0,1:T(4,128)}), f32[4,16,2048]{2,0,1:T(4,128)S(1)}, u32[]{:S(2)}, u32[]{:S(2)}) async-start(f32[4,16,2048]{2,0,1:T(4,128)} %copy.97), calls=%async_computation.1 | async-start | bytes 1048576 | tf_op jit(solution)/shard_map/all_to_all | solution.py:162
  48.9 11.5 %copy-start.11 = (f32[8,8,2048]{2,1,0:T(8,128)S(1)}, f32[8,8,2048]{2,1,0:T(8,128)}, u32[]{:S(2)}) copy-start(f32[8,8,2048]{2,1,0:T(8,128)} %param.9) | copy-start | bytes 1572868
  48.9 11.5 %copy-start.35 = (f32[8,2048]{1,0:T(8,128)S(1)}, f32[8,2048]{1,0:T(8,128)}, u32[]{:S(2)}) copy-start(f32[8,2048]{1,0:T(8,128)} %param.11) | copy-start | bytes 196612
  48.9 11.5 %copy-start.37 = (f32[8]{0:T(128)S(1)}, f32[8]{0:T(128)}, u32[]{:S(2)}) copy-start(f32[8]{0:T(128)} %param.13) | copy-start | bytes 100
  48.9 11.5 %copy-start.38 = (f32[8]{0:T(128)S(1)}, f32[8]{0:T(128)}, u32[]{:S(2)}) copy-start(f32[8]{0:T(128)} %param.12) | copy-start | bytes 100
  65.3 8.6 %collective-permute-start.4 = (f32[3,8,8,1]{3,1,2,0:T(8,128)S(1)}, f32[3,8,8,1]{3,1,2,0:T(8,128)S(1)}, u32[]{:S(2)}, u32[]{:S(2)}) collective-permute-start(f32[3,8,8,1]{3,1,2,0:T(8,128)S(1)} %get-tuple-element.16), channel_id=1, source_target_pairs={{0,16},{16,32},{32,48},{48,64},{64,80},{80,96},{96,112},{112,128},... | collective-permute-start | bytes 2312 | tf_op jit(solution)/shard_map/ppermute | solution.py:21
  65.8 8.7 %collective-permute-start.5 = (f32[3,8,8,1]{3,1,2,0:T(8,128)S(1)}, f32[3,8,8,1]{3,1,2,0:T(8,128)}, u32[]{:S(2)}, u32[]{:S(2)}) collective-permute-start(f32[3,8,8,1]{3,1,2,0:T(8,128)S(1)} %get-tuple-element.15), channel_id=1, source_target_pairs={{16,0},{32,16},{48,32},{64,48},{80,64},{96,80},{112,96},{128,112},... | collective-permute-start | bytes 2312 | tf_op jit(solution)/shard_map/ppermute | solution.py:22
  76.4 10.5 %collective-permute-start.6 = (f32[3,8,1,2050]{3,1,2,0:T(8,128)S(1)}, f32[3,8,1,2050]{3,1,2,0:T(8,128)S(1)}, u32[]{:S(2)}, u32[]{:S(2)}) collective-permute-start(f32[3,8,1,2050]{3,1,2,0:T(8,128)S(1)} %get-tuple-element.11), channel_id=1, source_target_pairs={{0,1},{1,2},{2,3},{3,4},{4,5},{5,6},{6,7},{7,8},{8,9},{9,10},{10,1... | collective-permute-start | bytes 590408 | tf_op jit(solution)/shard_map/ppermute | solution.py:21
  76.7 10.2 %collective-permute-start.7 = (f32[3,8,1,2050]{3,1,2,0:T(8,128)S(1)}, f32[3,8,1,2050]{3,1,2,0:T(8,128)S(1)}, u32[]{:S(2)}, u32[]{:S(2)}) collective-permute-start(f32[3,8,1,2050]{3,1,2,0:T(8,128)S(1)} %get-tuple-element.12), channel_id=1, source_target_pairs={{1,0},{2,1},{3,2},{4,3},{5,4},{6,5},{7,6},{8,7},{9,8},{10,9},{11,1... | collective-permute-start | bytes 590408 | tf_op jit(solution)/shard_map/ppermute | solution.py:22
  80.4 18.4 %all-to-all-start.2 = ((f32[16,4,2048]{2,1,0:T(4,128)}), f32[16,4,2048]{2,1,0:T(4,128)S(1)}, u32[]{:S(2)}, u32[]{:S(2)}) async-start(f32[16,4,2048]{2,1,0:T(4,128)} %all_to_all.54), calls=%async_computation.2 | async-start | bytes 1048576 | tf_op jit(solution)/shard_map/all_to_all | solution.py:154
  104.7 14.3 %all-to-all-start.3 = ((f32[4,16,2048]{2,0,1:T(4,128)}), f32[4,16,2048]{2,0,1:T(4,128)S(1)}, u32[]{:S(2)}, u32[]{:S(2)}) async-start(f32[4,16,2048]{2,0,1:T(4,128)} %copy.111), calls=%async_computation.3 | async-start | bytes 1048576 | tf_op jit(solution)/shard_map/all_to_all | solution.py:162
  124.7 3.6 %collective-permute-start.8 = (f32[2,128]{1,0:T(2,128)S(1)}, f32[2,128]{1,0:T(2,128)S(1)}, u32[]{:S(2)}, u32[]{:S(2)}) collective-permute-start(f32[2,128]{1,0:T(2,128)S(1)} %broadcast_in_dim.40), channel_id=1, source_target_pairs={{0,16},{16,0},{32,48},{48,32},{64,80},{80,64},{96,112},{112,96},{1... | collective-permute-start | bytes 3080 | tf_op jit(solution)/shard_map/ppermute | solution.py:105
  128.3 5.1 %collective-permute-start.9 = (f32[2,128]{1,0:T(2,128)S(1)}, f32[2,128]{1,0:T(2,128)S(1)}, u32[]{:S(2)}, u32[]{:S(2)}) collective-permute-start(f32[2,128]{1,0:T(2,128)S(1)} %broadcast_add_fusion), channel_id=1, source_target_pairs={{0,32},{16,48},{32,0},{48,16},{64,96},{80,112},{96,64},{112,80},{1... | collective-permute-start | bytes 3080 | tf_op jit(solution)/shard_map/ppermute | solution.py:105
  133.4 3.6 %collective-permute-start.10 = (f32[2,128]{1,0:T(2,128)S(1)}, f32[2,128]{1,0:T(2,128)S(1)}, u32[]{:S(2)}, u32[]{:S(2)}) collective-permute-start(f32[2,128]{1,0:T(2,128)S(1)} %fusion.128), channel_id=1, source_target_pairs={{0,64},{16,80},{32,96},{48,112},{64,0},{80,16},{96,32},{112,48},{1... | collective-permute-start | bytes 3080 | tf_op jit(solution)/shard_map/ppermute | solution.py:105
  137.0 5.1 %collective-permute-start.11 = (f32[2,128]{1,0:T(2,128)S(1)}, f32[2,128]{1,0:T(2,128)S(1)}, u32[]{:S(2)}, u32[]{:S(2)}) collective-permute-start(f32[2,128]{1,0:T(2,128)S(1)} %add.200), channel_id=1, source_target_pairs={{0,128},{16,144},{32,160},{48,176},{64,192},{80,208},{96,224},{112... | collective-permute-start | bytes 3080 | tf_op jit(solution)/shard_map/ppermute | solution.py:105
  142.1 1.2 collective-permute-start.12
  143.3 3.6 %collective-permute-start.13 = (f32[2,128]{1,0:T(2,128)S(1)}, f32[2,128]{1,0:T(2,128)S(1)}, u32[]{:S(2)}, u32[]{:S(2)}) collective-permute-start(f32[2,128]{1,0:T(2,128)S(1)} %add.202), channel_id=1, source_target_pairs={{0,2},{1,3},{2,0},{3,1},{4,6},{5,7},{6,4},{7,5},{8,10},{9,11},{10,... | collective-permute-start | bytes 3080 | tf_op jit(solution)/shard_map/ppermute | solution.py:105
  146.9 4.5 %collective-permute-start.14 = (f32[2,128]{1,0:T(2,128)S(1)}, f32[2,128]{1,0:T(2,128)S(1)}, u32[]{:S(2)}, u32[]{:S(2)}) collective-permute-start(f32[2,128]{1,0:T(2,128)S(1)} %add.203), channel_id=1, source_target_pairs={{0,4},{1,5},{2,6},{3,7},{4,0},{5,1},{6,2},{7,3},{8,12},{9,13},{10,... | collective-permute-start | bytes 3080 | tf_op jit(solution)/shard_map/ppermute | solution.py:105
  151.3 7.5 %collective-permute-start.15 = (f32[2,128]{1,0:T(2,128)S(1)}, f32[2,128]{1,0:T(2,128)S(1)}, u32[]{:S(2)}, u32[]{:S(2)}) collective-permute-start(f32[2,128]{1,0:T(2,128)S(1)} %add.204), channel_id=1, source_target_pairs={{0,8},{1,9},{2,10},{3,11},{4,12},{5,13},{6,14},{7,15},{8,0},{9,1},... | collective-permute-start | bytes 3080 | tf_op jit(solution)/shard_map/ppermute | solution.py:105
  (35 other events, 173.3 us)

commit v4 on v3

--- a/solution.py
+++ b/solution.py
@@ -124,22 +124,18 @@
     inside = lax.broadcasted_iota(jnp.int32, (regimes, support), 1) < jump_len[:, None]
     weights = jnp.where(inside, kernel_vals, jnp.zeros_like(kernel_vals))
     weights = weights / jnp.sum(weights, axis=1, keepdims=True)
-    padded = jnp.concatenate(
-        [
-            jnp.zeros((regimes, 1), jnp.float32),
-            weights,
-            jnp.zeros((regimes, length - support - 1), jnp.float32),
-        ],
-        axis=1,
-    )
+
+    def pad_lines(rows):
+        return jnp.pad(rows, ((0, 0), (1, length - support - 1)))
+
     first_line = lax.axis_index("gx") * per_dev
     if y_rows % per_dev == 0:
-        own = lax.dynamic_slice_in_dim(padded, first_line // y_rows, 1, axis=0)
+        own = pad_lines(lax.dynamic_slice_in_dim(weights, first_line // y_rows, 1, axis=0))
         own_re, own_im = forward_lines(own, tables)
         line_re = jnp.broadcast_to(own_re / length, (per_dev,) + own_re.shape[1:])
         line_im = jnp.broadcast_to(own_im / length, (per_dev,) + own_im.shape[1:])
     else:
-        kern_re, kern_im = forward_lines(padded, tables)
+        kern_re, kern_im = forward_lines(pad_lines(weights), tables)
         line_ids = first_line + lax.iota(jnp.int32, per_dev)
         owner_mask = (line_ids // y_rows)[:, None] == lax.iota(jnp.int32, regimes)[None, :]
         select = owner_mask.astype(jnp.float32)
@@ -162,21 +158,17 @@
         jumped = lax.all_to_all(jump_line, "gx", split_axis=1, concat_axis=0, tiled=True).reshape(
             regimes, y_rows, x_cols
         )
-        beside_all = with_halo(
-            jnp.stack([field, drift[0][None] * field, drift[1][None] * field]),
-            (("gx", 3), ("gy", 2)),
-            1,
-        )
-        field_pad = beside_all[0]
+        beside_x = with_halo(jnp.stack([field, drift[0][None] * field]), (("gx", 3),), 1)
+        beside_y = with_halo(jnp.stack([field, drift[1][None] * field]), (("gy", 2),), 1)
         laplace = (
-            field_pad[:, 1:-1, 2:]
-            + field_pad[:, 1:-1, :-2]
-            + field_pad[:, 2:, 1:-1]
-            + field_pad[:, :-2, 1:-1]
+            beside_x[0][:, :, 2:]
+            + beside_x[0][:, :, :-2]
+            + beside_y[0][:, 2:, :]
+            + beside_y[0][:, :-2, :]
             - 4.0 * field
         )
-        flow_x = (beside_all[1][:, 1:-1, 2:] - beside_all[1][:, 1:-1, :-2]) * 0.5
-        flow_y = (beside_all[2][:, 2:, 1:-1] - beside_all[2][:, :-2, 1:-1]) * 0.5
+        flow_x = (beside_x[1][:, :, 2:] - beside_x[1][:, :, :-2]) * 0.5
+        flow_y = (beside_y[1][:, 2:, :] - beside_y[1][:, :-2, :]) * 0.5
         updated = (
             field
             + scale_diff * laplace

time: 163 us -> 154 us (0.945)
  waiting for transfers between devices: 60.4 us -> 52.5 us
  local copies, waits for them, and re-layouts: 27.6 us -> 23 us
  other arithmetic: 11.3 us -> 13.4 us
  starting transfers between devices: 44.7 us -> 46.5 us
    all_to_all x2, waiting for transfers between devices: 10.4 us -> 0.01 us  [local(): lax.all_to_all(field.reshape(regimes * y_rows, x_cols), 'gx', split_axis=...]
    all_to_all x2, starting transfers between devices: 7.41 us -> 11 us  [local(): lax.all_to_all(jump_line, 'gx', split_axis=1, concat_axis=0, tiled=True)]
    another operation x3 -> x7, other arithmetic: 0.66 us -> 3.78 us  [the longest x5 2.35 us: local(): jnp.stack([field, drift[0][None] * field])]
    concatenate x1 -> x0, local copies, waits for them, and re-layouts: 3.11 us -> none  [local(): jnp.concatenate([jnp.zeros((regimes, 1), jnp.float32), weights, jnp.zeros...]
    all_to_all x2, waiting for transfers between devices: 19.1 us -> 22 us  [local(): lax.all_to_all(jump_line, 'gx', split_axis=1, concat_axis=0, tiled=True)]
    ppermute x4, waiting for transfers between devices: 6.38 us -> 3.61 us  [with_halo(): before = lax.ppermute(last, axis, up)]
    ppermute x4, starting transfers between devices: 2.74 us -> 0.01 us  [with_halo(): before = lax.ppermute(last, axis, up)]
    ppermute x4, starting transfers between devices: 11.5 us -> 13.8 us  [with_halo(): after = lax.ppermute(leading, axis, down)]
  transfers between devices with their start and end apart: 20 -> 20, of which waited for: 13 -> 12; matrix products, arithmetic and copies ran while one was open for 15% -> 12% of each run, Pallas kernels for 0% -> 0%
where the time goes in v4:
time: 154 us; the launch traced here: 153 us
  waiting for transfers between devices  52.5 us (34%)
  starting transfers between devices  46.5 us (30%)
  local copies, waits for them, and re-layouts  23 us (15%)
  matrix products  15 us (10%)
  other arithmetic  13.4 us (9%)
  between operations  2.75 us (2%)
    ppermute x8, waiting for transfers between devices, tree_sum(): values = values + lax.ppermute(values, axis, pairs)  25.8 us
    all_to_all x2, waiting for transfers between devices, local(): lax.all_to_all(jump_line, 'gx', split_axis=1, concat_axis=0, tiled=True)  22 us
    ppermute x4, starting transfers between devices, with_halo(): after = lax.ppermute(leading, axis, down)  13.8 us
    all_to_all x2, starting transfers between devices, local(): lax.all_to_all(field.reshape(regimes * y_rows, x_cols), 'gx', split_axis=...  11.3 us
    all_to_all x2, starting transfers between devices, local(): lax.all_to_all(jump_line, 'gx', split_axis=1, concat_axis=0, tiled=True)  11 us
    ppermute x8, starting transfers between devices, tree_sum(): values = values + lax.ppermute(values, axis, pairs)  10.3 us
    dot_general x2, matrix products, local(): jnp.einsum('rs,ryx->syx', generator_matrix, field, precision=HIGHEST_PREC...  6.38 us
    all_to_all x4, local copies, waits for them, and re-layouts, local(): lax.all_to_all(field.reshape(regimes * y_rows, x_cols), 'gx', split_axis=...  5.72 us
  transfers between devices with their start and end apart: 20, of which 12 were waited for; matrix products, arithmetic and copies ran while one was open for 12% of the time, Pallas kernels for 0%

profile of v4, /device:TPU:32, one launch (start us, length us, event | category | flops | bytes accessed | tf_op | source)
XLA Modules:
  0.0 153.1 jit_solution(13203362056793423160)
XLA Ops:
  0.0 2.0 %all_to_all.48 = f32[16,4,2048]{2,1,0:T(4,128)} reshape(f32[8,8,2048]{2,1,0:T(8,128)} %param.9) | data formatting | bytes 1048576 | tf_op jit(solution)/shard_map/all_to_all | solution.py:150
  2.1 7.1 %all-to-all-start = ((f32[16,4,2048]{2,1,0:T(4,128)}), f32[16,4,2048]{2,1,0:T(4,128)}, u32[]{:S(2)}, u32[]{:S(2)}) async-start(f32[16,4,2048]{2,1,0:T(4,128)} %all_to_all.48), calls=%async_computation | async-start | bytes 1048576 | tf_op jit(solution)/shard_map/all_to_all | solution.py:150
  10.3 5.2 %collective-permute-start.1 = (f32[2,8,8,1]{3,1,2,0:T(8,128)}, f32[2,8,8,1]{3,1,2,0:T(8,128)}, u32[]{:S(2)}, u32[]{:S(2)}) collective-permute-start(f32[2,8,8,1]{3,1,2,0:T(8,128)} %get-tuple-element.31), channel_id=1, source_target_pairs={{16,0},{32,16},{48,32},{64,48},{80,64},{96,80},{112,96},{128,112},... | collective-permute-start | bytes 1544 | tf_op jit(solution)/shard_map/ppermute | solution.py:22
  16.2 1.7 %collective-permute-start.3 = (f32[2,8,1,2048]{3,1,2,0:T(8,128)}, f32[2,8,1,2048]{3,1,2,0:T(8,128)}, u32[]{:S(2)}, u32[]{:S(2)}) collective-permute-start(f32[2,8,1,2048]{3,1,2,0:T(8,128)} %get-tuple-element.34), channel_id=1, source_target_pairs={{1,0},{2,1},{3,2},{4,3},{5,4},{6,5},{7,6},{8,7},{9,8},{10,9},{11,1... | collective-permute-start | bytes 393224 | tf_op jit(solution)/shard_map/ppermute | solution.py:22
  25.7 1.7 %concatenate.69 = f32[2,8,8,2050]{3,1,2,0:T(8,128)S(1)} concatenate(f32[2,8,8,1]{3,1,2,0:T(8,128)} %collective-permute-done, f32[2,8,8,2048]{3,1,2,0:T(8,128)} %pad_maximum_fusion, f32[2,8,8,1]{3,1,2,0:T(8,128)} %collective-permute-done.1), dimensions={3} | concatenate | bytes 2099200 | tf_op jit(solution)/shard_map/concatenate | solution.py:23
  37.1 6.7 %all-to-all-start.1 = ((f32[4,16,2048]{2,0,1:T(4,128)}), f32[4,16,2048]{2,0,1:T(4,128)S(1)}, u32[]{:S(2)}, u32[]{:S(2)}) async-start(f32[4,16,2048]{2,0,1:T(4,128)} %copy.97), calls=%async_computation.1 | async-start | bytes 1048576 | tf_op jit(solution)/shard_map/all_to_all | solution.py:158
  45.1 10.7 %all-to-all-done.1 = f32[4,16,2048]{2,0,1:T(4,128)S(1)} async-done(((f32[4,16,2048]{2,0,1:T(4,128)}), f32[4,16,2048]{2,0,1:T(4,128)S(1)}, u32[]{:S(2)}, u32[]{:S(2)}) %all-to-all-start.1) | async-done | bytes 524320 | tf_op jit(solution)/shard_map/all_to_all | solution.py:158
  56.1 3.3 %convolution_add_fusion.1 = f32[8,8,2048]{2,0,1:T(8,128)S(1)} fusion(f32[8,10,2048]{2,0,1:T(8,128)} %get-tuple-element.22, f32[8,8,2050]{2,0,1:T(8,128)} %get-tuple-element.26, f32[8,10,2048]{2,0,1:T(8,128)} %get-tuple-element.21, f32[8,8,2050]{2,0,1:T(8,128)S(1)} %copy-done.3, f32[8,8,2048]{2,1,0:T(8,128)S(1)} %reshape.125, f32[8,8,2048]{2,1,0:T(8,128)S(1)} %copy-done, ...), kind=kOutput, calls=%fused_computation.1 | convolution fusion | flops 8782208 | bytes 6362624 | tf_op jit(solution)/shard_map/rs,ryx->syx/dot_general | solution.py:157
  61.5 4.2 %all-to-all-start.2 = ((f32[16,4,2048]{2,1,0:T(4,128)}), f32[16,4,2048]{2,1,0:T(4,128)}, u32[]{:S(2)}, u32[]{:S(2)}) async-start(f32[16,4,2048]{2,1,0:T(4,128)} %all_to_all.54), calls=%async_computation.2 | async-start | bytes 1048576 | tf_op jit(solution)/shard_map/all_to_all | solution.py:150
  65.7 5.2 %collective-permute-start.5 = (f32[2,8,8,1]{3,1,2,0:T(8,128)S(1)}, f32[2,8,8,1]{3,1,2,0:T(8,128)S(1)}, u32[]{:S(2)}, u32[]{:S(2)}) collective-permute-start(f32[2,8,8,1]{3,1,2,0:T(8,128)S(1)} %get-tuple-element.27), channel_id=1, source_target_pairs={{16,0},{32,16},{48,32},{64,48},{80,64},{96,80},{112,96},{128,112},... | collective-permute-start | bytes 1544 | tf_op jit(solution)/shard_map/ppermute | solution.py:22
  71.6 1.7 %collective-permute-start.7 = (f32[2,8,1,2048]{3,1,2,0:T(8,128)}, f32[2,8,1,2048]{3,1,2,0:T(8,128)}, u32[]{:S(2)}, u32[]{:S(2)}) collective-permute-start(f32[2,8,1,2048]{3,1,2,0:T(8,128)} %get-tuple-element.30), channel_id=1, source_target_pairs={{1,0},{2,1},{3,2},{4,3},{5,4},{6,5},{7,6},{8,7},{9,8},{10,9},{11,1... | collective-permute-start | bytes 393224 | tf_op jit(solution)/shard_map/ppermute | solution.py:22
  75.0 3.6 %collective-permute-done.4 = f32[2,8,8,1]{3,1,2,0:T(8,128)} collective-permute-done((f32[2,8,8,1]{3,1,2,0:T(8,128)S(1)}, f32[2,8,8,1]{3,1,2,0:T(8,128)}, u32[]{:S(2)}, u32[]{:S(2)}) %collective-permute-start.4) | collective-permute-done | bytes 544 | tf_op jit(solution)/shard_map/ppermute | solution.py:21
  84.5 1.7 %convolution_bitcast_fusion = f32[4,256,256]{1,2,0:T(8,128)S(1)} fusion(f32[4,128,256]{2,1,0:T(8,128)} %reshape.126, f32[128,128]{1,0:T(8,128)S(1)} %get-tuple-element.51, f32[128,128]{1,0:T(8,128)S(1)} %copy-done.2), kind=kOutput, calls=%fused_computation.18 | convolution fusion | flops 201359360 | bytes 1703936 | tf_op jit(solution)/shard_map/mab,ak->mkb/dot_general | solution.py:54
  91.6 4.2 %all-to-all-start.3 = ((f32[4,16,2048]{2,0,1:T(4,128)}), f32[4,16,2048]{2,0,1:T(4,128)}, u32[]{:S(2)}, u32[]{:S(2)}) async-start(f32[4,16,2048]{2,0,1:T(4,128)} %copy.111), calls=%async_computation.3 | async-start | bytes 1048576 | tf_op jit(solution)/shard_map/all_to_all | solution.py:158
  96.0 11.3 %all-to-all-done.3 = f32[4,16,2048]{2,0,1:T(4,128)} async-done(((f32[4,16,2048]{2,0,1:T(4,128)}), f32[4,16,2048]{2,0,1:T(4,128)}, u32[]{:S(2)}, u32[]{:S(2)}) %all-to-all-start.3) | async-done | bytes 524320 | tf_op jit(solution)/shard_map/all_to_all | solution.py:158
  108.5 3.1 %fusion.125 = (f32[]{:T(128)}, f32[8,8,2048]{2,0,1:T(8,128)S(1)}) fusion(f32[8,8,2048]{2,0,1:T(8,128)S(1)} %convolution_add_fusion.1, f32[8,8]{1,0:T(8,128)S(1)} %select_reduce_fusion, f32[8]{0:T(128)S(1)} %fusion.100, f32[8,2048]{1,0:T(8,128)S(1)} %copy-done.13, f32[8,8,2048]{2,1,0:T(8,128)S(1)} %reshape.127, f32[8]{0:T(128)S(1)} %copy-done.27, ...), kind=kOutput, calls=%fused_computation.219 | convolution fusion | flops 8913279 | bytes 6362628 | tf_op jit(solution)/shard_map/rs,ryx->syx/dot_general | solution.py:157
  113.5 3.0 %collective-permute-done.8 = f32[2,128]{1,0:T(2,128)S(1)} collective-permute-done((f32[2,128]{1,0:T(2,128)S(1)}, f32[2,128]{1,0:T(2,128)S(1)}, u32[]{:S(2)}, u32[]{:S(2)}) %collective-permute-start.8) | collective-permute-done | bytes 1056 | tf_op jit(solution)/shard_map/ppermute | solution.py:105
  117.7 4.0 %collective-permute-done.9 = f32[2,128]{1,0:T(2,128)S(1)} collective-permute-done((f32[2,128]{1,0:T(2,128)S(1)}, f32[2,128]{1,0:T(2,128)S(1)}, u32[]{:S(2)}, u32[]{:S(2)}) %collective-permute-start.9) | collective-permute-done | bytes 1056 | tf_op jit(solution)/shard_map/ppermute | solution.py:105
  121.8 3.6 %collective-permute-done.10 = f32[2,128]{1,0:T(2,128)S(1)} collective-permute-done((f32[2,128]{1,0:T(2,128)S(1)}, f32[2,128]{1,0:T(2,128)S(1)}, u32[]{:S(2)}, u32[]{:S(2)}) %collective-permute-start.10) | collective-permute-done | bytes 1056 | tf_op jit(solution)/shard_map/ppermute | solution.py:105
  126.4 4.0 %collective-permute-done.11 = f32[2,128]{1,0:T(2,128)S(1)} collective-permute-done((f32[2,128]{1,0:T(2,128)S(1)}, f32[2,128]{1,0:T(2,128)S(1)}, u32[]{:S(2)}, u32[]{:S(2)}) %collective-permute-start.11) | collective-permute-done | bytes 1056 | tf_op jit(solution)/shard_map/ppermute | solution.py:105
  131.7 3.5 %collective-permute-done.13 = f32[2,128]{1,0:T(2,128)S(1)} collective-permute-done((f32[2,128]{1,0:T(2,128)S(1)}, f32[2,128]{1,0:T(2,128)S(1)}, u32[]{:S(2)}, u32[]{:S(2)}) %collective-permute-start.13) | collective-permute-done | bytes 1056 | tf_op jit(solution)/shard_map/ppermute | solution.py:105
  135.2 5.1 %collective-permute-start.14 = (f32[2,128]{1,0:T(2,128)S(1)}, f32[2,128]{1,0:T(2,128)S(1)}, u32[]{:S(2)}, u32[]{:S(2)}) collective-permute-start(f32[2,128]{1,0:T(2,128)S(1)} %add.205), channel_id=1, source_target_pairs={{0,4},{1,5},{2,6},{3,7},{4,0},{5,1},{6,2},{7,3},{8,12},{9,13},{10,... | collective-permute-start | bytes 3080 | tf_op jit(solution)/shard_map/ppermute | solution.py:105
  141.8 2.4 %collective-permute-start.15 = (f32[2,128]{1,0:T(2,128)S(1)}, f32[2,128]{1,0:T(2,128)S(1)}, u32[]{:S(2)}, u32[]{:S(2)}) collective-permute-start(f32[2,128]{1,0:T(2,128)S(1)} %add.206), channel_id=1, source_target_pairs={{0,8},{1,9},{2,10},{3,11},{4,12},{5,13},{6,14},{7,15},{8,0},{9,1},... | collective-permute-start | bytes 3080 | tf_op jit(solution)/shard_map/ppermute | solution.py:105
  144.2 5.1 %collective-permute-done.15 = f32[2,128]{1,0:T(2,128)S(1)} collective-permute-done((f32[2,128]{1,0:T(2,128)S(1)}, f32[2,128]{1,0:T(2,128)S(1)}, u32[]{:S(2)}, u32[]{:S(2)}) %collective-permute-start.15) | collective-permute-done | bytes 1056 | tf_op jit(solution)/shard_map/ppermute | solution.py:105
  (152 shorter events, 46.2 us)
Async XLA Ops:
  2.1 27.6 %all-to-all-start = ((f32[16,4,2048]{2,1,0:T(4,128)}), f32[16,4,2048]{2,1,0:T(4,128)}, u32[]{:S(2)}, u32[]{:S(2)}) async-start(f32[16,4,2048]{2,1,0:T(4,128)} %all_to_all.48), calls=%async_computation | async-start | bytes 1048576 | tf_op jit(solution)/shard_map/all_to_all | solution.py:150
  10.3 15.4 %collective-permute-start.1 = (f32[2,8,8,1]{3,1,2,0:T(8,128)}, f32[2,8,8,1]{3,1,2,0:T(8,128)}, u32[]{:S(2)}, u32[]{:S(2)}) collective-permute-start(f32[2,8,8,1]{3,1,2,0:T(8,128)} %get-tuple-element.31), channel_id=1, source_target_pairs={{16,0},{32,16},{48,32},{64,48},{80,64},{96,80},{112,96},{128,112},... | collective-permute-start | bytes 1544 | tf_op jit(solution)/shard_map/ppermute | solution.py:22
  15.5 10.2 %collective-permute-start = (f32[2,8,8,1]{3,1,2,0:T(8,128)}, f32[2,8,8,1]{3,1,2,0:T(8,128)}, u32[]{:S(2)}, u32[]{:S(2)}) collective-permute-start(f32[2,8,8,1]{3,1,2,0:T(8,128)} %get-tuple-element.32), channel_id=1, source_target_pairs={{0,16},{16,32},{32,48},{48,64},{64,80},{80,96},{96,112},{112,128},... | collective-permute-start | bytes 1544 | tf_op jit(solution)/shard_map/ppermute | solution.py:21
  16.2 12.3 %collective-permute-start.2 = (f32[2,8,1,2048]{3,1,2,0:T(8,128)}, f32[2,8,1,2048]{3,1,2,0:T(8,128)}, u32[]{:S(2)}, u32[]{:S(2)}) collective-permute-start(f32[2,8,1,2048]{3,1,2,0:T(8,128)} %get-tuple-element.33), channel_id=1, source_target_pairs={{0,1},{1,2},{2,3},{3,4},{4,5},{5,6},{6,7},{7,8},{8,9},{9,10},{10,1... | collective-permute-start | bytes 393224 | tf_op jit(solution)/shard_map/ppermute | solution.py:21
  16.2 12.3 %collective-permute-start.3 = (f32[2,8,1,2048]{3,1,2,0:T(8,128)}, f32[2,8,1,2048]{3,1,2,0:T(8,128)}, u32[]{:S(2)}, u32[]{:S(2)}) collective-permute-start(f32[2,8,1,2048]{3,1,2,0:T(8,128)} %get-tuple-element.34), channel_id=1, source_target_pairs={{1,0},{2,1},{3,2},{4,3},{5,4},{6,5},{7,6},{8,7},{9,8},{10,9},{11,1... | collective-permute-start | bytes 393224 | tf_op jit(solution)/shard_map/ppermute | solution.py:22
  18.2 16.9 %copy-start.1 = (f32[128,128]{1,0:T(8,128)}, f32[128,128]{1,0:T(8,128)S(1)}, u32[]{:S(2)}) copy-start(f32[128,128]{1,0:T(8,128)S(1)} %get-tuple-element.52) | copy-start | bytes 196612
  37.1 18.7 %all-to-all-start.1 = ((f32[4,16,2048]{2,0,1:T(4,128)}), f32[4,16,2048]{2,0,1:T(4,128)S(1)}, u32[]{:S(2)}, u32[]{:S(2)}) async-start(f32[4,16,2048]{2,0,1:T(4,128)} %copy.97), calls=%async_computation.1 | async-start | bytes 1048576 | tf_op jit(solution)/shard_map/all_to_all | solution.py:158
  43.9 12.1 %copy-start.3 = (f32[8,8,2050]{2,0,1:T(8,128)S(1)}, f32[8,8,2050]{2,0,1:T(8,128)}, u32[]{:S(2)}) copy-start(f32[8,8,2050]{2,0,1:T(8,128)} %get-tuple-element.25) | copy-start | bytes 1574404
  43.9 12.1 %copy-start.12 = (f32[8,2048]{1,0:T(8,128)S(1)}, f32[8,2048]{1,0:T(8,128)}, u32[]{:S(2)}) copy-start(f32[8,2048]{1,0:T(8,128)} %param.11) | copy-start | bytes 196612
  61.5 20.8 %all-to-all-start.2 = ((f32[16,4,2048]{2,1,0:T(4,128)}), f32[16,4,2048]{2,1,0:T(4,128)}, u32[]{:S(2)}, u32[]{:S(2)}) async-start(f32[16,4,2048]{2,1,0:T(4,128)} %all_to_all.54), calls=%async_computation.2 | async-start | bytes 1048576 | tf_op jit(solution)/shard_map/all_to_all | solution.py:150
  65.7 8.6 %collective-permute-start.5 = (f32[2,8,8,1]{3,1,2,0:T(8,128)S(1)}, f32[2,8,8,1]{3,1,2,0:T(8,128)S(1)}, u32[]{:S(2)}, u32[]{:S(2)}) collective-permute-start(f32[2,8,8,1]{3,1,2,0:T(8,128)S(1)} %get-tuple-element.27), channel_id=1, source_target_pairs={{16,0},{32,16},{48,32},{64,48},{80,64},{96,80},{112,96},{128,112},... | collective-permute-start | bytes 1544 | tf_op jit(solution)/shard_map/ppermute | solution.py:22
  70.9 7.7 %collective-permute-start.4 = (f32[2,8,8,1]{3,1,2,0:T(8,128)S(1)}, f32[2,8,8,1]{3,1,2,0:T(8,128)}, u32[]{:S(2)}, u32[]{:S(2)}) collective-permute-start(f32[2,8,8,1]{3,1,2,0:T(8,128)S(1)} %get-tuple-element.28), channel_id=1, source_target_pairs={{0,16},{16,32},{32,48},{48,64},{64,80},{80,96},{96,112},{112,128},... | collective-permute-start | bytes 1544 | tf_op jit(solution)/shard_map/ppermute | solution.py:21
  71.6 9.6 %collective-permute-start.6 = (f32[2,8,1,2048]{3,1,2,0:T(8,128)}, f32[2,8,1,2048]{3,1,2,0:T(8,128)}, u32[]{:S(2)}, u32[]{:S(2)}) collective-permute-start(f32[2,8,1,2048]{3,1,2,0:T(8,128)} %get-tuple-element.29), channel_id=1, source_target_pairs={{0,1},{1,2},{2,3},{3,4},{4,5},{5,6},{6,7},{7,8},{8,9},{9,10},{10,1... | collective-permute-start | bytes 393224 | tf_op jit(solution)/shard_map/ppermute | solution.py:21
  71.6 9.6 %collective-permute-start.7 = (f32[2,8,1,2048]{3,1,2,0:T(8,128)}, f32[2,8,1,2048]{3,1,2,0:T(8,128)}, u32[]{:S(2)}, u32[]{:S(2)}) collective-permute-start(f32[2,8,1,2048]{3,1,2,0:T(8,128)} %get-tuple-element.30), channel_id=1, source_target_pairs={{1,0},{2,1},{3,2},{4,3},{5,4},{6,5},{7,6},{8,7},{9,8},{10,9},{11,1... | collective-permute-start | bytes 393224 | tf_op jit(solution)/shard_map/ppermute | solution.py:22
  91.6 15.7 %all-to-all-start.3 = ((f32[4,16,2048]{2,0,1:T(4,128)}), f32[4,16,2048]{2,0,1:T(4,128)}, u32[]{:S(2)}, u32[]{:S(2)}) async-start(f32[4,16,2048]{2,0,1:T(4,128)} %copy.111), calls=%async_computation.3 | async-start | bytes 1048576 | tf_op jit(solution)/shard_map/all_to_all | solution.py:158
  95.9 12.6 %copy-start.13 = (f32[8,2048]{1,0:T(8,128)S(1)}, f32[8,2048]{1,0:T(8,128)}, u32[]{:S(2)}) copy-start(f32[8,2048]{1,0:T(8,128)} %param.11) | copy-start | bytes 196612
  113.0 3.6 %collective-permute-start.8 = (f32[2,128]{1,0:T(2,128)S(1)}, f32[2,128]{1,0:T(2,128)S(1)}, u32[]{:S(2)}, u32[]{:S(2)}) collective-permute-start(f32[2,128]{1,0:T(2,128)S(1)} %broadcast_in_dim.37), channel_id=1, source_target_pairs={{0,16},{16,0},{32,48},{48,32},{64,80},{80,64},{96,112},{112,96},{1... | collective-permute-start | bytes 3080 | tf_op jit(solution)/shard_map/ppermute | solution.py:105
  116.6 5.1 %collective-permute-start.9 = (f32[2,128]{1,0:T(2,128)S(1)}, f32[2,128]{1,0:T(2,128)S(1)}, u32[]{:S(2)}, u32[]{:S(2)}) collective-permute-start(f32[2,128]{1,0:T(2,128)S(1)} %broadcast_add_fusion), channel_id=1, source_target_pairs={{0,32},{16,48},{32,0},{48,16},{64,96},{80,112},{96,64},{112,80},{1... | collective-permute-start | bytes 3080 | tf_op jit(solution)/shard_map/ppermute | solution.py:105
  121.8 3.6 %collective-permute-start.10 = (f32[2,128]{1,0:T(2,128)S(1)}, f32[2,128]{1,0:T(2,128)S(1)}, u32[]{:S(2)}, u32[]{:S(2)}) collective-permute-start(f32[2,128]{1,0:T(2,128)S(1)} %fusion.130), channel_id=1, source_target_pairs={{0,64},{16,80},{32,96},{48,112},{64,0},{80,16},{96,32},{112,48},{1... | collective-permute-start | bytes 3080 | tf_op jit(solution)/shard_map/ppermute | solution.py:105
  125.4 5.1 %collective-permute-start.11 = (f32[2,128]{1,0:T(2,128)S(1)}, f32[2,128]{1,0:T(2,128)S(1)}, u32[]{:S(2)}, u32[]{:S(2)}) collective-permute-start(f32[2,128]{1,0:T(2,128)S(1)} %add.202), channel_id=1, source_target_pairs={{0,128},{16,144},{32,160},{48,176},{64,192},{80,208},{96,224},{112... | collective-permute-start | bytes 3080 | tf_op jit(solution)/shard_map/ppermute | solution.py:105
  130.4 1.2 collective-permute-start.12
  131.6 3.6 %collective-permute-start.13 = (f32[2,128]{1,0:T(2,128)S(1)}, f32[2,128]{1,0:T(2,128)S(1)}, u32[]{:S(2)}, u32[]{:S(2)}) collective-permute-start(f32[2,128]{1,0:T(2,128)S(1)} %add.204), channel_id=1, source_target_pairs={{0,2},{1,3},{2,0},{3,1},{4,6},{5,7},{6,4},{7,5},{8,10},{9,11},{10,... | collective-permute-start | bytes 3080 | tf_op jit(solution)/shard_map/ppermute | solution.py:105
  135.2 6.6 %collective-permute-start.14 = (f32[2,128]{1,0:T(2,128)S(1)}, f32[2,128]{1,0:T(2,128)S(1)}, u32[]{:S(2)}, u32[]{:S(2)}) collective-permute-start(f32[2,128]{1,0:T(2,128)S(1)} %add.205), channel_id=1, source_target_pairs={{0,4},{1,5},{2,6},{3,7},{4,0},{5,1},{6,2},{7,3},{8,12},{9,13},{10,... | collective-permute-start | bytes 3080 | tf_op jit(solution)/shard_map/ppermute | solution.py:105
  141.8 7.5 %collective-permute-start.15 = (f32[2,128]{1,0:T(2,128)S(1)}, f32[2,128]{1,0:T(2,128)S(1)}, u32[]{:S(2)}, u32[]{:S(2)}) collective-permute-start(f32[2,128]{1,0:T(2,128)S(1)} %add.206), channel_id=1, source_target_pairs={{0,8},{1,9},{2,10},{3,11},{4,12},{5,13},{6,14},{7,15},{8,0},{9,1},... | collective-permute-start | bytes 3080 | tf_op jit(solution)/shard_map/ppermute | solution.py:105
  (27 other events, 99.1 us)

commit v5 on v4

--- a/solution.py
+++ b/solution.py
@@ -99,11 +99,17 @@
 def tree_sum(values):
     for axis in ("gx", "gy"):
         peers = lax.axis_size(axis)
-        step = 1
-        while step < peers:
-            pairs = [(i, i ^ step) for i in range(peers)]
-            values = values + lax.ppermute(values, axis, pairs)
-            step *= 2
+        low = 0
+        while (1 << low) < peers:
+            bits = 2 if (1 << (low + 2)) <= peers else 1
+            parts = [values] + [
+                lax.ppermute(values, axis, [(i, i ^ (d << low)) for i in range(peers)])
+                for d in range(1, 1 << bits)
+            ]
+            while len(parts) > 1:
+                parts = [parts[k] + parts[k + 1] for k in range(0, len(parts), 2)]
+            values = parts[0]
+            low += bits
     return values
 
 
@@ -129,6 +135,7 @@
         return jnp.pad(rows, ((0, 0), (1, length - support - 1)))
 
     first_line = lax.axis_index("gx") * per_dev
+    line_rates = jnp.take(jump_rate, (first_line + lax.iota(jnp.int32, per_dev)) // y_rows)
     if y_rows % per_dev == 0:
         own = pad_lines(lax.dynamic_slice_in_dim(weights, first_line // y_rows, 1, axis=0))
         own_re, own_im = forward_lines(own, tables)
@@ -178,7 +185,17 @@
             - kill[None] * field
             + mixing
         )
-        sums.append(jnp.sum(updated))
+        rest = (
+            field
+            + scale_diff * laplace
+            - flow_x
+            - flow_y
+            - scale_jump * field
+            - kill[None] * field
+            + mixing
+        )
+        jump_mass = length * (spec_re[:, 0, 0] * line_re[:, 0, 0] - spec_im[:, 0, 0] * line_im[:, 0, 0])
+        sums.append(jnp.sum(rest) + jnp.sum(line_rates * jump_mass))
         field = updated
     cell_count = field.size * lax.axis_size("gx") * lax.axis_size("gy")
     totals = tree_sum(jnp.broadcast_to(jnp.stack(sums)[:, None], (len(sums), 128)))[:, 0]

time: 154 us -> 144 us (0.935)
  waiting for transfers between devices: 52.5 us -> 21.1 us
  other arithmetic: 13.4 us -> 23.8 us
  local copies, waits for them, and re-layouts: 23 us -> 29.8 us
  starting transfers between devices: 46.5 us -> 51.7 us
  matrix products: 15 us -> 11 us
  between operations: 2.75 us -> 5.37 us
    ppermute x8 -> x12, waiting for transfers between devices: 25.8 us -> 7.55 us  [tree_sum(): lax.ppermute(values, axis, [(i, i ^ d << low) for i in range(peers)])]
    all_to_all x2, waiting for transfers between devices: 22 us -> 8.59 us  [local(): lax.all_to_all(jump_line, 'gx', split_axis=1, concat_axis=0, tiled=True)]
    ppermute x8 -> x12, starting transfers between devices: 10.3 us -> 17 us  [tree_sum(): lax.ppermute(values, axis, [(i, i ^ d << low) for i in range(peers)])]
    dot_general x2, matrix products: 6.38 us -> 1.16 us  [local(): jnp.einsum('rs,ryx->syx', generator_matrix, field, precision=HIGHEST_PREC...]
    all_to_all x2, waiting for transfers between devices: 0.01 us -> 4.94 us  [local(): lax.all_to_all(field.reshape(regimes * y_rows, x_cols), 'gx', split_axis=...]
    another operation x5 -> x6, other arithmetic: 2.35 us -> 7.06 us  [local(): jnp.stack([field, drift[0][None] * field])]
    ppermute x4, starting transfers between devices: 13.8 us -> 9.86 us  [with_halo(): after = lax.ppermute(leading, axis, down)]
    ppermute x4, waiting for transfers between devices: 3.61 us -> 0.01 us  [with_halo(): before = lax.ppermute(last, axis, up)]
  transfers between devices with their start and end apart: 20 -> 24, of which waited for: 12 -> 8; matrix products, arithmetic and copies ran while one was open for 12% -> 24% of each run, Pallas kernels for 0% -> 0%
where the time goes in v5:
time: 144 us; the launch traced here: 143 us
  starting transfers between devices  51.7 us (36%)
  local copies, waits for them, and re-layouts  29.8 us (21%)
  other arithmetic  23.8 us (17%)
  waiting for transfers between devices  21.1 us (15%)
  matrix products  11 us (8%)
  between operations  5.37 us (4%)
    ppermute x12, starting transfers between devices, tree_sum(): lax.ppermute(values, axis, [(i, i ^ d << low) for i in range(peers)])  17 us
    all_to_all x2, starting transfers between devices, local(): lax.all_to_all(field.reshape(regimes * y_rows, x_cols), 'gx', split_axis=...  13 us
    all_to_all x2, starting transfers between devices, local(): lax.all_to_all(jump_line, 'gx', split_axis=1, concat_axis=0, tiled=True)  10.9 us
    ppermute x4, starting transfers between devices, with_halo(): after = lax.ppermute(leading, axis, down)  9.86 us
    all_to_all x2, waiting for transfers between devices, local(): lax.all_to_all(jump_line, 'gx', split_axis=1, concat_axis=0, tiled=True)  8.59 us
    ppermute x12, waiting for transfers between devices, tree_sum(): lax.ppermute(values, axis, [(i, i ^ d << low) for i in range(peers)])  7.55 us
    another operation x6, other arithmetic, local(): jnp.stack([field, drift[0][None] * field])  7.06 us
    all_to_all x4, local copies, waits for them, and re-layouts, local(): lax.all_to_all(field.reshape(regimes * y_rows, x_cols), 'gx', split_axis=...  6.77 us
  transfers between devices with their start and end apart: 24, of which 8 were waited for; matrix products, arithmetic and copies ran while one was open for 24% of the time, Pallas kernels for 0%

profile of v5, /device:TPU:32, one launch (start us, length us, event | category | flops | bytes accessed | tf_op | source)
XLA Modules:
  0.0 142.7 jit_solution(5563851027079285829)
XLA Ops:
  0.0 2.0 %all_to_all.48 = f32[16,4,2048]{2,1,0:T(4,128)} reshape(f32[8,8,2048]{2,1,0:T(8,128)} %param.9) | data formatting | bytes 1048576 | tf_op jit(solution)/shard_map/all_to_all | solution.py:157
  2.1 7.1 %all-to-all-start = ((f32[16,4,2048]{2,1,0:T(4,128)}), f32[16,4,2048]{2,1,0:T(4,128)}, u32[]{:S(2)}, u32[]{:S(2)}) async-start(f32[16,4,2048]{2,1,0:T(4,128)} %all_to_all.48), calls=%async_computation | async-start | bytes 1048576 | tf_op jit(solution)/shard_map/all_to_all | solution.py:157
  10.3 5.2 %collective-permute-start.1 = (f32[2,8,8,1]{3,1,2,0:T(8,128)}, f32[2,8,8,1]{3,1,2,0:T(8,128)}, u32[]{:S(2)}, u32[]{:S(2)}) collective-permute-start(f32[2,8,8,1]{3,1,2,0:T(8,128)} %get-tuple-element.39), channel_id=1, source_target_pairs={{16,0},{32,16},{48,32},{64,48},{80,64},{96,80},{112,96},{128,112},... | collective-permute-start | bytes 1544 | tf_op jit(solution)/shard_map/ppermute | solution.py:22
  16.2 1.7 %collective-permute-start.3 = (f32[2,8,1,2048]{3,1,2,0:T(8,128)}, f32[2,8,1,2048]{3,1,2,0:T(8,128)}, u32[]{:S(2)}, u32[]{:S(2)}) collective-permute-start(f32[2,8,1,2048]{3,1,2,0:T(8,128)} %get-tuple-element.42), channel_id=1, source_target_pairs={{1,0},{2,1},{3,2},{4,3},{5,4},{6,5},{7,6},{8,7},{9,8},{10,9},{11,1... | collective-permute-start | bytes 393224 | tf_op jit(solution)/shard_map/ppermute | solution.py:22
  30.0 1.7 %concatenate.69 = f32[2,8,8,2050]{3,1,2,0:T(8,128)S(1)} concatenate(f32[2,8,8,1]{3,1,2,0:T(8,128)} %collective-permute-done, f32[2,8,8,2048]{3,1,2,0:T(8,128)} %pad_maximum_fusion, f32[2,8,8,1]{3,1,2,0:T(8,128)} %collective-permute-done.1), dimensions={3} | concatenate | bytes 2099200 | tf_op jit(solution)/shard_map/concatenate | solution.py:23
  37.0 1.7 %convolution_bitcast_fusion.1 = f32[4,256,256]{1,2,0:T(8,128)S(1)} fusion(f32[4,128,256]{2,1,0:T(8,128)} %reshape.204, f32[128,128]{1,0:T(8,128)S(1)} %copy-done.6, f32[128,128]{1,0:T(8,128)S(1)} %copy-done.9), kind=kOutput, calls=%fused_computation.18 | convolution fusion | flops 201359360 | bytes 1703936 | tf_op jit(solution)/shard_map/mab,ak->mkb/dot_general | solution.py:54
  43.7 2.2 %copy.100 = f32[4,16,2048]{2,0,1:T(4,128)} copy(f32[4,16,2048]{2,1,0:T(8,128)} %all_to_all.51) | data formatting | bytes 1048576 | tf_op jit(solution)/shard_map/all_to_all | solution.py:165
  45.9 6.7 %all-to-all-start.1 = ((f32[4,16,2048]{2,0,1:T(4,128)}), f32[4,16,2048]{2,0,1:T(4,128)S(1)}, u32[]{:S(2)}, u32[]{:S(2)}) async-start(f32[4,16,2048]{2,0,1:T(4,128)} %copy.100), calls=%async_computation.1 | async-start | bytes 1048576 | tf_op jit(solution)/shard_map/all_to_all | solution.py:165
  53.8 2.2 %multiply_reduce_fusion.1 = f32[4]{0:T(128)S(1)} fusion(f32[4,128,512]{2,1,0:T(8,128)} %copy-done.17, f32[]{:T(128)} %bitcast.38, f32[]{:T(128)} %bitcast.37), kind=kLoop, calls=%fused_computation.209 | loop fusion | flops 16 | bytes 56 | tf_op jit(solution)/shard_map/mul | solution.py:197
  56.0 8.6 %all-to-all-done.1 = f32[4,16,2048]{2,0,1:T(4,128)S(1)} async-done(((f32[4,16,2048]{2,0,1:T(4,128)}), f32[4,16,2048]{2,0,1:T(4,128)S(1)}, u32[]{:S(2)}, u32[]{:S(2)}) %all-to-all-start.1) | async-done | bytes 524320 | tf_op jit(solution)/shard_map/all_to_all | solution.py:165
  64.8 3.1 %multiply_bitcast_fusion.1 = (f32[1,8,8,2048]{3,1,2,0:T(8,128)S(1)}, f32[8,8,2048]{2,0,1:T(8,128)S(1)}, f32[8,8,2048]{2,0,1:T(8,128)S(1)}) fusion(f32[8,2048]{1,0:T(8,128)} %copy-done.19, f32[8,8,2048]{2,0,1:T(8,128)S(1)} %fusion.55, f32[8,2048]{1,0:T(8,128)} %param.11, f32[8,8,2048]{2,1,0:T(8,128)S(1)} %copy-done.1, f32[8,8,2048]{2,1,0:T(8,128)S(1)} %reshape.207, ...), kind=kLoop, calls=%fused_computation.106 | loop fusion | flops 2621440 | bytes 7471168 | tf_op jit(solution)/shard_map/stack | solution.py:168
  74.0 1.7 %collective-permute-start.7 = (f32[2,8,1,2048]{3,1,2,0:T(8,128)}, f32[2,8,1,2048]{3,1,2,0:T(8,128)}, u32[]{:S(2)}, u32[]{:S(2)}) collective-permute-start(f32[2,8,1,2048]{3,1,2,0:T(8,128)} %get-tuple-element.38), channel_id=1, source_target_pairs={{1,0},{2,1},{3,2},{4,3},{5,4},{6,5},{7,6},{8,7},{9,8},{10,9},{11,1... | collective-permute-start | bytes 393224 | tf_op jit(solution)/shard_map/ppermute | solution.py:22
  75.8 2.0 %all_to_all.54 = f32[16,4,2048]{2,1,0:T(4,128)} reshape(f32[8,8,2048]{2,1,0:T(8,128)} %copy.106) | data formatting | bytes 1048576 | tf_op jit(solution)/shard_map/all_to_all | solution.py:157
  77.7 5.9 %all-to-all-start.2 = ((f32[16,4,2048]{2,1,0:T(4,128)}), f32[16,4,2048]{2,1,0:T(4,128)}, u32[]{:S(2)}, u32[]{:S(2)}) async-start(f32[16,4,2048]{2,1,0:T(4,128)} %all_to_all.54), calls=%async_computation.2 | async-start | bytes 1048576 | tf_op jit(solution)/shard_map/all_to_all | solution.py:157
  83.7 2.3 %concatenate.83 = f32[2,8,8,2050]{3,1,2,0:T(8,128)} concatenate(f32[2,8,8,1]{3,1,2,0:T(8,128)} %collective-permute-done.4, f32[2,8,8,2048]{3,1,2,0:T(8,128)} %pad_maximum_fusion.1, f32[2,8,8,1]{3,1,2,0:T(8,128)} %collective-permute-done.5), dimensions={3} | concatenate | bytes 2099200 | tf_op jit(solution)/shard_map/concatenate | solution.py:23
  90.7 4.9 %all-to-all-done.2 = f32[16,4,2048]{2,1,0:T(4,128)} async-done(((f32[16,4,2048]{2,1,0:T(4,128)}), f32[16,4,2048]{2,1,0:T(4,128)}, u32[]{:S(2)}, u32[]{:S(2)}) %all-to-all-start.2) | async-done | bytes 524320 | tf_op jit(solution)/shard_map/all_to_all | solution.py:157
  106.1 2.1 %collective-permute-start.10 = (f32[2,128]{1,0:T(2,128)S(1)}, f32[2,128]{1,0:T(2,128)S(1)}, u32[]{:S(2)}, u32[]{:S(2)}) collective-permute-start(f32[2,128]{1,0:T(2,128)S(1)} %broadcast_in_dim.51), channel_id=1, source_target_pairs={{0,48},{16,32},{32,16},{48,0},{64,112},{80,96},{96,80},{112,64},{1... | collective-permute-start | bytes 3080 | tf_op jit(solution)/shard_map/ppermute | solution.py:106
  108.5 2.2 %fusion.18 = f32[4,128,512]{1,2,0:T(8,128)S(1)} fusion(f32[4,128,256]{2,1,0:T(8,128)S(1)} %get-tuple-element.18, f32[4,128,256]{2,1,0:T(8,128)S(1)} %get-tuple-element.17, f32[256,256]{1,0:T(8,128)} %copy-done.29, f32[256,256]{1,0:T(8,128)} %copy-done.23, f32[256,256]{1,0:T(8,128)} %copy-done.26), kind=kOutput, calls=%fused_computation.45 | convolution fusion | flops 806354944 | bytes 2883584 | tf_op jit(solution)/shard_map/mkj,jb->mkb/dot_general | solution.py:72
  113.4 2.5 %collective-permute-start.11 = (f32[2,128]{1,0:T(2,128)S(1)}, f32[2,128]{1,0:T(2,128)S(1)}, u32[]{:S(2)}, u32[]{:S(2)}) collective-permute-start(f32[2,128]{1,0:T(2,128)S(1)} %add_add_fusion.3), channel_id=1, source_target_pairs={{0,64},{16,80},{32,96},{48,112},{64,0},{80,16},{96,32},{112,48},{1... | collective-permute-start | bytes 3080 | tf_op jit(solution)/shard_map/ppermute | solution.py:106
  121.9 4.2 %all-to-all-start.3 = ((f32[4,16,2048]{2,0,1:T(4,128)}), f32[4,16,2048]{2,0,1:T(4,128)S(1)}, u32[]{:S(2)}, u32[]{:S(2)}) async-start(f32[4,16,2048]{2,0,1:T(4,128)} %copy.114), calls=%async_computation.3 | async-start | bytes 1048576 | tf_op jit(solution)/shard_map/all_to_all | solution.py:165
  126.2 2.7 %collective-permute-start.19 = (f32[2,128]{1,0:T(2,128)S(1)}, f32[2,128]{1,0:T(2,128)S(1)}, u32[]{:S(2)}, u32[]{:S(2)}) collective-permute-start(f32[2,128]{1,0:T(2,128)S(1)} %add_add_fusion.1), channel_id=1, source_target_pairs={{0,12},{1,13},{2,14},{3,15},{4,8},{5,9},{6,10},{7,11},{8,4},{9,5},... | collective-permute-start | bytes 3080 | tf_op jit(solution)/shard_map/ppermute | solution.py:106
  128.9 4.8 %collective-permute-start.18 = (f32[2,128]{1,0:T(2,128)S(1)}, f32[2,128]{1,0:T(2,128)S(1)}, u32[]{:S(2)}, u32[]{:S(2)}) collective-permute-start(f32[2,128]{1,0:T(2,128)S(1)} %add_add_fusion.1), channel_id=1, source_target_pairs={{0,8},{1,9},{2,10},{3,11},{4,12},{5,13},{6,14},{7,15},{8,0},{9,1},... | collective-permute-start | bytes 3080 | tf_op jit(solution)/shard_map/ppermute | solution.py:106
  133.7 2.7 %collective-permute-done.18 = f32[2,128]{1,0:T(2,128)S(1)} collective-permute-done((f32[2,128]{1,0:T(2,128)S(1)}, f32[2,128]{1,0:T(2,128)S(1)}, u32[]{:S(2)}, u32[]{:S(2)}) %collective-permute-start.18) | collective-permute-done | bytes 1056 | tf_op jit(solution)/shard_map/ppermute | solution.py:106
  136.4 1.8 %collective-permute-done.17 = f32[2,128]{1,0:T(2,128)S(1)} collective-permute-done((f32[2,128]{1,0:T(2,128)S(1)}, f32[2,128]{1,0:T(2,128)S(1)}, u32[]{:S(2)}, u32[]{:S(2)}) %collective-permute-start.17) | collective-permute-done | bytes 1056 | tf_op jit(solution)/shard_map/ppermute | solution.py:106
  (180 shorter events, 55.2 us)
Async XLA Ops:
  2.1 32.6 %all-to-all-start = ((f32[16,4,2048]{2,1,0:T(4,128)}), f32[16,4,2048]{2,1,0:T(4,128)}, u32[]{:S(2)}, u32[]{:S(2)}) async-start(f32[16,4,2048]{2,1,0:T(4,128)} %all_to_all.48), calls=%async_computation | async-start | bytes 1048576 | tf_op jit(solution)/shard_map/all_to_all | solution.py:157
  10.3 19.7 %collective-permute-start.1 = (f32[2,8,8,1]{3,1,2,0:T(8,128)}, f32[2,8,8,1]{3,1,2,0:T(8,128)}, u32[]{:S(2)}, u32[]{:S(2)}) collective-permute-start(f32[2,8,8,1]{3,1,2,0:T(8,128)} %get-tuple-element.39), channel_id=1, source_target_pairs={{16,0},{32,16},{48,32},{64,48},{80,64},{96,80},{112,96},{128,112},... | collective-permute-start | bytes 1544 | tf_op jit(solution)/shard_map/ppermute | solution.py:22
  15.5 14.5 %collective-permute-start = (f32[2,8,8,1]{3,1,2,0:T(8,128)}, f32[2,8,8,1]{3,1,2,0:T(8,128)}, u32[]{:S(2)}, u32[]{:S(2)}) collective-permute-start(f32[2,8,8,1]{3,1,2,0:T(8,128)} %get-tuple-element.40), channel_id=1, source_target_pairs={{0,16},{16,32},{32,48},{48,64},{64,80},{80,96},{96,112},{112,128},... | collective-permute-start | bytes 1544 | tf_op jit(solution)/shard_map/ppermute | solution.py:21
  16.2 16.7 %collective-permute-start.2 = (f32[2,8,1,2048]{3,1,2,0:T(8,128)}, f32[2,8,1,2048]{3,1,2,0:T(8,128)S(1)}, u32[]{:S(2)}, u32[]{:S(2)}) collective-permute-start(f32[2,8,1,2048]{3,1,2,0:T(8,128)} %get-tuple-element.41), channel_id=1, source_target_pairs={{0,1},{1,2},{2,3},{3,4},{4,5},{5,6},{6,7},{7,8},{8,9},{9,10},{10,1... | collective-permute-start | bytes 393224 | tf_op jit(solution)/shard_map/ppermute | solution.py:21
  16.2 17.3 %collective-permute-start.3 = (f32[2,8,1,2048]{3,1,2,0:T(8,128)}, f32[2,8,1,2048]{3,1,2,0:T(8,128)}, u32[]{:S(2)}, u32[]{:S(2)}) collective-permute-start(f32[2,8,1,2048]{3,1,2,0:T(8,128)} %get-tuple-element.42), channel_id=1, source_target_pairs={{1,0},{2,1},{3,2},{4,3},{5,4},{6,5},{7,6},{8,7},{9,8},{10,9},{11,1... | collective-permute-start | bytes 393224 | tf_op jit(solution)/shard_map/ppermute | solution.py:22
  45.9 18.7 %all-to-all-start.1 = ((f32[4,16,2048]{2,0,1:T(4,128)}), f32[4,16,2048]{2,0,1:T(4,128)S(1)}, u32[]{:S(2)}, u32[]{:S(2)}) async-start(f32[4,16,2048]{2,0,1:T(4,128)} %copy.100), calls=%async_computation.1 | async-start | bytes 1048576 | tf_op jit(solution)/shard_map/all_to_all | solution.py:165
  70.2 13.5 %collective-permute-start.5 = (f32[2,8,8,1]{3,1,2,0:T(8,128)}, f32[2,8,8,1]{3,1,2,0:T(8,128)}, u32[]{:S(2)}, u32[]{:S(2)}) collective-permute-start(f32[2,8,8,1]{3,1,2,0:T(8,128)} %get-tuple-element.35), channel_id=1, source_target_pairs={{16,0},{32,16},{48,32},{64,48},{80,64},{96,80},{112,96},{128,112},... | collective-permute-start | bytes 1544 | tf_op jit(solution)/shard_map/ppermute | solution.py:22
  71.3 12.3 %collective-permute-start.4 = (f32[2,8,8,1]{3,1,2,0:T(8,128)S(1)}, f32[2,8,8,1]{3,1,2,0:T(8,128)}, u32[]{:S(2)}, u32[]{:S(2)}) collective-permute-start(f32[2,8,8,1]{3,1,2,0:T(8,128)S(1)} %get-tuple-element.36), channel_id=1, source_target_pairs={{0,16},{16,32},{32,48},{48,64},{64,80},{80,96},{96,112},{112,128},... | collective-permute-start | bytes 1544 | tf_op jit(solution)/shard_map/ppermute | solution.py:21
  74.0 13.3 %collective-permute-start.6 = (f32[2,8,1,2048]{3,1,2,0:T(8,128)}, f32[2,8,1,2048]{3,1,2,0:T(8,128)S(1)}, u32[]{:S(2)}, u32[]{:S(2)}) collective-permute-start(f32[2,8,1,2048]{3,1,2,0:T(8,128)} %get-tuple-element.37), channel_id=1, source_target_pairs={{0,1},{1,2},{2,3},{3,4},{4,5},{5,6},{6,7},{7,8},{8,9},{9,10},{10,1... | collective-permute-start | bytes 393224 | tf_op jit(solution)/shard_map/ppermute | solution.py:21
  74.0 13.3 %collective-permute-start.7 = (f32[2,8,1,2048]{3,1,2,0:T(8,128)}, f32[2,8,1,2048]{3,1,2,0:T(8,128)}, u32[]{:S(2)}, u32[]{:S(2)}) collective-permute-start(f32[2,8,1,2048]{3,1,2,0:T(8,128)} %get-tuple-element.38), channel_id=1, source_target_pairs={{1,0},{2,1},{3,2},{4,3},{5,4},{6,5},{7,6},{8,7},{9,8},{10,9},{11,1... | collective-permute-start | bytes 393224 | tf_op jit(solution)/shard_map/ppermute | solution.py:22
  77.7 17.9 %all-to-all-start.2 = ((f32[16,4,2048]{2,1,0:T(4,128)}), f32[16,4,2048]{2,1,0:T(4,128)}, u32[]{:S(2)}, u32[]{:S(2)}) async-start(f32[16,4,2048]{2,1,0:T(4,128)} %all_to_all.54), calls=%async_computation.2 | async-start | bytes 1048576 | tf_op jit(solution)/shard_map/all_to_all | solution.py:157
  105.0 5.7 %collective-permute-start.9 = (f32[2,128]{1,0:T(2,128)S(1)}, f32[2,128]{1,0:T(2,128)S(1)}, u32[]{:S(2)}, u32[]{:S(2)}) collective-permute-start(f32[2,128]{1,0:T(2,128)S(1)} %broadcast_in_dim.51), channel_id=1, source_target_pairs={{0,32},{16,48},{32,0},{48,16},{64,96},{80,112},{96,64},{112,80},{1... | collective-permute-start | bytes 3080 | tf_op jit(solution)/shard_map/ppermute | solution.py:106
  106.1 4.8 %collective-permute-start.10 = (f32[2,128]{1,0:T(2,128)S(1)}, f32[2,128]{1,0:T(2,128)S(1)}, u32[]{:S(2)}, u32[]{:S(2)}) collective-permute-start(f32[2,128]{1,0:T(2,128)S(1)} %broadcast_in_dim.51), channel_id=1, source_target_pairs={{0,48},{16,32},{32,16},{48,0},{64,112},{80,96},{96,80},{112,64},{1... | collective-permute-start | bytes 3080 | tf_op jit(solution)/shard_map/ppermute | solution.py:106
  108.2 3.6 %collective-permute-start.8 = (f32[2,128]{1,0:T(2,128)S(1)}, f32[2,128]{1,0:T(2,128)S(1)}, u32[]{:S(2)}, u32[]{:S(2)}) collective-permute-start(f32[2,128]{1,0:T(2,128)S(1)} %broadcast_in_dim.51), channel_id=1, source_target_pairs={{0,16},{16,0},{32,48},{48,32},{64,80},{80,64},{96,112},{112,96},{1... | collective-permute-start | bytes 3080 | tf_op jit(solution)/shard_map/ppermute | solution.py:106
  111.8 4.8 %collective-permute-start.13 = (f32[2,128]{1,0:T(2,128)S(1)}, f32[2,128]{1,0:T(2,128)S(1)}, u32[]{:S(2)}, u32[]{:S(2)}) collective-permute-start(f32[2,128]{1,0:T(2,128)S(1)} %add_add_fusion.3), channel_id=1, source_target_pairs={{0,192},{16,208},{32,224},{48,240},{64,128},{80,144},{96,160},{112... | collective-permute-start | bytes 3080 | tf_op jit(solution)/shard_map/ppermute | solution.py:106
  113.0 5.1 %collective-permute-start.12 = (f32[2,128]{1,0:T(2,128)S(1)}, f32[2,128]{1,0:T(2,128)S(1)}, u32[]{:S(2)}, u32[]{:S(2)}) collective-permute-start(f32[2,128]{1,0:T(2,128)S(1)} %add_add_fusion.3), channel_id=1, source_target_pairs={{0,128},{16,144},{32,160},{48,176},{64,192},{80,208},{96,224},{112... | collective-permute-start | bytes 3080 | tf_op jit(solution)/shard_map/ppermute | solution.py:106
  113.4 4.6 %collective-permute-start.11 = (f32[2,128]{1,0:T(2,128)S(1)}, f32[2,128]{1,0:T(2,128)S(1)}, u32[]{:S(2)}, u32[]{:S(2)}) collective-permute-start(f32[2,128]{1,0:T(2,128)S(1)} %add_add_fusion.3), channel_id=1, source_target_pairs={{0,64},{16,80},{32,96},{48,112},{64,0},{80,16},{96,32},{112,48},{1... | collective-permute-start | bytes 3080 | tf_op jit(solution)/shard_map/ppermute | solution.py:106
  118.0 8.1 %collective-permute-start.16 = (f32[2,128]{1,0:T(2,128)S(1)}, f32[2,128]{1,0:T(2,128)S(1)}, u32[]{:S(2)}, u32[]{:S(2)}) collective-permute-start(f32[2,128]{1,0:T(2,128)S(1)} %add_add_fusion.2), channel_id=1, source_target_pairs={{0,3},{1,2},{2,1},{3,0},{4,7},{5,6},{6,5},{7,4},{8,11},{9,10},{10,... | collective-permute-start | bytes 3080 | tf_op jit(solution)/shard_map/ppermute | solution.py:106
  118.2 8.0 %collective-permute-start.15 = (f32[2,128]{1,0:T(2,128)S(1)}, f32[2,128]{1,0:T(2,128)S(1)}, u32[]{:S(2)}, u32[]{:S(2)}) collective-permute-start(f32[2,128]{1,0:T(2,128)S(1)} %add_add_fusion.2), channel_id=1, source_target_pairs={{0,2},{1,3},{2,0},{3,1},{4,6},{5,7},{6,4},{7,5},{8,10},{9,11},{10,... | collective-permute-start | bytes 3080 | tf_op jit(solution)/shard_map/ppermute | solution.py:106
  118.3 7.9 %collective-permute-start.14 = (f32[2,128]{1,0:T(2,128)S(1)}, f32[2,128]{1,0:T(2,128)S(1)}, u32[]{:S(2)}, u32[]{:S(2)}) collective-permute-start(f32[2,128]{1,0:T(2,128)S(1)} %add_add_fusion.2), channel_id=1, source_target_pairs={{0,1},{1,0},{2,3},{3,2},{4,5},{5,4},{6,7},{7,6},{8,9},{9,8},{10,11... | collective-permute-start | bytes 3080 | tf_op jit(solution)/shard_map/ppermute | solution.py:106
  121.9 18.9 %all-to-all-start.3 = ((f32[4,16,2048]{2,0,1:T(4,128)}), f32[4,16,2048]{2,0,1:T(4,128)S(1)}, u32[]{:S(2)}, u32[]{:S(2)}) async-start(f32[4,16,2048]{2,0,1:T(4,128)} %copy.114), calls=%async_computation.3 | async-start | bytes 1048576 | tf_op jit(solution)/shard_map/all_to_all | solution.py:165
  126.2 7.5 %collective-permute-start.19 = (f32[2,128]{1,0:T(2,128)S(1)}, f32[2,128]{1,0:T(2,128)S(1)}, u32[]{:S(2)}, u32[]{:S(2)}) collective-permute-start(f32[2,128]{1,0:T(2,128)S(1)} %add_add_fusion.1), channel_id=1, source_target_pairs={{0,12},{1,13},{2,14},{3,15},{4,8},{5,9},{6,10},{7,11},{8,4},{9,5},... | collective-permute-start | bytes 3080 | tf_op jit(solution)/shard_map/ppermute | solution.py:106
  128.9 7.5 %collective-permute-start.18 = (f32[2,128]{1,0:T(2,128)S(1)}, f32[2,128]{1,0:T(2,128)S(1)}, u32[]{:S(2)}, u32[]{:S(2)}) collective-permute-start(f32[2,128]{1,0:T(2,128)S(1)} %add_add_fusion.1), channel_id=1, source_target_pairs={{0,8},{1,9},{2,10},{3,11},{4,12},{5,13},{6,14},{7,15},{8,0},{9,1},... | collective-permute-start | bytes 3080 | tf_op jit(solution)/shard_map/ppermute | solution.py:106
  133.7 4.5 %collective-permute-start.17 = (f32[2,128]{1,0:T(2,128)S(1)}, f32[2,128]{1,0:T(2,128)S(1)}, u32[]{:S(2)}, u32[]{:S(2)}) collective-permute-start(f32[2,128]{1,0:T(2,128)S(1)} %add_add_fusion.1), channel_id=1, source_target_pairs={{0,4},{1,5},{2,6},{3,7},{4,0},{5,1},{6,2},{7,3},{8,12},{9,13},{10,... | collective-permute-start | bytes 3080 | tf_op jit(solution)/shard_map/ppermute | solution.py:106
  (38 other events, 131.9 us)

commit v6 on v5

--- a/solution.py
+++ b/solution.py
@@ -161,7 +161,7 @@
         prod_re = spec_re * line_re - spec_im * line_im
         prod_im = spec_re * line_im + spec_im * line_re
         jump_line = inverse_lines(prod_re, prod_im, tables)
-        mixing = jnp.einsum("rs,ryx->syx", generator_matrix, field, precision=HIGHEST_PRECISION)
+        mixing = jnp.sum(generator_matrix[:, :, None, None] * field[:, None], axis=0)
         jumped = lax.all_to_all(jump_line, "gx", split_axis=1, concat_axis=0, tiled=True).reshape(
             regimes, y_rows, x_cols
         )

time: 144 us -> 144 us (level)
    unnamed x76 -> x66, local copies, waits for them, and re-layouts: 3.61 us -> 2.46 us
  transfers between devices with their start and end apart: 24 -> 24, of which waited for: 8 -> 8; matrix products, arithmetic and copies ran while one was open for 24% -> 22% of each run, Pallas kernels for 0% -> 0%
where the time goes in v6:
time: 144 us; the launch traced here: 143 us
  starting transfers between devices  51.8 us (36%)
  local copies, waits for them, and re-layouts  29.6 us (21%)
  other arithmetic  24.5 us (17%)
  waiting for transfers between devices  20.8 us (14%)
  matrix products  10.8 us (8%)
  between operations  5.11 us (4%)
    ppermute x12, starting transfers between devices, tree_sum(): lax.ppermute(values, axis, [(i, i ^ d << low) for i in range(peers)])  17 us
    all_to_all x2, starting transfers between devices, local(): lax.all_to_all(field.reshape(regimes * y_rows, x_cols), 'gx', split_axis=...  13 us
    all_to_all x2, starting transfers between devices, local(): lax.all_to_all(jump_line, 'gx', split_axis=1, concat_axis=0, tiled=True)  11.1 us
    ppermute x4, starting transfers between devices, with_halo(): after = lax.ppermute(leading, axis, down)  9.85 us
    all_to_all x2, waiting for transfers between devices, local(): lax.all_to_all(jump_line, 'gx', split_axis=1, concat_axis=0, tiled=True)  8.46 us
    another operation x6, other arithmetic, local(): jnp.stack([field, drift[0][None] * field])  8.16 us
    ppermute x12, waiting for transfers between devices, tree_sum(): lax.ppermute(values, axis, [(i, i ^ d << low) for i in range(peers)])  7.47 us
    all_to_all x4, local copies, waits for them, and re-layouts, local(): lax.all_to_all(field.reshape(regimes * y_rows, x_cols), 'gx', split_axis=...  6.47 us
  transfers between devices with their start and end apart: 24, of which 8 were waited for; matrix products, arithmetic and copies ran while one was open for 22% of the time, Pallas kernels for 0%

profile of v6, /device:TPU:32, one launch (start us, length us, event | category | flops | bytes accessed | tf_op | source)
XLA Modules:
  0.0 142.6 jit_solution(14558215742688267896)
XLA Ops:
  0.0 2.0 %all_to_all.48 = f32[16,4,2048]{2,1,0:T(4,128)} reshape(f32[8,8,2048]{2,1,0:T(8,128)} %param.9) | data formatting | bytes 1048576 | tf_op jit(solution)/shard_map/all_to_all | solution.py:157
  2.1 7.1 %all-to-all-start = ((f32[16,4,2048]{2,1,0:T(4,128)}), f32[16,4,2048]{2,1,0:T(4,128)}, u32[]{:S(2)}, u32[]{:S(2)}) async-start(f32[16,4,2048]{2,1,0:T(4,128)} %all_to_all.48), calls=%async_computation | async-start | bytes 1048576 | tf_op jit(solution)/shard_map/all_to_all | solution.py:157
  10.8 5.2 %collective-permute-start.1 = (f32[2,8,8,1]{3,2,1,0:T(8,128)}, f32[2,8,8,1]{3,2,1,0:T(8,128)}, u32[]{:S(2)}, u32[]{:S(2)}) collective-permute-start(f32[2,8,8,1]{3,2,1,0:T(8,128)} %get-tuple-element.39), channel_id=1, source_target_pairs={{16,0},{32,16},{48,32},{64,48},{80,64},{96,80},{112,96},{128,112},... | collective-permute-start | bytes 1544 | tf_op jit(solution)/shard_map/ppermute | solution.py:22
  33.1 2.1 %copy.54 = f32[4,16,2048]{2,1,0:T(8,128)} copy(f32[4,16,2048]{2,0,1:T(4,128)} %bitcast.11) | data formatting | bytes 1048576 | tf_op jit(solution)/shard_map/all_to_all | solution.py:157
  35.3 1.9 %reshape.234 = f32[4,128,256]{2,1,0:T(8,128)} reshape(f32[4,16,2048]{2,1,0:T(8,128)} %copy.54) | data formatting | bytes 1048576 | tf_op jit(solution)/shard_map/reshape | solution.py:52
  37.2 1.7 %convolution_bitcast_fusion.1 = f32[4,256,256]{1,2,0:T(8,128)S(1)} fusion(f32[4,128,256]{2,1,0:T(8,128)} %reshape.234, f32[128,128]{1,0:T(8,128)S(1)} %get-tuple-element.53, f32[128,128]{1,0:T(8,128)S(1)} %get-tuple-element.54), kind=kOutput, calls=%fused_computation.22 | convolution fusion | flops 201359360 | bytes 1703936 | tf_op jit(solution)/shard_map/mab,ak->mkb/dot_general | solution.py:54
  43.0 1.9 %all_to_all.51 = f32[4,16,2048]{2,1,0:T(8,128)} reshape(f32[4,128,256]{2,1,0:T(8,128)} %convolution_bitcast_fusion.3) | data formatting | bytes 1048576 | tf_op jit(solution)/shard_map/all_to_all | solution.py:165
  44.9 2.2 %copy.61 = f32[4,16,2048]{2,0,1:T(4,128)} copy(f32[4,16,2048]{2,1,0:T(8,128)} %all_to_all.51) | data formatting | bytes 1048576 | tf_op jit(solution)/shard_map/all_to_all | solution.py:165
  47.1 6.8 %all-to-all-start.1 = ((f32[4,16,2048]{2,0,1:T(4,128)}), f32[4,16,2048]{2,0,1:T(4,128)}, u32[]{:S(2)}, u32[]{:S(2)}) async-start(f32[4,16,2048]{2,0,1:T(4,128)} %copy.61), calls=%async_computation.1 | async-start | bytes 1048576 | tf_op jit(solution)/shard_map/all_to_all | solution.py:165
  55.4 2.0 %multiply_reduce_fusion.3 = f32[4]{0:T(128)S(1)} fusion(f32[4,128,512]{2,1,0:T(8,128)} %copy-done.11, f32[]{:T(128)} %bitcast.36, f32[]{:T(128)} %bitcast.35), kind=kLoop, calls=%fused_computation.196 | loop fusion | flops 16 | bytes 56 | tf_op jit(solution)/shard_map/mul | solution.py:197
  57.4 8.5 %all-to-all-done.1 = f32[4,16,2048]{2,0,1:T(4,128)} async-done(((f32[4,16,2048]{2,0,1:T(4,128)}), f32[4,16,2048]{2,0,1:T(4,128)}, u32[]{:S(2)}, u32[]{:S(2)}) %all-to-all-start.1) | async-done | bytes 524320 | tf_op jit(solution)/shard_map/all_to_all | solution.py:165
  67.1 4.4 %multiply_bitcast_fusion.1 = (f32[1,8,8,2048]{3,2,1,0:T(8,128)S(1)}, f32[8,8,2048]{2,1,0:T(8,128)S(1)}, f32[8,8,2048]{2,1,0:T(8,128)}) fusion(f32[8,2048]{1,0:T(8,128)} %copy-done.14, f32[8,8,2048]{2,1,0:T(8,128)S(1)} %multiply_reduce_fusion.1, f32[8,8,2048]{2,1,0:T(8,128)S(1)} %copy-done.1, f32[8,2048]{1,0:T(8,128)} %param.11, ...), kind=kLoop, calls=%fused_computation.98 | loop fusion | flops 2621440 | bytes 7471168 | tf_op jit(solution)/shard_map/stack | solution.py:168
  76.8 1.7 %collective-permute-start.7 = (f32[2,8,1,2048]{3,2,1,0:T(1,128)S(1)}, f32[2,8,1,2048]{3,2,1,0:T(1,128)S(1)}, u32[]{:S(2)}, u32[]{:S(2)}) collective-permute-start(f32[2,8,1,2048]{3,2,1,0:T(1,128)S(1)} %get-tuple-element.38), channel_id=1, source_target_pairs={{1,0},{2,1},{3,2},{4,3},{5,4},{6,5},{7,6},{8,7},{9,8},{10,9},{11,1... | collective-permute-start | bytes 393224 | tf_op jit(solution)/shard_map/ppermute | solution.py:22
  78.5 5.9 %all-to-all-start.2 = ((f32[16,4,2048]{2,1,0:T(4,128)}), f32[16,4,2048]{2,1,0:T(4,128)}, u32[]{:S(2)}, u32[]{:S(2)}) async-start(f32[16,4,2048]{2,1,0:T(4,128)} %all_to_all.54), calls=%async_computation.2 | async-start | bytes 1048576 | tf_op jit(solution)/shard_map/all_to_all | solution.py:157
  84.5 2.3 %concatenate.83 = f32[2,8,8,2050]{3,2,1,0:T(8,128)} concatenate(f32[2,8,8,1]{3,2,1,0:T(8,128)} %collective-permute-done.4, f32[2,8,8,2048]{3,2,1,0:T(8,128)} %pad_maximum_fusion.3, f32[2,8,8,1]{3,2,1,0:T(8,128)} %collective-permute-done.5), dimensions={3} | concatenate | bytes 2099200 | tf_op jit(solution)/shard_map/concatenate | solution.py:23
  89.5 2.1 %add_reduce_fusion.1 = (f32[]{:T(128)}, f32[]{:T(128)}, f32[8,8,2048]{2,1,0:T(8,128)}) fusion(f32[8,8,2048]{2,1,0:T(8,128)S(1)} %multiply_reduce_fusion.1, f32[8,8,2048]{2,1,0:T(8,128)S(1)} %copy-done.4, f32[8,8,2048]{2,1,0:T(8,128)S(1)} %copy-done.1, f32[8,2048]{1,0:T(8,128)S(1)} %copy-done.12, f32[8]{0:T(128)S(1)} %copy-done, ...), kind=kLoop, calls=%fused_computation.89 | loop fusion | flops 3276798 | bytes 7405640 | tf_op jit(solution)/shard_map/reduce_sum | solution.py:198
  91.6 4.8 %all-to-all-done.2 = f32[16,4,2048]{2,1,0:T(4,128)} async-done(((f32[16,4,2048]{2,1,0:T(4,128)}), f32[16,4,2048]{2,1,0:T(4,128)}, u32[]{:S(2)}, u32[]{:S(2)}) %all-to-all-start.2) | async-done | bytes 524320 | tf_op jit(solution)/shard_map/all_to_all | solution.py:157
  106.6 2.1 %collective-permute-start.10 = (f32[2,128]{1,0:T(2,128)S(1)}, f32[2,128]{1,0:T(2,128)S(1)}, u32[]{:S(2)}, u32[]{:S(2)}) collective-permute-start(f32[2,128]{1,0:T(2,128)S(1)} %broadcast_in_dim.51), channel_id=1, source_target_pairs={{0,48},{16,32},{32,16},{48,0},{64,112},{80,96},{96,80},{112,64},{1... | collective-permute-start | bytes 3080 | tf_op jit(solution)/shard_map/ppermute | solution.py:106
  109.0 2.3 %fusion.18 = f32[4,128,512]{1,2,0:T(8,128)S(1)} fusion(f32[4,128,256]{2,1,0:T(8,128)} %get-tuple-element.22, f32[4,128,256]{2,1,0:T(8,128)S(1)} %get-tuple-element.21, f32[256,256]{1,0:T(8,128)} %copy-done.24, f32[256,256]{1,0:T(8,128)S(1)} %copy-done.20, f32[256,256]{1,0:T(8,128)} %copy-done.21), kind=kOutput, calls=%fused_computation.51 | convolution fusion | flops 806354944 | bytes 2883584 | tf_op jit(solution)/shard_map/mkj,jb->mkb/dot_general | solution.py:72
  113.9 2.6 %collective-permute-start.11 = (f32[2,128]{1,0:T(2,128)S(1)}, f32[2,128]{1,0:T(2,128)S(1)}, u32[]{:S(2)}, u32[]{:S(2)}) collective-permute-start(f32[2,128]{1,0:T(2,128)S(1)} %add_add_fusion.3), channel_id=1, source_target_pairs={{0,64},{16,80},{32,96},{48,112},{64,0},{80,16},{96,32},{112,48},{1... | collective-permute-start | bytes 3080 | tf_op jit(solution)/shard_map/ppermute | solution.py:106
  122.5 4.3 %all-to-all-start.3 = ((f32[4,16,2048]{2,0,1:T(4,128)}), f32[4,16,2048]{2,0,1:T(4,128)S(1)}, u32[]{:S(2)}, u32[]{:S(2)}) async-start(f32[4,16,2048]{2,0,1:T(4,128)} %copy.69), calls=%async_computation.3 | async-start | bytes 1048576 | tf_op jit(solution)/shard_map/all_to_all | solution.py:165
  126.8 2.8 %collective-permute-start.19 = (f32[2,128]{1,0:T(2,128)S(1)}, f32[2,128]{1,0:T(2,128)S(1)}, u32[]{:S(2)}, u32[]{:S(2)}) collective-permute-start(f32[2,128]{1,0:T(2,128)S(1)} %add_add_fusion.1), channel_id=1, source_target_pairs={{0,12},{1,13},{2,14},{3,15},{4,8},{5,9},{6,10},{7,11},{8,4},{9,5},... | collective-permute-start | bytes 3080 | tf_op jit(solution)/shard_map/ppermute | solution.py:106
  129.7 4.7 %collective-permute-start.18 = (f32[2,128]{1,0:T(2,128)S(1)}, f32[2,128]{1,0:T(2,128)S(1)}, u32[]{:S(2)}, u32[]{:S(2)}) collective-permute-start(f32[2,128]{1,0:T(2,128)S(1)} %add_add_fusion.1), channel_id=1, source_target_pairs={{0,8},{1,9},{2,10},{3,11},{4,12},{5,13},{6,14},{7,15},{8,0},{9,1},... | collective-permute-start | bytes 3080 | tf_op jit(solution)/shard_map/ppermute | solution.py:106
  134.4 2.8 %collective-permute-done.18 = f32[2,128]{1,0:T(2,128)S(1)} collective-permute-done((f32[2,128]{1,0:T(2,128)S(1)}, f32[2,128]{1,0:T(2,128)S(1)}, u32[]{:S(2)}, u32[]{:S(2)}) %collective-permute-start.18) | collective-permute-done | bytes 1056 | tf_op jit(solution)/shard_map/ppermute | solution.py:106
  (169 shorter events, 53.1 us)
Async XLA Ops:
  2.1 31.0 %all-to-all-start = ((f32[16,4,2048]{2,1,0:T(4,128)}), f32[16,4,2048]{2,1,0:T(4,128)}, u32[]{:S(2)}, u32[]{:S(2)}) async-start(f32[16,4,2048]{2,1,0:T(4,128)} %all_to_all.48), calls=%async_computation | async-start | bytes 1048576 | tf_op jit(solution)/shard_map/all_to_all | solution.py:157
  10.8 18.0 %collective-permute-start.1 = (f32[2,8,8,1]{3,2,1,0:T(8,128)}, f32[2,8,8,1]{3,2,1,0:T(8,128)}, u32[]{:S(2)}, u32[]{:S(2)}) collective-permute-start(f32[2,8,8,1]{3,2,1,0:T(8,128)} %get-tuple-element.39), channel_id=1, source_target_pairs={{16,0},{32,16},{48,32},{64,48},{80,64},{96,80},{112,96},{128,112},... | collective-permute-start | bytes 1544 | tf_op jit(solution)/shard_map/ppermute | solution.py:22
  15.9 12.8 %collective-permute-start = (f32[2,8,8,1]{3,2,1,0:T(8,128)}, f32[2,8,8,1]{3,2,1,0:T(8,128)}, u32[]{:S(2)}, u32[]{:S(2)}) collective-permute-start(f32[2,8,8,1]{3,2,1,0:T(8,128)} %get-tuple-element.40), channel_id=1, source_target_pairs={{0,16},{16,32},{32,48},{48,64},{64,80},{80,96},{96,112},{112,128},... | collective-permute-start | bytes 1544 | tf_op jit(solution)/shard_map/ppermute | solution.py:21
  16.2 15.5 %collective-permute-start.2 = (f32[2,8,1,2048]{3,2,1,0:T(1,128)S(1)}, f32[2,8,1,2048]{3,2,1,0:T(1,128)}, u32[]{:S(2)}, u32[]{:S(2)}) collective-permute-start(f32[2,8,1,2048]{3,2,1,0:T(1,128)S(1)} %get-tuple-element.41), channel_id=1, source_target_pairs={{0,1},{1,2},{2,3},{3,4},{4,5},{5,6},{6,7},{7,8},{8,9},{9,10},{10,1... | collective-permute-start | bytes 393224 | tf_op jit(solution)/shard_map/ppermute | solution.py:21
  16.2 15.4 %collective-permute-start.3 = (f32[2,8,1,2048]{3,2,1,0:T(1,128)S(1)}, f32[2,8,1,2048]{3,2,1,0:T(1,128)}, u32[]{:S(2)}, u32[]{:S(2)}) collective-permute-start(f32[2,8,1,2048]{3,2,1,0:T(1,128)S(1)} %get-tuple-element.42), channel_id=1, source_target_pairs={{1,0},{2,1},{3,2},{4,3},{5,4},{6,5},{7,6},{8,7},{9,8},{10,9},{11,1... | collective-permute-start | bytes 393224 | tf_op jit(solution)/shard_map/ppermute | solution.py:22
  47.1 18.8 %all-to-all-start.1 = ((f32[4,16,2048]{2,0,1:T(4,128)}), f32[4,16,2048]{2,0,1:T(4,128)}, u32[]{:S(2)}, u32[]{:S(2)}) async-start(f32[4,16,2048]{2,0,1:T(4,128)} %copy.61), calls=%async_computation.1 | async-start | bytes 1048576 | tf_op jit(solution)/shard_map/all_to_all | solution.py:165
  73.2 11.2 %collective-permute-start.5 = (f32[2,8,8,1]{3,2,1,0:T(8,128)}, f32[2,8,8,1]{3,2,1,0:T(8,128)}, u32[]{:S(2)}, u32[]{:S(2)}) collective-permute-start(f32[2,8,8,1]{3,2,1,0:T(8,128)} %get-tuple-element.35), channel_id=1, source_target_pairs={{16,0},{32,16},{48,32},{64,48},{80,64},{96,80},{112,96},{128,112},... | collective-permute-start | bytes 1544 | tf_op jit(solution)/shard_map/ppermute | solution.py:22
  74.4 10.1 %collective-permute-start.4 = (f32[2,8,8,1]{3,2,1,0:T(8,128)}, f32[2,8,8,1]{3,2,1,0:T(8,128)}, u32[]{:S(2)}, u32[]{:S(2)}) collective-permute-start(f32[2,8,8,1]{3,2,1,0:T(8,128)} %get-tuple-element.36), channel_id=1, source_target_pairs={{0,16},{16,32},{32,48},{48,64},{64,80},{80,96},{96,112},{112,128},... | collective-permute-start | bytes 1544 | tf_op jit(solution)/shard_map/ppermute | solution.py:21
  76.8 11.3 %collective-permute-start.6 = (f32[2,8,1,2048]{3,2,1,0:T(1,128)S(1)}, f32[2,8,1,2048]{3,2,1,0:T(1,128)S(1)}, u32[]{:S(2)}, u32[]{:S(2)}) collective-permute-start(f32[2,8,1,2048]{3,2,1,0:T(1,128)S(1)} %get-tuple-element.37), channel_id=1, source_target_pairs={{0,1},{1,2},{2,3},{3,4},{4,5},{5,6},{6,7},{7,8},{8,9},{9,10},{10,1... | collective-permute-start | bytes 393224 | tf_op jit(solution)/shard_map/ppermute | solution.py:21
  76.8 11.3 %collective-permute-start.7 = (f32[2,8,1,2048]{3,2,1,0:T(1,128)S(1)}, f32[2,8,1,2048]{3,2,1,0:T(1,128)S(1)}, u32[]{:S(2)}, u32[]{:S(2)}) collective-permute-start(f32[2,8,1,2048]{3,2,1,0:T(1,128)S(1)} %get-tuple-element.38), channel_id=1, source_target_pairs={{1,0},{2,1},{3,2},{4,3},{5,4},{6,5},{7,6},{8,7},{9,8},{10,9},{11,1... | collective-permute-start | bytes 393224 | tf_op jit(solution)/shard_map/ppermute | solution.py:22
  78.5 17.9 %all-to-all-start.2 = ((f32[16,4,2048]{2,1,0:T(4,128)}), f32[16,4,2048]{2,1,0:T(4,128)}, u32[]{:S(2)}, u32[]{:S(2)}) async-start(f32[16,4,2048]{2,1,0:T(4,128)} %all_to_all.54), calls=%async_computation.2 | async-start | bytes 1048576 | tf_op jit(solution)/shard_map/all_to_all | solution.py:157
  105.5 5.8 %collective-permute-start.9 = (f32[2,128]{1,0:T(2,128)S(1)}, f32[2,128]{1,0:T(2,128)S(1)}, u32[]{:S(2)}, u32[]{:S(2)}) collective-permute-start(f32[2,128]{1,0:T(2,128)S(1)} %broadcast_in_dim.51), channel_id=1, source_target_pairs={{0,32},{16,48},{32,0},{48,16},{64,96},{80,112},{96,64},{112,80},{1... | collective-permute-start | bytes 3080 | tf_op jit(solution)/shard_map/ppermute | solution.py:106
  106.6 4.8 %collective-permute-start.10 = (f32[2,128]{1,0:T(2,128)S(1)}, f32[2,128]{1,0:T(2,128)S(1)}, u32[]{:S(2)}, u32[]{:S(2)}) collective-permute-start(f32[2,128]{1,0:T(2,128)S(1)} %broadcast_in_dim.51), channel_id=1, source_target_pairs={{0,48},{16,32},{32,16},{48,0},{64,112},{80,96},{96,80},{112,64},{1... | collective-permute-start | bytes 3080 | tf_op jit(solution)/shard_map/ppermute | solution.py:106
  108.7 3.6 %collective-permute-start.8 = (f32[2,128]{1,0:T(2,128)S(1)}, f32[2,128]{1,0:T(2,128)S(1)}, u32[]{:S(2)}, u32[]{:S(2)}) collective-permute-start(f32[2,128]{1,0:T(2,128)S(1)} %broadcast_in_dim.51), channel_id=1, source_target_pairs={{0,16},{16,0},{32,48},{48,32},{64,80},{80,64},{96,112},{112,96},{1... | collective-permute-start | bytes 3080 | tf_op jit(solution)/shard_map/ppermute | solution.py:106
  112.4 4.8 %collective-permute-start.13 = (f32[2,128]{1,0:T(2,128)S(1)}, f32[2,128]{1,0:T(2,128)S(1)}, u32[]{:S(2)}, u32[]{:S(2)}) collective-permute-start(f32[2,128]{1,0:T(2,128)S(1)} %add_add_fusion.3), channel_id=1, source_target_pairs={{0,192},{16,208},{32,224},{48,240},{64,128},{80,144},{96,160},{112... | collective-permute-start | bytes 3080 | tf_op jit(solution)/shard_map/ppermute | solution.py:106
  113.5 5.1 %collective-permute-start.12 = (f32[2,128]{1,0:T(2,128)S(1)}, f32[2,128]{1,0:T(2,128)S(1)}, u32[]{:S(2)}, u32[]{:S(2)}) collective-permute-start(f32[2,128]{1,0:T(2,128)S(1)} %add_add_fusion.3), channel_id=1, source_target_pairs={{0,128},{16,144},{32,160},{48,176},{64,192},{80,208},{96,224},{112... | collective-permute-start | bytes 3080 | tf_op jit(solution)/shard_map/ppermute | solution.py:106
  113.9 4.6 %collective-permute-start.11 = (f32[2,128]{1,0:T(2,128)S(1)}, f32[2,128]{1,0:T(2,128)S(1)}, u32[]{:S(2)}, u32[]{:S(2)}) collective-permute-start(f32[2,128]{1,0:T(2,128)S(1)} %add_add_fusion.3), channel_id=1, source_target_pairs={{0,64},{16,80},{32,96},{48,112},{64,0},{80,16},{96,32},{112,48},{1... | collective-permute-start | bytes 3080 | tf_op jit(solution)/shard_map/ppermute | solution.py:106
  118.6 8.2 %collective-permute-start.16 = (f32[2,128]{1,0:T(2,128)S(1)}, f32[2,128]{1,0:T(2,128)S(1)}, u32[]{:S(2)}, u32[]{:S(2)}) collective-permute-start(f32[2,128]{1,0:T(2,128)S(1)} %add_add_fusion.2), channel_id=1, source_target_pairs={{0,3},{1,2},{2,1},{3,0},{4,7},{5,6},{6,5},{7,4},{8,11},{9,10},{10,... | collective-permute-start | bytes 3080 | tf_op jit(solution)/shard_map/ppermute | solution.py:106
  118.7 8.1 %collective-permute-start.15 = (f32[2,128]{1,0:T(2,128)S(1)}, f32[2,128]{1,0:T(2,128)S(1)}, u32[]{:S(2)}, u32[]{:S(2)}) collective-permute-start(f32[2,128]{1,0:T(2,128)S(1)} %add_add_fusion.2), channel_id=1, source_target_pairs={{0,2},{1,3},{2,0},{3,1},{4,6},{5,7},{6,4},{7,5},{8,10},{9,11},{10,... | collective-permute-start | bytes 3080 | tf_op jit(solution)/shard_map/ppermute | solution.py:106
  118.9 8.0 %collective-permute-start.14 = (f32[2,128]{1,0:T(2,128)S(1)}, f32[2,128]{1,0:T(2,128)S(1)}, u32[]{:S(2)}, u32[]{:S(2)}) collective-permute-start(f32[2,128]{1,0:T(2,128)S(1)} %add_add_fusion.2), channel_id=1, source_target_pairs={{0,1},{1,0},{2,3},{3,2},{4,5},{5,4},{6,7},{7,6},{8,9},{9,8},{10,11... | collective-permute-start | bytes 3080 | tf_op jit(solution)/shard_map/ppermute | solution.py:106
  122.5 18.8 %all-to-all-start.3 = ((f32[4,16,2048]{2,0,1:T(4,128)}), f32[4,16,2048]{2,0,1:T(4,128)S(1)}, u32[]{:S(2)}, u32[]{:S(2)}) async-start(f32[4,16,2048]{2,0,1:T(4,128)} %copy.69), calls=%async_computation.3 | async-start | bytes 1048576 | tf_op jit(solution)/shard_map/all_to_all | solution.py:165
  126.8 7.5 %collective-permute-start.19 = (f32[2,128]{1,0:T(2,128)S(1)}, f32[2,128]{1,0:T(2,128)S(1)}, u32[]{:S(2)}, u32[]{:S(2)}) collective-permute-start(f32[2,128]{1,0:T(2,128)S(1)} %add_add_fusion.1), channel_id=1, source_target_pairs={{0,12},{1,13},{2,14},{3,15},{4,8},{5,9},{6,10},{7,11},{8,4},{9,5},... | collective-permute-start | bytes 3080 | tf_op jit(solution)/shard_map/ppermute | solution.py:106
  129.7 7.5 %collective-permute-start.18 = (f32[2,128]{1,0:T(2,128)S(1)}, f32[2,128]{1,0:T(2,128)S(1)}, u32[]{:S(2)}, u32[]{:S(2)}) collective-permute-start(f32[2,128]{1,0:T(2,128)S(1)} %add_add_fusion.1), channel_id=1, source_target_pairs={{0,8},{1,9},{2,10},{3,11},{4,12},{5,13},{6,14},{7,15},{8,0},{9,1},... | collective-permute-start | bytes 3080 | tf_op jit(solution)/shard_map/ppermute | solution.py:106
  134.4 4.5 %collective-permute-start.17 = (f32[2,128]{1,0:T(2,128)S(1)}, f32[2,128]{1,0:T(2,128)S(1)}, u32[]{:S(2)}, u32[]{:S(2)}) collective-permute-start(f32[2,128]{1,0:T(2,128)S(1)} %add_add_fusion.1), channel_id=1, source_target_pairs={{0,4},{1,5},{2,6},{3,7},{4,0},{5,1},{6,2},{7,3},{8,12},{9,13},{10,... | collective-permute-start | bytes 3080 | tf_op jit(solution)/shard_map/ppermute | solution.py:106
  (33 other events, 152.1 us)

commit v7 on v5

--- a/solution.py
+++ b/solution.py
@@ -135,7 +135,7 @@
         return jnp.pad(rows, ((0, 0), (1, length - support - 1)))
 
     first_line = lax.axis_index("gx") * per_dev
-    line_rates = jnp.take(jump_rate, (first_line + lax.iota(jnp.int32, per_dev)) // y_rows)
+    kernel_mass = jnp.sum(weights, axis=1)
     if y_rows % per_dev == 0:
         own = pad_lines(lax.dynamic_slice_in_dim(weights, first_line // y_rows, 1, axis=0))
         own_re, own_im = forward_lines(own, tables)
@@ -194,8 +194,8 @@
             - kill[None] * field
             + mixing
         )
-        jump_mass = length * (spec_re[:, 0, 0] * line_re[:, 0, 0] - spec_im[:, 0, 0] * line_im[:, 0, 0])
-        sums.append(jnp.sum(rest) + jnp.sum(line_rates * jump_mass))
+        jump_mass = kernel_mass * jnp.sum(field, axis=(1, 2))
+        sums.append(jnp.sum(rest) + jnp.sum(jump_rate * jump_mass))
         field = updated
     cell_count = field.size * lax.axis_size("gx") * lax.axis_size("gy")
     totals = tree_sum(jnp.broadcast_to(jnp.stack(sums)[:, None], (len(sums), 128)))[:, 0]

time: 144 us -> 141 us (0.979)
  the two profiles are of different devices: /device:TPU:32 before, /device:TPU:2 now
where the time goes in v7:
time: 141 us; the launch traced here: 140 us
  starting transfers between devices  58.7 us (42%)
  local copies, waits for them, and re-layouts  27.6 us (20%)
  other arithmetic  20.9 us (15%)
  waiting for transfers between devices  18.2 us (13%)
  matrix products  9.8 us (7%)
  between operations  5.15 us (4%)
    ppermute x12, starting transfers between devices, tree_sum(): lax.ppermute(values, axis, [(i, i ^ d << low) for i in range(peers)])  16.6 us
    all_to_all x2, starting transfers between devices, local(): lax.all_to_all(field.reshape(regimes * y_rows, x_cols), 'gx', split_axis=...  15.1 us
    ppermute x4, starting transfers between devices, with_halo(): after = lax.ppermute(leading, axis, down)  13.4 us
    all_to_all x2, starting transfers between devices, local(): lax.all_to_all(jump_line, 'gx', split_axis=1, concat_axis=0, tiled=True)  11.5 us
    ppermute x12, waiting for transfers between devices, tree_sum(): lax.ppermute(values, axis, [(i, i ^ d << low) for i in range(peers)])  11.5 us
    another operation x6, other arithmetic, local(): jnp.stack([field, drift[0][None] * field])  7.16 us
    all_to_all x4, local copies, waits for them, and re-layouts, local(): lax.all_to_all(field.reshape(regimes * y_rows, x_cols), 'gx', split_axis=...  6.78 us
    all_to_all x2, waiting for transfers between devices, local(): lax.all_to_all(jump_line, 'gx', split_axis=1, concat_axis=0, tiled=True)  6.67 us
  transfers between devices with their start and end apart: 24, of which 9 were waited for; matrix products, arithmetic and copies ran while one was open for 23% of the time, Pallas kernels for 0%

profile of v7, /device:TPU:2, one launch (start us, length us, event | category | flops | bytes accessed | tf_op | source)
XLA Modules:
  0.0 140.4 jit_solution(3448397726861096853)
XLA Ops:
  0.0 2.0 %all_to_all.48 = f32[16,4,2048]{2,1,0:T(4,128)} reshape(f32[8,8,2048]{2,1,0:T(8,128)} %param.9) | data formatting | bytes 1048576 | tf_op jit(solution)/shard_map/all_to_all | solution.py:157
  2.1 7.5 %all-to-all-start = ((f32[16,4,2048]{2,1,0:T(4,128)}), f32[16,4,2048]{2,1,0:T(4,128)}, u32[]{:S(2)}, u32[]{:S(2)}) async-start(f32[16,4,2048]{2,1,0:T(4,128)} %all_to_all.48), calls=%async_computation | async-start | bytes 1048576 | tf_op jit(solution)/shard_map/all_to_all | solution.py:157
  12.1 2.7 %collective-permute-start.1 = (f32[2,8,8,1]{3,1,2,0:T(8,128)}, f32[2,8,8,1]{3,1,2,0:T(8,128)}, u32[]{:S(2)}, u32[]{:S(2)}) collective-permute-start(f32[2,8,8,1]{3,1,2,0:T(8,128)} %get-tuple-element.40), channel_id=1, source_target_pairs={{16,0},{32,16},{48,32},{64,48},{80,64},{96,80},{112,96},{128,112},... | collective-permute-start | bytes 1544 | tf_op jit(solution)/shard_map/ppermute | solution.py:22
  15.5 4.2 %collective-permute-start.3 = (f32[2,8,1,2048]{3,1,2,0:T(8,128)}, f32[2,8,1,2048]{3,1,2,0:T(8,128)}, u32[]{:S(2)}, u32[]{:S(2)}) collective-permute-start(f32[2,8,1,2048]{3,1,2,0:T(8,128)} %get-tuple-element.43), channel_id=1, source_target_pairs={{1,0},{2,1},{3,2},{4,3},{5,4},{6,5},{7,6},{8,7},{9,8},{10,9},{11,1... | collective-permute-start | bytes 393224 | tf_op jit(solution)/shard_map/ppermute | solution.py:22
  29.6 1.7 %concatenate.69 = f32[2,8,8,2050]{3,1,2,0:T(8,128)S(1)} concatenate(f32[2,8,8,1]{3,1,2,0:T(8,128)} %collective-permute-done, f32[2,8,8,2048]{3,1,2,0:T(8,128)} %pad_maximum_fusion, f32[2,8,8,1]{3,1,2,0:T(8,128)} %collective-permute-done.1), dimensions={3} | concatenate | bytes 2099200 | tf_op jit(solution)/shard_map/concatenate | solution.py:23
  43.2 2.2 %copy.100 = f32[4,16,2048]{2,0,1:T(4,128)} copy(f32[4,16,2048]{2,1,0:T(8,128)} %all_to_all.51) | data formatting | bytes 1048576 | tf_op jit(solution)/shard_map/all_to_all | solution.py:165
  45.4 5.1 %all-to-all-start.1 = ((f32[4,16,2048]{2,0,1:T(4,128)}), f32[4,16,2048]{2,0,1:T(4,128)S(1)}, u32[]{:S(2)}, u32[]{:S(2)}) async-start(f32[4,16,2048]{2,0,1:T(4,128)} %copy.100), calls=%async_computation.1 | async-start | bytes 1048576 | tf_op jit(solution)/shard_map/all_to_all | solution.py:165
  51.7 6.7 %all-to-all-done.1 = f32[4,16,2048]{2,0,1:T(4,128)S(1)} async-done(((f32[4,16,2048]{2,0,1:T(4,128)}), f32[4,16,2048]{2,0,1:T(4,128)S(1)}, u32[]{:S(2)}, u32[]{:S(2)}) %all-to-all-start.1) | async-done | bytes 524320 | tf_op jit(solution)/shard_map/all_to_all | solution.py:165
  59.4 3.2 %multiply_bitcast_fusion.1 = (f32[1,8,8,2048]{3,1,2,0:T(8,128)S(1)}, f32[8,8,2048]{2,0,1:T(8,128)S(1)}, f32[8,8,2048]{2,0,1:T(8,128)S(1)}) fusion(f32[8,2048]{1,0:T(8,128)} %copy-done.16, f32[8,8,2048]{2,0,1:T(8,128)S(1)} %fusion.55, f32[8,2048]{1,0:T(8,128)} %param.11, f32[8,8,2048]{2,1,0:T(8,128)S(1)} %copy-done, f32[8,8,2048]{2,1,0:T(8,128)} %reshape.125, ...), kind=kLoop, calls=%fused_computation.105 | loop fusion | flops 2621440 | bytes 7471168 | tf_op jit(solution)/shard_map/stack | solution.py:168
  65.5 3.6 %collective-permute-start.5 = (f32[2,8,8,1]{3,1,2,0:T(8,128)S(1)}, f32[2,8,8,1]{3,1,2,0:T(8,128)}, u32[]{:S(2)}, u32[]{:S(2)}) collective-permute-start(f32[2,8,8,1]{3,1,2,0:T(8,128)S(1)} %get-tuple-element.36), channel_id=1, source_target_pairs={{16,0},{32,16},{48,32},{64,48},{80,64},{96,80},{112,96},{128,112},... | collective-permute-start | bytes 1544 | tf_op jit(solution)/shard_map/ppermute | solution.py:22
  70.9 3.0 %collective-permute-start.7 = (f32[2,8,1,2048]{3,1,2,0:T(8,128)}, f32[2,8,1,2048]{3,1,2,0:T(8,128)}, u32[]{:S(2)}, u32[]{:S(2)}) collective-permute-start(f32[2,8,1,2048]{3,1,2,0:T(8,128)} %get-tuple-element.39), channel_id=1, source_target_pairs={{1,0},{2,1},{3,2},{4,3},{5,4},{6,5},{7,6},{8,7},{9,8},{10,9},{11,1... | collective-permute-start | bytes 393224 | tf_op jit(solution)/shard_map/ppermute | solution.py:22
  73.9 2.0 %all_to_all.54 = f32[16,4,2048]{2,1,0:T(4,128)} reshape(f32[8,8,2048]{2,1,0:T(8,128)} %copy.106) | data formatting | bytes 1048576 | tf_op jit(solution)/shard_map/all_to_all | solution.py:157
  75.9 7.6 %all-to-all-start.2 = ((f32[16,4,2048]{2,1,0:T(4,128)}), f32[16,4,2048]{2,1,0:T(4,128)}, u32[]{:S(2)}, u32[]{:S(2)}) async-start(f32[16,4,2048]{2,1,0:T(4,128)} %all_to_all.54), calls=%async_computation.2 | async-start | bytes 1048576 | tf_op jit(solution)/shard_map/all_to_all | solution.py:157
  83.5 2.3 %concatenate.83 = f32[2,8,8,2050]{3,1,2,0:T(8,128)} concatenate(f32[2,8,8,1]{3,1,2,0:T(8,128)} %collective-permute-done.4, f32[2,8,8,2048]{3,1,2,0:T(8,128)} %pad_maximum_fusion.1, f32[2,8,8,1]{3,1,2,0:T(8,128)} %collective-permute-done.5), dimensions={3} | concatenate | bytes 2099200 | tf_op jit(solution)/shard_map/concatenate | solution.py:23
  93.7 2.7 %collective-permute-start.10 = (f32[2,128]{1,0:T(2,128)S(1)}, f32[2,128]{1,0:T(2,128)S(1)}, u32[]{:S(2)}, u32[]{:S(2)}) collective-permute-start(f32[2,128]{1,0:T(2,128)S(1)} %broadcast_in_dim.37), channel_id=1, source_target_pairs={{0,48},{16,32},{32,16},{48,0},{64,112},{80,96},{96,80},{112,64},{1... | collective-permute-start | bytes 3080 | tf_op jit(solution)/shard_map/ppermute | solution.py:106
  96.7 1.8 %collective-permute-start.9 = (f32[2,128]{1,0:T(2,128)S(1)}, f32[2,128]{1,0:T(2,128)S(1)}, u32[]{:S(2)}, u32[]{:S(2)}) collective-permute-start(f32[2,128]{1,0:T(2,128)S(1)} %broadcast_in_dim.37), channel_id=1, source_target_pairs={{0,32},{16,48},{32,0},{48,16},{64,96},{80,112},{96,64},{112,80},{1... | collective-permute-start | bytes 3080 | tf_op jit(solution)/shard_map/ppermute | solution.py:106
  100.0 1.7 %collective-permute-done.9 = f32[2,128]{1,0:T(2,128)S(1)} collective-permute-done((f32[2,128]{1,0:T(2,128)S(1)}, f32[2,128]{1,0:T(2,128)S(1)}, u32[]{:S(2)}, u32[]{:S(2)}) %collective-permute-start.9) | collective-permute-done | bytes 1056 | tf_op jit(solution)/shard_map/ppermute | solution.py:106
  102.4 2.4 %collective-permute-start.12 = (f32[2,128]{1,0:T(2,128)S(1)}, f32[2,128]{1,0:T(2,128)S(1)}, u32[]{:S(2)}, u32[]{:S(2)}) collective-permute-start(f32[2,128]{1,0:T(2,128)S(1)} %add_add_fusion.3), channel_id=1, source_target_pairs={{0,128},{16,144},{32,160},{48,176},{64,192},{80,208},{96,224},{112... | collective-permute-start | bytes 3080 | tf_op jit(solution)/shard_map/ppermute | solution.py:106
  105.4 2.0 %collective-permute-done.12 = f32[2,128]{1,0:T(2,128)S(1)} collective-permute-done((f32[2,128]{1,0:T(2,128)S(1)}, f32[2,128]{1,0:T(2,128)S(1)}, u32[]{:S(2)}, u32[]{:S(2)}) %collective-permute-start.12) | collective-permute-done | bytes 1056 | tf_op jit(solution)/shard_map/ppermute | solution.py:106
  117.9 6.4 %all-to-all-start.3 = ((f32[4,16,2048]{2,0,1:T(4,128)}), f32[4,16,2048]{2,0,1:T(4,128)S(1)}, u32[]{:S(2)}, u32[]{:S(2)}) async-start(f32[4,16,2048]{2,0,1:T(4,128)} %copy.114), calls=%async_computation.3 | async-start | bytes 1048576 | tf_op jit(solution)/shard_map/all_to_all | solution.py:165
  124.3 2.0 %collective-permute-start.17 = (f32[2,128]{1,0:T(2,128)S(1)}, f32[2,128]{1,0:T(2,128)S(1)}, u32[]{:S(2)}, u32[]{:S(2)}) collective-permute-start(f32[2,128]{1,0:T(2,128)S(1)} %add_add_fusion.1), channel_id=1, source_target_pairs={{0,4},{1,5},{2,6},{3,7},{4,0},{5,1},{6,2},{7,3},{8,12},{9,13},{10,... | collective-permute-start | bytes 3080 | tf_op jit(solution)/shard_map/ppermute | solution.py:106
  126.3 4.1 %collective-permute-start.18 = (f32[2,128]{1,0:T(2,128)S(1)}, f32[2,128]{1,0:T(2,128)S(1)}, u32[]{:S(2)}, u32[]{:S(2)}) collective-permute-start(f32[2,128]{1,0:T(2,128)S(1)} %add_add_fusion.1), channel_id=1, source_target_pairs={{0,8},{1,9},{2,10},{3,11},{4,12},{5,13},{6,14},{7,15},{8,0},{9,1},... | collective-permute-start | bytes 3080 | tf_op jit(solution)/shard_map/ppermute | solution.py:106
  130.9 2.9 %collective-permute-done.18 = f32[2,128]{1,0:T(2,128)S(1)} collective-permute-done((f32[2,128]{1,0:T(2,128)S(1)}, f32[2,128]{1,0:T(2,128)S(1)}, u32[]{:S(2)}, u32[]{:S(2)}) %collective-permute-start.18) | collective-permute-done | bytes 1056 | tf_op jit(solution)/shard_map/ppermute | solution.py:106
  133.8 2.3 %collective-permute-done.19 = f32[2,128]{1,0:T(2,128)S(1)} collective-permute-done((f32[2,128]{1,0:T(2,128)S(1)}, f32[2,128]{1,0:T(2,128)S(1)}, u32[]{:S(2)}, u32[]{:S(2)}) %collective-permute-start.19) | collective-permute-done | bytes 1056 | tf_op jit(solution)/shard_map/ppermute | solution.py:106
  (172 shorter events, 53.3 us)
Async XLA Ops:
  2.1 32.1 %all-to-all-start = ((f32[16,4,2048]{2,1,0:T(4,128)}), f32[16,4,2048]{2,1,0:T(4,128)}, u32[]{:S(2)}, u32[]{:S(2)}) async-start(f32[16,4,2048]{2,1,0:T(4,128)} %all_to_all.48), calls=%async_computation | async-start | bytes 1048576 | tf_op jit(solution)/shard_map/all_to_all | solution.py:157
  10.7 18.9 %collective-permute-start = (f32[2,8,8,1]{3,1,2,0:T(8,128)}, f32[2,8,8,1]{3,1,2,0:T(8,128)}, u32[]{:S(2)}, u32[]{:S(2)}) collective-permute-start(f32[2,8,8,1]{3,1,2,0:T(8,128)} %get-tuple-element.41), channel_id=1, source_target_pairs={{0,16},{16,32},{32,48},{48,64},{64,80},{80,96},{96,112},{112,128},... | collective-permute-start | bytes 1544 | tf_op jit(solution)/shard_map/ppermute | solution.py:21
  12.1 17.4 %collective-permute-start.1 = (f32[2,8,8,1]{3,1,2,0:T(8,128)}, f32[2,8,8,1]{3,1,2,0:T(8,128)}, u32[]{:S(2)}, u32[]{:S(2)}) collective-permute-start(f32[2,8,8,1]{3,1,2,0:T(8,128)} %get-tuple-element.40), channel_id=1, source_target_pairs={{16,0},{32,16},{48,32},{64,48},{80,64},{96,80},{112,96},{128,112},... | collective-permute-start | bytes 1544 | tf_op jit(solution)/shard_map/ppermute | solution.py:22
  15.5 16.8 %collective-permute-start.2 = (f32[2,8,1,2048]{3,1,2,0:T(8,128)}, f32[2,8,1,2048]{3,1,2,0:T(8,128)S(1)}, u32[]{:S(2)}, u32[]{:S(2)}) collective-permute-start(f32[2,8,1,2048]{3,1,2,0:T(8,128)} %get-tuple-element.42), channel_id=1, source_target_pairs={{0,1},{1,2},{2,3},{3,4},{4,5},{5,6},{6,7},{7,8},{8,9},{9,10},{10,1... | collective-permute-start | bytes 393224 | tf_op jit(solution)/shard_map/ppermute | solution.py:21
  15.5 17.5 %collective-permute-start.3 = (f32[2,8,1,2048]{3,1,2,0:T(8,128)}, f32[2,8,1,2048]{3,1,2,0:T(8,128)}, u32[]{:S(2)}, u32[]{:S(2)}) collective-permute-start(f32[2,8,1,2048]{3,1,2,0:T(8,128)} %get-tuple-element.43), channel_id=1, source_target_pairs={{1,0},{2,1},{3,2},{4,3},{5,4},{6,5},{7,6},{8,7},{9,8},{10,9},{11,1... | collective-permute-start | bytes 393224 | tf_op jit(solution)/shard_map/ppermute | solution.py:22
  45.4 13.0 %all-to-all-start.1 = ((f32[4,16,2048]{2,0,1:T(4,128)}), f32[4,16,2048]{2,0,1:T(4,128)S(1)}, u32[]{:S(2)}, u32[]{:S(2)}) async-start(f32[4,16,2048]{2,0,1:T(4,128)} %copy.100), calls=%async_computation.1 | async-start | bytes 1048576 | tf_op jit(solution)/shard_map/all_to_all | solution.py:165
  64.9 18.6 %collective-permute-start.4 = (f32[2,8,8,1]{3,1,2,0:T(8,128)}, f32[2,8,8,1]{3,1,2,0:T(8,128)}, u32[]{:S(2)}, u32[]{:S(2)}) collective-permute-start(f32[2,8,8,1]{3,1,2,0:T(8,128)} %get-tuple-element.37), channel_id=1, source_target_pairs={{0,16},{16,32},{32,48},{48,64},{64,80},{80,96},{96,112},{112,128},... | collective-permute-start | bytes 1544 | tf_op jit(solution)/shard_map/ppermute | solution.py:21
  65.5 18.0 %collective-permute-start.5 = (f32[2,8,8,1]{3,1,2,0:T(8,128)S(1)}, f32[2,8,8,1]{3,1,2,0:T(8,128)}, u32[]{:S(2)}, u32[]{:S(2)}) collective-permute-start(f32[2,8,8,1]{3,1,2,0:T(8,128)S(1)} %get-tuple-element.36), channel_id=1, source_target_pairs={{16,0},{32,16},{48,32},{64,48},{80,64},{96,80},{112,96},{128,112},... | collective-permute-start | bytes 1544 | tf_op jit(solution)/shard_map/ppermute | solution.py:22
  70.9 16.2 %collective-permute-start.6 = (f32[2,8,1,2048]{3,1,2,0:T(8,128)}, f32[2,8,1,2048]{3,1,2,0:T(8,128)S(1)}, u32[]{:S(2)}, u32[]{:S(2)}) collective-permute-start(f32[2,8,1,2048]{3,1,2,0:T(8,128)} %get-tuple-element.38), channel_id=1, source_target_pairs={{0,1},{1,2},{2,3},{3,4},{4,5},{5,6},{6,7},{7,8},{8,9},{9,10},{10,1... | collective-permute-start | bytes 393224 | tf_op jit(solution)/shard_map/ppermute | solution.py:21
  70.9 16.2 %collective-permute-start.7 = (f32[2,8,1,2048]{3,1,2,0:T(8,128)}, f32[2,8,1,2048]{3,1,2,0:T(8,128)}, u32[]{:S(2)}, u32[]{:S(2)}) collective-permute-start(f32[2,8,1,2048]{3,1,2,0:T(8,128)} %get-tuple-element.39), channel_id=1, source_target_pairs={{1,0},{2,1},{3,2},{4,3},{5,4},{6,5},{7,6},{8,7},{9,8},{10,9},{11,1... | collective-permute-start | bytes 393224 | tf_op jit(solution)/shard_map/ppermute | solution.py:22
  75.9 34.3 %all-to-all-start.2 = ((f32[16,4,2048]{2,1,0:T(4,128)}), f32[16,4,2048]{2,1,0:T(4,128)}, u32[]{:S(2)}, u32[]{:S(2)}) async-start(f32[16,4,2048]{2,1,0:T(4,128)} %all_to_all.54), calls=%async_computation.2 | async-start | bytes 1048576 | tf_op jit(solution)/shard_map/all_to_all | solution.py:157
  93.7 4.8 %collective-permute-start.10 = (f32[2,128]{1,0:T(2,128)S(1)}, f32[2,128]{1,0:T(2,128)S(1)}, u32[]{:S(2)}, u32[]{:S(2)}) collective-permute-start(f32[2,128]{1,0:T(2,128)S(1)} %broadcast_in_dim.37), channel_id=1, source_target_pairs={{0,48},{16,32},{32,16},{48,0},{64,112},{80,96},{96,80},{112,64},{1... | collective-permute-start | bytes 3080 | tf_op jit(solution)/shard_map/ppermute | solution.py:106
  96.4 3.6 %collective-permute-start.8 = (f32[2,128]{1,0:T(2,128)S(1)}, f32[2,128]{1,0:T(2,128)S(1)}, u32[]{:S(2)}, u32[]{:S(2)}) collective-permute-start(f32[2,128]{1,0:T(2,128)S(1)} %broadcast_in_dim.37), channel_id=1, source_target_pairs={{0,16},{16,0},{32,48},{48,32},{64,80},{80,64},{96,112},{112,96},{1... | collective-permute-start | bytes 3080 | tf_op jit(solution)/shard_map/ppermute | solution.py:106
  96.7 5.1 %collective-permute-start.9 = (f32[2,128]{1,0:T(2,128)S(1)}, f32[2,128]{1,0:T(2,128)S(1)}, u32[]{:S(2)}, u32[]{:S(2)}) collective-permute-start(f32[2,128]{1,0:T(2,128)S(1)} %broadcast_in_dim.37), channel_id=1, source_target_pairs={{0,32},{16,48},{32,0},{48,16},{64,96},{80,112},{96,64},{112,80},{1... | collective-permute-start | bytes 3080 | tf_op jit(solution)/shard_map/ppermute | solution.py:106
  101.8 3.6 %collective-permute-start.11 = (f32[2,128]{1,0:T(2,128)S(1)}, f32[2,128]{1,0:T(2,128)S(1)}, u32[]{:S(2)}, u32[]{:S(2)}) collective-permute-start(f32[2,128]{1,0:T(2,128)S(1)} %add_add_fusion.3), channel_id=1, source_target_pairs={{0,64},{16,80},{32,96},{48,112},{64,0},{80,16},{96,32},{112,48},{1... | collective-permute-start | bytes 3080 | tf_op jit(solution)/shard_map/ppermute | solution.py:106
  102.4 5.1 %collective-permute-start.12 = (f32[2,128]{1,0:T(2,128)S(1)}, f32[2,128]{1,0:T(2,128)S(1)}, u32[]{:S(2)}, u32[]{:S(2)}) collective-permute-start(f32[2,128]{1,0:T(2,128)S(1)} %add_add_fusion.3), channel_id=1, source_target_pairs={{0,128},{16,144},{32,160},{48,176},{64,192},{80,208},{96,224},{112... | collective-permute-start | bytes 3080 | tf_op jit(solution)/shard_map/ppermute | solution.py:106
  104.8 3.6 %collective-permute-start.13 = (f32[2,128]{1,0:T(2,128)S(1)}, f32[2,128]{1,0:T(2,128)S(1)}, u32[]{:S(2)}, u32[]{:S(2)}) collective-permute-start(f32[2,128]{1,0:T(2,128)S(1)} %add_add_fusion.3), channel_id=1, source_target_pairs={{0,192},{16,208},{32,224},{48,240},{64,128},{80,144},{96,160},{112... | collective-permute-start | bytes 3080 | tf_op jit(solution)/shard_map/ppermute | solution.py:106
  108.4 15.9 %collective-permute-start.14 = (f32[2,128]{1,0:T(2,128)S(1)}, f32[2,128]{1,0:T(2,128)S(1)}, u32[]{:S(2)}, u32[]{:S(2)}) collective-permute-start(f32[2,128]{1,0:T(2,128)S(1)} %add_add_fusion.2), channel_id=1, source_target_pairs={{0,1},{1,0},{2,3},{3,2},{4,5},{5,4},{6,7},{7,6},{8,9},{9,8},{10,11... | collective-permute-start | bytes 3080 | tf_op jit(solution)/shard_map/ppermute | solution.py:106
  108.4 15.9 %collective-permute-start.15 = (f32[2,128]{1,0:T(2,128)S(1)}, f32[2,128]{1,0:T(2,128)S(1)}, u32[]{:S(2)}, u32[]{:S(2)}) collective-permute-start(f32[2,128]{1,0:T(2,128)S(1)} %add_add_fusion.2), channel_id=1, source_target_pairs={{0,2},{1,3},{2,0},{3,1},{4,6},{5,7},{6,4},{7,5},{8,10},{9,11},{10,... | collective-permute-start | bytes 3080 | tf_op jit(solution)/shard_map/ppermute | solution.py:106
  108.6 15.7 %collective-permute-start.16 = (f32[2,128]{1,0:T(2,128)S(1)}, f32[2,128]{1,0:T(2,128)S(1)}, u32[]{:S(2)}, u32[]{:S(2)}) collective-permute-start(f32[2,128]{1,0:T(2,128)S(1)} %add_add_fusion.2), channel_id=1, source_target_pairs={{0,3},{1,2},{2,1},{3,0},{4,7},{5,6},{6,5},{7,4},{8,11},{9,10},{10,... | collective-permute-start | bytes 3080 | tf_op jit(solution)/shard_map/ppermute | solution.py:106
  117.9 20.8 %all-to-all-start.3 = ((f32[4,16,2048]{2,0,1:T(4,128)}), f32[4,16,2048]{2,0,1:T(4,128)S(1)}, u32[]{:S(2)}, u32[]{:S(2)}) async-start(f32[4,16,2048]{2,0,1:T(4,128)} %copy.114), calls=%async_computation.3 | async-start | bytes 1048576 | tf_op jit(solution)/shard_map/all_to_all | solution.py:165
  124.3 6.6 %collective-permute-start.17 = (f32[2,128]{1,0:T(2,128)S(1)}, f32[2,128]{1,0:T(2,128)S(1)}, u32[]{:S(2)}, u32[]{:S(2)}) collective-permute-start(f32[2,128]{1,0:T(2,128)S(1)} %add_add_fusion.1), channel_id=1, source_target_pairs={{0,4},{1,5},{2,6},{3,7},{4,0},{5,1},{6,2},{7,3},{8,12},{9,13},{10,... | collective-permute-start | bytes 3080 | tf_op jit(solution)/shard_map/ppermute | solution.py:106
  126.3 7.5 %collective-permute-start.18 = (f32[2,128]{1,0:T(2,128)S(1)}, f32[2,128]{1,0:T(2,128)S(1)}, u32[]{:S(2)}, u32[]{:S(2)}) collective-permute-start(f32[2,128]{1,0:T(2,128)S(1)} %add_add_fusion.1), channel_id=1, source_target_pairs={{0,8},{1,9},{2,10},{3,11},{4,12},{5,13},{6,14},{7,15},{8,0},{9,1},... | collective-permute-start | bytes 3080 | tf_op jit(solution)/shard_map/ppermute | solution.py:106
  130.4 5.7 %collective-permute-start.19 = (f32[2,128]{1,0:T(2,128)S(1)}, f32[2,128]{1,0:T(2,128)S(1)}, u32[]{:S(2)}, u32[]{:S(2)}) collective-permute-start(f32[2,128]{1,0:T(2,128)S(1)} %add_add_fusion.1), channel_id=1, source_target_pairs={{0,12},{1,13},{2,14},{3,15},{4,8},{5,9},{6,10},{7,11},{8,4},{9,5},... | collective-permute-start | bytes 3080 | tf_op jit(solution)/shard_map/ppermute | solution.py:106
  (37 other events, 141.9 us)

commit v8 on v7

--- a/solution.py
+++ b/solution.py
@@ -4,6 +4,7 @@
 import jax.numpy as jnp
 from jax import lax
 from jax.sharding import PartitionSpec as P
+
 
 SWEEPS = 2
 
@@ -49,8 +50,9 @@
     width_a = cos_a.shape[0]
     width_b = cos_b.shape[0]
     line_count = line_data.shape[0]
-    blocks = line_data.reshape(line_count, width_a, width_b)
-    table_a = jnp.concatenate([cos_a, -sin_a], axis=1)
+    rows = line_data.shape[1] // width_b
+    blocks = line_data.reshape(line_count, rows, width_b)
+    table_a = jnp.concatenate([cos_a, -sin_a], axis=1)[:rows]
     first = jnp.einsum("mab,ak->mkb", blocks, table_a, precision=HIGHEST_PRECISION)
     first_re, first_im = first[:, :width_a], first[:, width_a:]
     turned_re = first_re * cos_t + first_im * sin_t
@@ -137,7 +139,11 @@
     first_line = lax.axis_index("gx") * per_dev
     kernel_mass = jnp.sum(weights, axis=1)
     if y_rows % per_dev == 0:
-        own = pad_lines(lax.dynamic_slice_in_dim(weights, first_line // y_rows, 1, axis=0))
+        rows = min(-(-(support + 1) // width_b), width_a)
+        own = jnp.pad(
+            lax.dynamic_slice_in_dim(weights, first_line // y_rows, 1, axis=0),
+            ((0, 0), (1, rows * width_b - support - 1)),
+        )
         own_re, own_im = forward_lines(own, tables)
         line_re = jnp.broadcast_to(own_re / length, (per_dev,) + own_re.shape[1:])
         line_im = jnp.broadcast_to(own_im / length, (per_dev,) + own_im.shape[1:])
@@ -153,7 +159,7 @@
     scale_jump = jump_rate[:, None, None]
     field = density
     sums = []
-    for sweep_index in range(SWEEPS):
+    for _ in range(SWEEPS):
         line_data = lax.all_to_all(
             field.reshape(regimes * y_rows, x_cols), "gx", split_axis=0, concat_axis=1, tiled=True
         )

time: 141 us -> 141 us (level)
  no operation moved by 1% of the time
where the time goes in v8:
time: 141 us; the launch traced here: 140 us
  starting transfers between devices  58.7 us (42%)
  local copies, waits for them, and re-layouts  27.6 us (20%)
  other arithmetic  20.9 us (15%)
  waiting for transfers between devices  18.2 us (13%)
  matrix products  9.81 us (7%)
  between operations  5.14 us (4%)
    ppermute x12, starting transfers between devices, tree_sum(): lax.ppermute(values, axis, [(i, i ^ d << low) for i in range(peers)])  16.6 us
    all_to_all x2, starting transfers between devices, local(): lax.all_to_all(field.reshape(regimes * y_rows, x_cols), 'gx', split_axis=...  15.1 us
    ppermute x4, starting transfers between devices, with_halo(): after = lax.ppermute(leading, axis, down)  13.4 us
    ppermute x12, waiting for transfers between devices, tree_sum(): lax.ppermute(values, axis, [(i, i ^ d << low) for i in range(peers)])  11.5 us
    all_to_all x2, starting transfers between devices, local(): lax.all_to_all(jump_line, 'gx', split_axis=1, concat_axis=0, tiled=True)  11.5 us
    another operation x6, other arithmetic, local(): jnp.stack([field, drift[0][None] * field])  7.16 us
    all_to_all x4, local copies, waits for them, and re-layouts, local(): lax.all_to_all(field.reshape(regimes * y_rows, x_cols), 'gx', split_axis=...  6.78 us
    all_to_all x2, waiting for transfers between devices, local(): lax.all_to_all(jump_line, 'gx', split_axis=1, concat_axis=0, tiled=True)  6.67 us
  transfers between devices with their start and end apart: 24, of which 9 were waited for; matrix products, arithmetic and copies ran while one was open for 23% of the time, Pallas kernels for 0%

profile of v8, /device:TPU:2, one launch (start us, length us, event | category | flops | bytes accessed | tf_op | source)
XLA Modules:
  0.0 140.4 jit_solution(4030161578966708316)
XLA Ops:
  0.0 2.0 %all_to_all.48 = f32[16,4,2048]{2,1,0:T(4,128)} reshape(f32[8,8,2048]{2,1,0:T(8,128)} %param.9) | data formatting | bytes 1048576 | tf_op jit(solution)/shard_map/all_to_all | solution.py:163
  2.1 7.5 %all-to-all-start = ((f32[16,4,2048]{2,1,0:T(4,128)}), f32[16,4,2048]{2,1,0:T(4,128)}, u32[]{:S(2)}, u32[]{:S(2)}) async-start(f32[16,4,2048]{2,1,0:T(4,128)} %all_to_all.48), calls=%async_computation | async-start | bytes 1048576 | tf_op jit(solution)/shard_map/all_to_all | solution.py:163
  12.1 2.7 %collective-permute-start.1 = (f32[2,8,8,1]{3,1,2,0:T(8,128)}, f32[2,8,8,1]{3,1,2,0:T(8,128)}, u32[]{:S(2)}, u32[]{:S(2)}) collective-permute-start(f32[2,8,8,1]{3,1,2,0:T(8,128)} %get-tuple-element.40), channel_id=1, source_target_pairs={{16,0},{32,16},{48,32},{64,48},{80,64},{96,80},{112,96},{128,112},... | collective-permute-start | bytes 1544 | tf_op jit(solution)/shard_map/ppermute | solution.py:23
  15.5 4.2 %collective-permute-start.3 = (f32[2,8,1,2048]{3,1,2,0:T(8,128)}, f32[2,8,1,2048]{3,1,2,0:T(8,128)}, u32[]{:S(2)}, u32[]{:S(2)}) collective-permute-start(f32[2,8,1,2048]{3,1,2,0:T(8,128)} %get-tuple-element.43), channel_id=1, source_target_pairs={{1,0},{2,1},{3,2},{4,3},{5,4},{6,5},{7,6},{8,7},{9,8},{10,9},{11,1... | collective-permute-start | bytes 393224 | tf_op jit(solution)/shard_map/ppermute | solution.py:23
  29.5 1.7 %concatenate.69 = f32[2,8,8,2050]{3,1,2,0:T(8,128)S(1)} concatenate(f32[2,8,8,1]{3,1,2,0:T(8,128)} %collective-permute-done, f32[2,8,8,2048]{3,1,2,0:T(8,128)} %pad_maximum_fusion, f32[2,8,8,1]{3,1,2,0:T(8,128)} %collective-permute-done.1), dimensions={3} | concatenate | bytes 2099200 | tf_op jit(solution)/shard_map/concatenate | solution.py:24
  43.1 2.2 %copy.100 = f32[4,16,2048]{2,0,1:T(4,128)} copy(f32[4,16,2048]{2,1,0:T(8,128)} %all_to_all.51) | data formatting | bytes 1048576 | tf_op jit(solution)/shard_map/all_to_all | solution.py:171
  45.3 5.1 %all-to-all-start.1 = ((f32[4,16,2048]{2,0,1:T(4,128)}), f32[4,16,2048]{2,0,1:T(4,128)S(1)}, u32[]{:S(2)}, u32[]{:S(2)}) async-start(f32[4,16,2048]{2,0,1:T(4,128)} %copy.100), calls=%async_computation.1 | async-start | bytes 1048576 | tf_op jit(solution)/shard_map/all_to_all | solution.py:171
  51.7 6.7 %all-to-all-done.1 = f32[4,16,2048]{2,0,1:T(4,128)S(1)} async-done(((f32[4,16,2048]{2,0,1:T(4,128)}), f32[4,16,2048]{2,0,1:T(4,128)S(1)}, u32[]{:S(2)}, u32[]{:S(2)}) %all-to-all-start.1) | async-done | bytes 524320 | tf_op jit(solution)/shard_map/all_to_all | solution.py:171
  59.3 3.2 %multiply_bitcast_fusion.1 = (f32[1,8,8,2048]{3,1,2,0:T(8,128)S(1)}, f32[8,8,2048]{2,0,1:T(8,128)S(1)}, f32[8,8,2048]{2,0,1:T(8,128)S(1)}) fusion(f32[8,2048]{1,0:T(8,128)} %copy-done.16, f32[8,8,2048]{2,0,1:T(8,128)S(1)} %fusion.55, f32[8,2048]{1,0:T(8,128)} %param.11, f32[8,8,2048]{2,1,0:T(8,128)S(1)} %copy-done, f32[8,8,2048]{2,1,0:T(8,128)} %reshape.125, ...), kind=kLoop, calls=%fused_computation.105 | loop fusion | flops 2621440 | bytes 7471168 | tf_op jit(solution)/shard_map/stack | solution.py:174
  65.4 3.6 %collective-permute-start.5 = (f32[2,8,8,1]{3,1,2,0:T(8,128)S(1)}, f32[2,8,8,1]{3,1,2,0:T(8,128)}, u32[]{:S(2)}, u32[]{:S(2)}) collective-permute-start(f32[2,8,8,1]{3,1,2,0:T(8,128)S(1)} %get-tuple-element.36), channel_id=1, source_target_pairs={{16,0},{32,16},{48,32},{64,48},{80,64},{96,80},{112,96},{128,112},... | collective-permute-start | bytes 1544 | tf_op jit(solution)/shard_map/ppermute | solution.py:23
  70.9 3.0 %collective-permute-start.7 = (f32[2,8,1,2048]{3,1,2,0:T(8,128)}, f32[2,8,1,2048]{3,1,2,0:T(8,128)}, u32[]{:S(2)}, u32[]{:S(2)}) collective-permute-start(f32[2,8,1,2048]{3,1,2,0:T(8,128)} %get-tuple-element.39), channel_id=1, source_target_pairs={{1,0},{2,1},{3,2},{4,3},{5,4},{6,5},{7,6},{8,7},{9,8},{10,9},{11,1... | collective-permute-start | bytes 393224 | tf_op jit(solution)/shard_map/ppermute | solution.py:23
  73.8 2.0 %all_to_all.54 = f32[16,4,2048]{2,1,0:T(4,128)} reshape(f32[8,8,2048]{2,1,0:T(8,128)} %copy.106) | data formatting | bytes 1048576 | tf_op jit(solution)/shard_map/all_to_all | solution.py:163
  75.8 7.6 %all-to-all-start.2 = ((f32[16,4,2048]{2,1,0:T(4,128)}), f32[16,4,2048]{2,1,0:T(4,128)}, u32[]{:S(2)}, u32[]{:S(2)}) async-start(f32[16,4,2048]{2,1,0:T(4,128)} %all_to_all.54), calls=%async_computation.2 | async-start | bytes 1048576 | tf_op jit(solution)/shard_map/all_to_all | solution.py:163
  83.4 2.3 %concatenate.83 = f32[2,8,8,2050]{3,1,2,0:T(8,128)} concatenate(f32[2,8,8,1]{3,1,2,0:T(8,128)} %collective-permute-done.4, f32[2,8,8,2048]{3,1,2,0:T(8,128)} %pad_maximum_fusion.1, f32[2,8,8,1]{3,1,2,0:T(8,128)} %collective-permute-done.5), dimensions={3} | concatenate | bytes 2099200 | tf_op jit(solution)/shard_map/concatenate | solution.py:24
  93.7 2.7 %collective-permute-start.10 = (f32[2,128]{1,0:T(2,128)S(1)}, f32[2,128]{1,0:T(2,128)S(1)}, u32[]{:S(2)}, u32[]{:S(2)}) collective-permute-start(f32[2,128]{1,0:T(2,128)S(1)} %broadcast_in_dim.37), channel_id=1, source_target_pairs={{0,48},{16,32},{32,16},{48,0},{64,112},{80,96},{96,80},{112,64},{1... | collective-permute-start | bytes 3080 | tf_op jit(solution)/shard_map/ppermute | solution.py:108
  96.6 1.8 %collective-permute-start.9 = (f32[2,128]{1,0:T(2,128)S(1)}, f32[2,128]{1,0:T(2,128)S(1)}, u32[]{:S(2)}, u32[]{:S(2)}) collective-permute-start(f32[2,128]{1,0:T(2,128)S(1)} %broadcast_in_dim.37), channel_id=1, source_target_pairs={{0,32},{16,48},{32,0},{48,16},{64,96},{80,112},{96,64},{112,80},{1... | collective-permute-start | bytes 3080 | tf_op jit(solution)/shard_map/ppermute | solution.py:108
  99.9 1.7 %collective-permute-done.9 = f32[2,128]{1,0:T(2,128)S(1)} collective-permute-done((f32[2,128]{1,0:T(2,128)S(1)}, f32[2,128]{1,0:T(2,128)S(1)}, u32[]{:S(2)}, u32[]{:S(2)}) %collective-permute-start.9) | collective-permute-done | bytes 1056 | tf_op jit(solution)/shard_map/ppermute | solution.py:108
  102.3 2.4 %collective-permute-start.12 = (f32[2,128]{1,0:T(2,128)S(1)}, f32[2,128]{1,0:T(2,128)S(1)}, u32[]{:S(2)}, u32[]{:S(2)}) collective-permute-start(f32[2,128]{1,0:T(2,128)S(1)} %add_add_fusion.3), channel_id=1, source_target_pairs={{0,128},{16,144},{32,160},{48,176},{64,192},{80,208},{96,224},{112... | collective-permute-start | bytes 3080 | tf_op jit(solution)/shard_map/ppermute | solution.py:108
  105.3 2.0 %collective-permute-done.12 = f32[2,128]{1,0:T(2,128)S(1)} collective-permute-done((f32[2,128]{1,0:T(2,128)S(1)}, f32[2,128]{1,0:T(2,128)S(1)}, u32[]{:S(2)}, u32[]{:S(2)}) %collective-permute-start.12) | collective-permute-done | bytes 1056 | tf_op jit(solution)/shard_map/ppermute | solution.py:108
  117.8 6.4 %all-to-all-start.3 = ((f32[4,16,2048]{2,0,1:T(4,128)}), f32[4,16,2048]{2,0,1:T(4,128)S(1)}, u32[]{:S(2)}, u32[]{:S(2)}) async-start(f32[4,16,2048]{2,0,1:T(4,128)} %copy.114), calls=%async_computation.3 | async-start | bytes 1048576 | tf_op jit(solution)/shard_map/all_to_all | solution.py:171
  124.3 2.0 %collective-permute-start.17 = (f32[2,128]{1,0:T(2,128)S(1)}, f32[2,128]{1,0:T(2,128)S(1)}, u32[]{:S(2)}, u32[]{:S(2)}) collective-permute-start(f32[2,128]{1,0:T(2,128)S(1)} %add_add_fusion.1), channel_id=1, source_target_pairs={{0,4},{1,5},{2,6},{3,7},{4,0},{5,1},{6,2},{7,3},{8,12},{9,13},{10,... | collective-permute-start | bytes 3080 | tf_op jit(solution)/shard_map/ppermute | solution.py:108
  126.3 4.0 %collective-permute-start.18 = (f32[2,128]{1,0:T(2,128)S(1)}, f32[2,128]{1,0:T(2,128)S(1)}, u32[]{:S(2)}, u32[]{:S(2)}) collective-permute-start(f32[2,128]{1,0:T(2,128)S(1)} %add_add_fusion.1), channel_id=1, source_target_pairs={{0,8},{1,9},{2,10},{3,11},{4,12},{5,13},{6,14},{7,15},{8,0},{9,1},... | collective-permute-start | bytes 3080 | tf_op jit(solution)/shard_map/ppermute | solution.py:108
  130.9 2.9 %collective-permute-done.18 = f32[2,128]{1,0:T(2,128)S(1)} collective-permute-done((f32[2,128]{1,0:T(2,128)S(1)}, f32[2,128]{1,0:T(2,128)S(1)}, u32[]{:S(2)}, u32[]{:S(2)}) %collective-permute-start.18) | collective-permute-done | bytes 1056 | tf_op jit(solution)/shard_map/ppermute | solution.py:108
  133.8 2.2 %collective-permute-done.19 = f32[2,128]{1,0:T(2,128)S(1)} collective-permute-done((f32[2,128]{1,0:T(2,128)S(1)}, f32[2,128]{1,0:T(2,128)S(1)}, u32[]{:S(2)}, u32[]{:S(2)}) %collective-permute-start.19) | collective-permute-done | bytes 1056 | tf_op jit(solution)/shard_map/ppermute | solution.py:108
  (172 shorter events, 53.2 us)
Async XLA Ops:
  2.1 32.0 %all-to-all-start = ((f32[16,4,2048]{2,1,0:T(4,128)}), f32[16,4,2048]{2,1,0:T(4,128)}, u32[]{:S(2)}, u32[]{:S(2)}) async-start(f32[16,4,2048]{2,1,0:T(4,128)} %all_to_all.48), calls=%async_computation | async-start | bytes 1048576 | tf_op jit(solution)/shard_map/all_to_all | solution.py:163
  10.7 18.8 %collective-permute-start = (f32[2,8,8,1]{3,1,2,0:T(8,128)}, f32[2,8,8,1]{3,1,2,0:T(8,128)}, u32[]{:S(2)}, u32[]{:S(2)}) collective-permute-start(f32[2,8,8,1]{3,1,2,0:T(8,128)} %get-tuple-element.41), channel_id=1, source_target_pairs={{0,16},{16,32},{32,48},{48,64},{64,80},{80,96},{96,112},{112,128},... | collective-permute-start | bytes 1544 | tf_op jit(solution)/shard_map/ppermute | solution.py:22
  12.1 17.3 %collective-permute-start.1 = (f32[2,8,8,1]{3,1,2,0:T(8,128)}, f32[2,8,8,1]{3,1,2,0:T(8,128)}, u32[]{:S(2)}, u32[]{:S(2)}) collective-permute-start(f32[2,8,8,1]{3,1,2,0:T(8,128)} %get-tuple-element.40), channel_id=1, source_target_pairs={{16,0},{32,16},{48,32},{64,48},{80,64},{96,80},{112,96},{128,112},... | collective-permute-start | bytes 1544 | tf_op jit(solution)/shard_map/ppermute | solution.py:23
  15.5 16.8 %collective-permute-start.2 = (f32[2,8,1,2048]{3,1,2,0:T(8,128)}, f32[2,8,1,2048]{3,1,2,0:T(8,128)S(1)}, u32[]{:S(2)}, u32[]{:S(2)}) collective-permute-start(f32[2,8,1,2048]{3,1,2,0:T(8,128)} %get-tuple-element.42), channel_id=1, source_target_pairs={{0,1},{1,2},{2,3},{3,4},{4,5},{5,6},{6,7},{7,8},{8,9},{9,10},{10,1... | collective-permute-start | bytes 393224 | tf_op jit(solution)/shard_map/ppermute | solution.py:22
  15.5 17.4 %collective-permute-start.3 = (f32[2,8,1,2048]{3,1,2,0:T(8,128)}, f32[2,8,1,2048]{3,1,2,0:T(8,128)}, u32[]{:S(2)}, u32[]{:S(2)}) collective-permute-start(f32[2,8,1,2048]{3,1,2,0:T(8,128)} %get-tuple-element.43), channel_id=1, source_target_pairs={{1,0},{2,1},{3,2},{4,3},{5,4},{6,5},{7,6},{8,7},{9,8},{10,9},{11,1... | collective-permute-start | bytes 393224 | tf_op jit(solution)/shard_map/ppermute | solution.py:23
  45.3 13.0 %all-to-all-start.1 = ((f32[4,16,2048]{2,0,1:T(4,128)}), f32[4,16,2048]{2,0,1:T(4,128)S(1)}, u32[]{:S(2)}, u32[]{:S(2)}) async-start(f32[4,16,2048]{2,0,1:T(4,128)} %copy.100), calls=%async_computation.1 | async-start | bytes 1048576 | tf_op jit(solution)/shard_map/all_to_all | solution.py:171
  64.8 18.6 %collective-permute-start.4 = (f32[2,8,8,1]{3,1,2,0:T(8,128)}, f32[2,8,8,1]{3,1,2,0:T(8,128)}, u32[]{:S(2)}, u32[]{:S(2)}) collective-permute-start(f32[2,8,8,1]{3,1,2,0:T(8,128)} %get-tuple-element.37), channel_id=1, source_target_pairs={{0,16},{16,32},{32,48},{48,64},{64,80},{80,96},{96,112},{112,128},... | collective-permute-start | bytes 1544 | tf_op jit(solution)/shard_map/ppermute | solution.py:22
  65.4 18.0 %collective-permute-start.5 = (f32[2,8,8,1]{3,1,2,0:T(8,128)S(1)}, f32[2,8,8,1]{3,1,2,0:T(8,128)}, u32[]{:S(2)}, u32[]{:S(2)}) collective-permute-start(f32[2,8,8,1]{3,1,2,0:T(8,128)S(1)} %get-tuple-element.36), channel_id=1, source_target_pairs={{16,0},{32,16},{48,32},{64,48},{80,64},{96,80},{112,96},{128,112},... | collective-permute-start | bytes 1544 | tf_op jit(solution)/shard_map/ppermute | solution.py:23
  70.9 16.2 %collective-permute-start.6 = (f32[2,8,1,2048]{3,1,2,0:T(8,128)}, f32[2,8,1,2048]{3,1,2,0:T(8,128)S(1)}, u32[]{:S(2)}, u32[]{:S(2)}) collective-permute-start(f32[2,8,1,2048]{3,1,2,0:T(8,128)} %get-tuple-element.38), channel_id=1, source_target_pairs={{0,1},{1,2},{2,3},{3,4},{4,5},{5,6},{6,7},{7,8},{8,9},{9,10},{10,1... | collective-permute-start | bytes 393224 | tf_op jit(solution)/shard_map/ppermute | solution.py:22
  70.9 16.2 %collective-permute-start.7 = (f32[2,8,1,2048]{3,1,2,0:T(8,128)}, f32[2,8,1,2048]{3,1,2,0:T(8,128)}, u32[]{:S(2)}, u32[]{:S(2)}) collective-permute-start(f32[2,8,1,2048]{3,1,2,0:T(8,128)} %get-tuple-element.39), channel_id=1, source_target_pairs={{1,0},{2,1},{3,2},{4,3},{5,4},{6,5},{7,6},{8,7},{9,8},{10,9},{11,1... | collective-permute-start | bytes 393224 | tf_op jit(solution)/shard_map/ppermute | solution.py:23
  75.8 34.3 %all-to-all-start.2 = ((f32[16,4,2048]{2,1,0:T(4,128)}), f32[16,4,2048]{2,1,0:T(4,128)}, u32[]{:S(2)}, u32[]{:S(2)}) async-start(f32[16,4,2048]{2,1,0:T(4,128)} %all_to_all.54), calls=%async_computation.2 | async-start | bytes 1048576 | tf_op jit(solution)/shard_map/all_to_all | solution.py:163
  93.7 4.8 %collective-permute-start.10 = (f32[2,128]{1,0:T(2,128)S(1)}, f32[2,128]{1,0:T(2,128)S(1)}, u32[]{:S(2)}, u32[]{:S(2)}) collective-permute-start(f32[2,128]{1,0:T(2,128)S(1)} %broadcast_in_dim.37), channel_id=1, source_target_pairs={{0,48},{16,32},{32,16},{48,0},{64,112},{80,96},{96,80},{112,64},{1... | collective-permute-start | bytes 3080 | tf_op jit(solution)/shard_map/ppermute | solution.py:108
  96.4 3.6 %collective-permute-start.8 = (f32[2,128]{1,0:T(2,128)S(1)}, f32[2,128]{1,0:T(2,128)S(1)}, u32[]{:S(2)}, u32[]{:S(2)}) collective-permute-start(f32[2,128]{1,0:T(2,128)S(1)} %broadcast_in_dim.37), channel_id=1, source_target_pairs={{0,16},{16,0},{32,48},{48,32},{64,80},{80,64},{96,112},{112,96},{1... | collective-permute-start | bytes 3080 | tf_op jit(solution)/shard_map/ppermute | solution.py:108
  96.6 5.1 %collective-permute-start.9 = (f32[2,128]{1,0:T(2,128)S(1)}, f32[2,128]{1,0:T(2,128)S(1)}, u32[]{:S(2)}, u32[]{:S(2)}) collective-permute-start(f32[2,128]{1,0:T(2,128)S(1)} %broadcast_in_dim.37), channel_id=1, source_target_pairs={{0,32},{16,48},{32,0},{48,16},{64,96},{80,112},{96,64},{112,80},{1... | collective-permute-start | bytes 3080 | tf_op jit(solution)/shard_map/ppermute | solution.py:108
  101.8 3.6 %collective-permute-start.11 = (f32[2,128]{1,0:T(2,128)S(1)}, f32[2,128]{1,0:T(2,128)S(1)}, u32[]{:S(2)}, u32[]{:S(2)}) collective-permute-start(f32[2,128]{1,0:T(2,128)S(1)} %add_add_fusion.3), channel_id=1, source_target_pairs={{0,64},{16,80},{32,96},{48,112},{64,0},{80,16},{96,32},{112,48},{1... | collective-permute-start | bytes 3080 | tf_op jit(solution)/shard_map/ppermute | solution.py:108
  102.3 5.1 %collective-permute-start.12 = (f32[2,128]{1,0:T(2,128)S(1)}, f32[2,128]{1,0:T(2,128)S(1)}, u32[]{:S(2)}, u32[]{:S(2)}) collective-permute-start(f32[2,128]{1,0:T(2,128)S(1)} %add_add_fusion.3), channel_id=1, source_target_pairs={{0,128},{16,144},{32,160},{48,176},{64,192},{80,208},{96,224},{112... | collective-permute-start | bytes 3080 | tf_op jit(solution)/shard_map/ppermute | solution.py:108
  104.7 3.6 %collective-permute-start.13 = (f32[2,128]{1,0:T(2,128)S(1)}, f32[2,128]{1,0:T(2,128)S(1)}, u32[]{:S(2)}, u32[]{:S(2)}) collective-permute-start(f32[2,128]{1,0:T(2,128)S(1)} %add_add_fusion.3), channel_id=1, source_target_pairs={{0,192},{16,208},{32,224},{48,240},{64,128},{80,144},{96,160},{112... | collective-permute-start | bytes 3080 | tf_op jit(solution)/shard_map/ppermute | solution.py:108
  108.3 15.9 %collective-permute-start.14 = (f32[2,128]{1,0:T(2,128)S(1)}, f32[2,128]{1,0:T(2,128)S(1)}, u32[]{:S(2)}, u32[]{:S(2)}) collective-permute-start(f32[2,128]{1,0:T(2,128)S(1)} %add_add_fusion.2), channel_id=1, source_target_pairs={{0,1},{1,0},{2,3},{3,2},{4,5},{5,4},{6,7},{7,6},{8,9},{9,8},{10,11... | collective-permute-start | bytes 3080 | tf_op jit(solution)/shard_map/ppermute | solution.py:108
  108.3 15.9 %collective-permute-start.15 = (f32[2,128]{1,0:T(2,128)S(1)}, f32[2,128]{1,0:T(2,128)S(1)}, u32[]{:S(2)}, u32[]{:S(2)}) collective-permute-start(f32[2,128]{1,0:T(2,128)S(1)} %add_add_fusion.2), channel_id=1, source_target_pairs={{0,2},{1,3},{2,0},{3,1},{4,6},{5,7},{6,4},{7,5},{8,10},{9,11},{10,... | collective-permute-start | bytes 3080 | tf_op jit(solution)/shard_map/ppermute | solution.py:108
  108.5 15.7 %collective-permute-start.16 = (f32[2,128]{1,0:T(2,128)S(1)}, f32[2,128]{1,0:T(2,128)S(1)}, u32[]{:S(2)}, u32[]{:S(2)}) collective-permute-start(f32[2,128]{1,0:T(2,128)S(1)} %add_add_fusion.2), channel_id=1, source_target_pairs={{0,3},{1,2},{2,1},{3,0},{4,7},{5,6},{6,5},{7,4},{8,11},{9,10},{10,... | collective-permute-start | bytes 3080 | tf_op jit(solution)/shard_map/ppermute | solution.py:108
  117.8 20.8 %all-to-all-start.3 = ((f32[4,16,2048]{2,0,1:T(4,128)}), f32[4,16,2048]{2,0,1:T(4,128)S(1)}, u32[]{:S(2)}, u32[]{:S(2)}) async-start(f32[4,16,2048]{2,0,1:T(4,128)} %copy.114), calls=%async_computation.3 | async-start | bytes 1048576 | tf_op jit(solution)/shard_map/all_to_all | solution.py:171
  124.3 6.6 %collective-permute-start.17 = (f32[2,128]{1,0:T(2,128)S(1)}, f32[2,128]{1,0:T(2,128)S(1)}, u32[]{:S(2)}, u32[]{:S(2)}) collective-permute-start(f32[2,128]{1,0:T(2,128)S(1)} %add_add_fusion.1), channel_id=1, source_target_pairs={{0,4},{1,5},{2,6},{3,7},{4,0},{5,1},{6,2},{7,3},{8,12},{9,13},{10,... | collective-permute-start | bytes 3080 | tf_op jit(solution)/shard_map/ppermute | solution.py:108
  126.3 7.5 %collective-permute-start.18 = (f32[2,128]{1,0:T(2,128)S(1)}, f32[2,128]{1,0:T(2,128)S(1)}, u32[]{:S(2)}, u32[]{:S(2)}) collective-permute-start(f32[2,128]{1,0:T(2,128)S(1)} %add_add_fusion.1), channel_id=1, source_target_pairs={{0,8},{1,9},{2,10},{3,11},{4,12},{5,13},{6,14},{7,15},{8,0},{9,1},... | collective-permute-start | bytes 3080 | tf_op jit(solution)/shard_map/ppermute | solution.py:108
  130.4 5.7 %collective-permute-start.19 = (f32[2,128]{1,0:T(2,128)S(1)}, f32[2,128]{1,0:T(2,128)S(1)}, u32[]{:S(2)}, u32[]{:S(2)}) collective-permute-start(f32[2,128]{1,0:T(2,128)S(1)} %add_add_fusion.1), channel_id=1, source_target_pairs={{0,12},{1,13},{2,14},{3,15},{4,8},{5,9},{6,10},{7,11},{8,4},{9,5},... | collective-permute-start | bytes 3080 | tf_op jit(solution)/shard_map/ppermute | solution.py:108
  (37 other events, 141.5 us)
